TPU v7x, 32 devices: a whole 2x2x4 slice. The times are simulated.
32 devices in a mesh: src: 4 (over y, x), tile: 8 (over z, core).
Axes of the slice: x: 2, y: 2, z: 4, core: 2. Of those that a mesh axis runs over, the one named last changes fastest.
Arguments:
- latent: bfloat16 [3, 32, 16, 160], P(None, ('src', 'tile')), may hold values from -6 to 6
- row_map: int32 [32], replicated, may hold values from 0 to 31, each once
- latent_cache: bfloat16 [2, 32, 16, 160], P(None, 'tile'), may hold values from -6 to 6
- cache_one: bfloat16 [2, 32, 384, 160], P(None, 'tile', 'src'), may hold values from -5 to 5
- cache_two: bfloat16 [2, 32, 384, 160], P(None, 'tile', 'src'), may hold values from -5 to 5
- conv_in_w: bfloat16 [3, 3, 3, 16, 384], P(None, None, None, None, 'src'), may hold values from -0.3125 to 0.3125
- weight_one: bfloat16 [3, 3, 3, 384, 384], P(None, None, None, 'src'), may hold values from -0.0625 to 0.0625
- weight_two: bfloat16 [3, 3, 3, 384, 384], P(None, None, None, 'src'), may hold values from -0.0625 to 0.0625
- gain_one: float32 [384], P('src'), may hold values from 0.1 to 1.9
- gain_two: float32 [384], P('src'), may hold values from 0.1 to 1.9
Outputs:
- decoded: bfloat16 [3, 32, 384, 160], P(None, 'tile', 'src')
All inputs are finite; a program needn't handle non-finite values.
Results may differ from a plain program's by a relative error of at most 0.0037.
The roundings to bfloat16 on the way count: a program that leaves them out, or rounds other values in their place, can miss the bound.
Values may be sent and summed in bfloat16 or wider, within the bound.
No kernel may reach another device: no remote copies, remote signals or barrier semaphores. Data moves between devices by JAX's collectives and lax.ppermute only.
A program may use at most 128 MiB of HBM per device.

v0:
```python
import functools

import jax
import jax.numpy as jnp
from jax import lax
from jax.experimental import pallas as pl
from jax.experimental.pallas import tpu as pltpu
from jax.sharding import PartitionSpec as P


GSIZE = 12
F32 = jnp.float32
BF16 = jnp.bfloat16
VMEM_LIMIT = 24 << 20
VMEM = pl.BlockSpec(memory_space=pltpu.VMEM)
SMEM = pl.BlockSpec(memory_space=pltpu.SMEM)
HBM = pl.BlockSpec(memory_space=pl.ANY)


def call(body, outs, flops=0, scratch=(), specs=None, n_in=0, out_specs=None, limit=VMEM_LIMIT):
    return pl.pallas_call(
        body,
        out_shape=outs,
        in_specs=specs if specs is not None else [VMEM] * n_in,
        out_specs=out_specs if out_specs is not None else jax.tree.map(lambda _: VMEM, outs),
        scratch_shapes=list(scratch),
        cost_estimate=pl.CostEstimate(flops=flops, bytes_accessed=1 << 20, transcendentals=0),
        compiler_params=pltpu.CompilerParams(vmem_limit_bytes=limit),
    )


def xor_send(x, axis, mask):
    return lax.ppermute(x, axis, [(i, i ^ mask) for i in range(lax.axis_size(axis))])


def xor_stage(x, axis, masks):
    return [x] + [xor_send(x, axis, m) for m in masks]


def far_masks(size):
    low, stages = 2, []
    while low < size:
        if low * 2 < size:
            stages.append([low, 2 * low, 3 * low])
            low *= 4
        else:
            stages.append([low])
            low *= 2
    return stages


def to_next(x):
    return lax.ppermute(x, "tile", [(i, i + 1) for i in range(lax.axis_size("tile") - 1)])


def to_previous(x):
    return lax.ppermute(x, "tile", [(i + 1, i) for i in range(lax.axis_size("tile") - 1)])


def fetch(sources, targets, sems):
    copies = [pltpu.make_async_copy(src, dst, sems.at[n]) for n, (src, dst) in enumerate(zip(sources, targets))]
    for copy in copies:
        copy.start()
    for copy in copies:
        copy.wait()


def message_body(*refs):
    out_ref, latent_ref, gain_a, gain_b, sems = refs[3:]
    fetch(refs[:3], (latent_ref, gain_a, gain_b), sems)
    lc, channels = latent_ref.shape[2], gain_a.shape[1]
    line = jnp.concatenate([latent_ref[f, 0].astype(F32) for f in range(latent_ref.shape[0])], axis=1)
    gains = jnp.concatenate([gain_a[...], gain_b[...]], axis=1)
    out_ref[0:lc, :] = line
    out_ref[lc:, :] = jnp.zeros_like(out_ref[lc:, :])
    out_ref[lc : lc + 1, 0 : 2 * channels] = gains


def pack_body(*refs):
    packed_ref, own_ref, low_ref, high_ref, *here, sems = refs[3:]
    fetch(refs[:3], here, sems)
    one_ref, two_ref, span_ref = here
    frames, rows = one_ref.shape[0], one_ref.shape[1]
    columns, lc = one_ref.shape[2], span_ref.shape[2]

    def joined(parts):
        return jnp.concatenate([part.astype(F32) for part in parts], axis=1).astype(BF16)

    every = [ref.at[f] for ref in (one_ref, two_ref) for f in range(frames)]
    for n, ref in enumerate(every):
        packed_ref[n] = joined([ref[h] for h in range(rows)])
    low_ref[0:columns, :] = joined([ref[0] for ref in every])
    high_ref[0:columns, :] = joined([ref[rows - 1] for ref in every])
    width = span_ref.shape[3] * frames
    for ref in (low_ref, high_ref):
        ref[columns:, :] = jnp.zeros_like(ref[columns:, :])
    for row in range(rows):
        both = joined([span_ref[f, row] for f in range(frames)])
        own_ref[row] = both
        if row < 2:
            low_ref[columns + row * lc : columns + (row + 1) * lc, 0:width] = both
        if row >= rows - 2:
            at = columns + (row - rows + 2) * lc
            high_ref[at : at + lc, 0:width] = both


def rim_body(packed_ref, before, after, one_ref, two_ref):
    columns = packed_ref.shape[1]
    channels = packed_ref.shape[2] // 4
    for n, ref in enumerate((one_ref, two_ref)):
        parts = []
        for f in range(2):
            ref[f] = packed_ref[2 * n + f]
            lanes = slice((2 * n + f) * channels, (2 * n + f + 1) * channels)
            parts += [side[0:columns, lanes].astype(F32) for side in (before, after)]
        ref[2] = jnp.concatenate(parts, axis=1).astype(BF16)


def weights_body(w_ref, late_ref, early_ref, turned):
    outs, ins = w_ref.shape[3], w_ref.shape[4]
    mine = lax.axis_index("src")
    late_ref[...] = jnp.zeros_like(late_ref)
    early_ref[...] = jnp.zeros_like(early_ref)

    def tap(n, _):
        b, e = n // 3, n % 3
        for a in range(3):
            turned[...] = w_ref[a, b, e].astype(F32).T
            for slot in range(ins // outs):
                start = pl.multiple_of(jnp.bitwise_xor(mine, slot) * outs, 8)
                rows = turned[pl.ds(start, outs), :].astype(BF16)
                here = pl.ds(slot * outs, outs)
                if a == 2:
                    late_ref[n, here, 0:outs] = rows
                if a == 1:
                    late_ref[n, here, 128 : 128 + outs] = rows
                    early_ref[n, here, 0:outs] = rows
                if a == 0:
                    early_ref[n, here, 128 : 128 + outs] = rows
        return 0

    lax.fori_loop(0, 9, tap, 0)


def first_body(map_ref, near_ref, far_ref, before, own, after, w0, w1, w2, w3, first_ref, stat_ref, taps, wall, tab_ref):
    half = near_ref.shape[0]
    rows = own.shape[0] + 4
    columns = own.shape[2] // 2
    frames = near_ref.shape[2] // columns
    s, t, tiles = lax.axis_index("src"), lax.axis_index("tile"), lax.axis_size("tile")
    top = t * (rows - 4) - 2
    for row in range(rows):
        tab_ref[row] = -1
    for i in range(map_ref.shape[0]):
        at = map_ref[i] - top
        to_t, to_s = jnp.bitwise_xor(i % tiles, t), jnp.bitwise_xor(i // tiles, s)
        place = to_t % 2 * half + to_t // 2 * 4 + to_s

        @pl.when(jnp.logical_and(at >= 0, at < rows))
        def _():
            tab_ref[jnp.clip(at, 0, rows - 1)] = place

    wall[...] = jnp.concatenate([w[...].astype(F32) for w in (w0, w1, w2, w3)], axis=1).astype(BF16)
    for row in range(rows):
        place = tab_ref[row]
        kept = (place >= 0).astype(F32)
        inner = jnp.maximum(jnp.where(place >= half, place - half, place), 0)
        new = jnp.where(place >= half, far_ref[inner].astype(F32), near_ref[inner].astype(F32)) * kept
        if 2 <= row < rows - 2:
            old = own[row - 2].astype(F32)
        else:
            at = columns + 16 * (row if row < 2 else row - rows + 2)
            old = (before if row < 2 else after)[at : at + 16, 0 : 2 * columns].astype(F32)
        for f in range(frames + 2):
            v = old[:, f * columns : (f + 1) * columns] if f < 2 else new[:, (f - 2) * columns : (f - 1) * columns]
            zero = jnp.zeros((16, 1), F32)
            left = jnp.concatenate([zero, v[:, : columns - 1]], axis=1)
            right = jnp.concatenate([v[:, 1:], zero], axis=1)
            taps[row, f] = jnp.concatenate([left, v, right], axis=0).astype(BF16)
    total = jnp.zeros((8, wall.shape[1]), F32)
    for t in range(frames):
        for r in range(rows - 2):
            patch = jnp.concatenate([taps[r + b, t + a] for a in range(3) for b in range(3)], axis=0)
            got = lax.dot_general(patch, wall[...], (((0,), (0,)), ((), ())), preferred_element_type=F32).astype(BF16)
            first_ref[t, r] = got
            if 0 < r < rows - 3:
                total += jnp.sum(got.astype(F32).reshape(columns // 8, 8, -1), axis=0)
    count = frames * (rows - 4) * columns
    mean = jnp.sum(total, axis=0, keepdims=True) * (1.0 / count)
    square = jnp.zeros((8, wall.shape[1]), F32)
    for t in range(frames):
        for r in range(1, rows - 3):
            d = first_ref[t, r].astype(F32) - mean
            square += jnp.sum((d * d).reshape(columns // 8, 8, -1), axis=0)
    stat_ref[0:1, :] = mean
    stat_ref[1:2, :] = jnp.sum(square, axis=0, keepdims=True)


def scale_shift(means, squares, gain, count):
    channels = gain.shape[1]
    lane = lax.broadcasted_iota(jnp.int32, (channels, channels), 0) // GSIZE
    other = lax.broadcasted_iota(jnp.int32, (channels, channels), 1) // GSIZE
    same = (lane == other).astype(F32)

    def over_group(v):
        v = jnp.broadcast_to(v, (8, channels))
        return jnp.dot(v, same, precision=lax.Precision.HIGHEST, preferred_element_type=F32)[0:1]

    tiles = sum(m.shape[0] for m in means)
    mean = over_group(sum(jnp.sum(m, axis=0, keepdims=True) for m in means)) * (1.0 / (tiles * GSIZE))
    spread = jnp.zeros_like(mean)
    for m, q in zip(means, squares):
        spread += jnp.sum(q + float(count) * (m - mean) * (m - mean), axis=0, keepdims=True)
    variance = over_group(spread) * (1.0 / (count * tiles * GSIZE))
    scale = lax.rsqrt(variance + 1e-06) * gain
    return mean, scale


def put_row(taps, f, r, v):
    columns, channels = v.shape
    at = lax.broadcasted_iota(jnp.int32, v.shape, 0)
    left = jnp.where(at == 0, 0.0, pltpu.roll(v, 1, axis=0))
    right = jnp.where(at == columns - 1, 0.0, pltpu.roll(v, columns - 1, axis=0))
    taps[f, r, :, 0:channels] = left.astype(BF16)
    taps[f, r, :, channels : 2 * channels] = v.astype(BF16)
    taps[f, r, :, 2 * channels :] = right.astype(BF16)


def activate(v, mean, scale):
    y = (v - mean) * scale
    return (0.5 * y) * (1.0 + jnp.tanh(0.5 * y))


def tap_product(taps, f, w_ref, lanes):
    _, rows, columns, depth = taps.shape
    summed = None
    for b in range(3):
        x = taps[f, b : b + rows - 2].reshape((rows - 2) * columns, depth)
        w = w_ref[3 * b : 3 * b + 3, :, lanes].reshape(depth, lanes.stop - lanes.start)
        got = jnp.dot(x, w, preferred_element_type=F32)
        summed = got if summed is None else summed + got
    return summed


def spread_rows(own, up, down, f, r, rows, channels):
    if r == 0:
        return up[f].astype(F32)
    if r == rows - 1:
        return down[f].astype(F32)
    lanes = slice((r - 1) * channels, r * channels)
    return jnp.concatenate([piece[f, :, lanes].astype(F32) for piece in own], axis=1)


def cached_body(p0, p1, p2, p3, early_ref, out_ref, taps):
    pieces = (p0, p1, p2, p3)
    rows = taps.shape[1]
    channels = p0.shape[2] // (rows - 2)
    for f in range(2):
        for r in range(rows):
            if 0 < r < rows - 1:
                v = spread_rows(pieces, None, None, f, r, rows, channels)
            else:
                at = (2 * f + (r > 0)) * channels
                v = jnp.concatenate([piece[2, :, at : at + channels].astype(F32) for piece in pieces], axis=1)
            put_row(taps, f, r, v)
    one = tap_product(taps, 0, early_ref, slice(128, 256))
    both = tap_product(taps, 1, early_ref, slice(0, 256))
    out_ref[0] = one + both[:, 0:128]
    out_ref[1] = both[:, 128:256]


def conv_current(taps, late_ref, early_ref, cached_ref):
    both = tap_product(taps, 0, late_ref, slice(0, 256))
    yield cached_ref[0] + both[:, 0:128]
    middle = cached_ref[1] + both[:, 128:256]
    last = tap_product(taps, 0, early_ref, slice(128, 256))
    both = tap_product(taps, 1, late_ref, slice(0, 256))
    yield middle + both[:, 0:128]
    last = last + both[:, 128:256]
    yield last + tap_product(taps, 2, late_ref, slice(0, 128))


def gain_of(refs, n, channels):
    at = refs[0].shape[0] - 8
    lanes = slice(n * channels, (n + 1) * channels)
    return jnp.concatenate([ref[at : at + 1, lanes] for ref in refs], axis=1)


def inside():
    t = lax.axis_index("tile")
    return (t > 0).astype(F32), (t < lax.axis_size("tile") - 1).astype(F32)


def middle_body(n_stats, count, *refs):
    stats = refs[:n_stats]
    gains = refs[n_stats : n_stats + 4]
    first_ref, cached_ref, late_ref, early_ref, out_ref, stat_ref, taps, kept = refs[n_stats + 4 :]
    edges = inside()
    means = [s[:, 0, :] for s in stats]
    squares = [s[:, 1, :] for s in stats]
    mean, scale = scale_shift(means, squares, gain_of(gains, 0, first_ref.shape[3] // 4), count)
    frames, rows, columns, _ = taps.shape
    for f in range(frames):
        for r in range(rows):
            v = activate(first_ref[f, r].astype(F32), mean, scale)
            if r == 0:
                v = v * edges[0]
            if r == rows - 1:
                v = v * edges[1]
            put_row(taps, f, r, v)
    channels = out_ref.shape[2] // (rows - 2)
    total = jnp.zeros((1, 128), F32)
    for f, got in enumerate(conv_current(taps, late_ref, early_ref, cached_ref)):
        kept[f] = got
        total += jnp.sum(got, axis=0, keepdims=True)
        parts = [got[h * columns : (h + 1) * columns, 0:channels] for h in range(rows - 2)]
        out_ref[f] = jnp.concatenate(parts, axis=1).astype(BF16)
    local = total * (1.0 / (frames * (rows - 2) * columns))
    square = jnp.zeros((1, 128), F32)
    for f in range(frames):
        d = kept[f] - local
        square += jnp.sum(d * d, axis=0, keepdims=True)
    stat_ref[0:1, :] = local
    stat_ref[1:2, :] = square


def last_body(n_stats, count, *refs):
    stats = refs[:n_stats]
    gains, (p0, p1, p2, p3) = refs[n_stats : n_stats + 4], refs[n_stats + 4 : n_stats + 8]
    cached_ref, late_ref, early_ref, out_ref, scale_ref, taps = refs[n_stats + 8 :]
    frames, rows, _, _ = taps.shape
    channels = p0.shape[2] // (rows - 2)

    def wide(s, n):
        return jnp.concatenate([s[:, slot, n, 0:channels] for slot in range(4)], axis=1)

    means = [wide(s, 0) for s in stats]
    squares = [wide(s, 1) for s in stats]
    mean, scale = scale_shift(means, squares, gain_of(gains, 1, channels), count)
    scale_ref[0:1, :] = mean
    scale_ref[1:2, :] = scale
    for f in range(frames):
        taps[f, 0] = jnp.zeros_like(taps[f, 0])
        taps[f, rows - 1] = jnp.zeros_like(taps[f, rows - 1])
        for r in range(1, rows - 1):
            v = spread_rows((p0, p1, p2, p3), None, None, f, r, rows, channels)
            put_row(taps, f, r, activate(v, mean, scale))
    for f, got in enumerate(conv_current(taps, late_ref, early_ref, cached_ref)):
        out_ref[f] = got


def edge_body(part_ref, scale_ref, up, down, first_ref, late_ref, early_ref, out_hbm, taps, out_ref, sems):
    frames, _, columns, depth = taps.shape
    rows = first_ref.shape[1]
    channels = out_ref.shape[3]
    mean, scale = scale_ref[0:1, :], scale_ref[1:2, :]
    added = []
    for side, (ref, kept, b) in enumerate(zip((up, down), inside(), (0, 2))):
        for f in range(frames):
            put_row(taps, f, side, activate(ref[f].astype(F32), mean, scale) * kept)
        taken = slice(3 * b, 3 * b + 3)
        x = jnp.concatenate([taps[f, side] for f in range(frames)], axis=0)
        both = jnp.dot(x, late_ref[taken].reshape(depth, 256), preferred_element_type=F32)
        late = jnp.dot(taps[0, side], early_ref[taken, :, 128:256].reshape(depth, 128), preferred_element_type=F32)
        now, then = both[:, 0:128], both[:, 128:256]
        added.append(
            [
                now[0:columns],
                now[columns : 2 * columns] + then[0:columns],
                now[2 * columns :] + then[columns : 2 * columns] + late,
            ]
        )
    for f in range(frames):
        for h in range(rows - 2):
            here = part_ref[f, h * columns : (h + 1) * columns]
            if h == 0:
                here = here + added[0][f]
            if h == rows - 3:
                here = here + added[1][f]
            here = here[:, 0:channels] + first_ref[f, h + 1][:, 0:channels].astype(F32)
            out_ref[f, h] = here.astype(BF16)
        pltpu.make_async_copy(out_ref.at[f], out_hbm.at[f], sems.at[f]).start()
    for f in range(frames):
        pltpu.make_async_copy(out_ref.at[f], out_hbm.at[f], sems.at[f]).wait()


def edges_of(pieces, channels):
    top = jnp.concatenate([p[:, :, :channels] for p in pieces], axis=2)
    bottom = jnp.concatenate([p[:, :, -channels:] for p in pieces], axis=2)
    return to_next(bottom), to_previous(top)


def shaped(shape, dtype):
    return jax.ShapeDtypeStruct(tuple(shape), dtype)


def window(
    latent,
    row_map,
    latent_cache,
    cache_one,
    cache_two,
    conv_in_w,
    weight_one,
    weight_two,
    gain_one,
    gain_two,
):
    frames, _, lc, columns = latent.shape
    tile_rows = latent_cache.shape[1]
    tiles, sources = lax.axis_size("tile"), lax.axis_size("src")
    channels = conv_in_w.shape[4]
    wide = channels * sources
    others = range(1, sources)

    message = call(
        message_body,
        shaped((lc + 8, frames * columns), F32),
        scratch=[
            pltpu.VMEM(latent.shape, BF16),
            pltpu.VMEM((1, channels), F32),
            pltpu.VMEM((1, channels), F32),
            pltpu.SemaphoreType.DMA((3,)),
        ],
        specs=[HBM] * 3,
        limit=60 * 1024 * 1024,
    )(latent, gain_one[None], gain_two[None])
    got = xor_stage(message, "src", others)
    near = jnp.stack([x[:lc].astype(BF16) for x in got])
    for masks in far_masks(tiles):
        near = jnp.concatenate(xor_stage(near, "tile", masks), axis=0)
    far = xor_send(near, "tile", 1)

    w_in = xor_stage(conv_in_w.reshape(27 * lc, channels), "src", others)
    caches = (cache_one.transpose(0, 1, 3, 2), cache_two.transpose(0, 1, 3, 2), latent_cache)
    strip = shaped((columns + 2 * lc, tile_rows * channels), BF16)
    packed, span, low, high = call(
        pack_body,
        (shaped((4, columns, tile_rows * channels), BF16), shaped((tile_rows, lc, 2 * columns), BF16), strip, strip),
        scratch=[pltpu.VMEM(x.shape, BF16) for x in caches] + [pltpu.SemaphoreType.DMA((3,))],
        specs=[HBM] * 3,
        limit=60 * 1024 * 1024,
    )(*caches)
    before = to_next(high)
    after = to_previous(low)
    rimmed = shaped((3, columns, tile_rows * channels), BF16)
    rim_one, rim_two = call(rim_body, (rimmed, rimmed), n_in=3)(packed, before, after)
    pieces_one = xor_stage(rim_one, "src", others)
    pieces_two = xor_stage(rim_two, "src", others)

    def turn(w):
        shape = shaped((9, wide, 256), BF16)
        return call(weights_body, (shape, shape), scratch=[pltpu.VMEM((wide, channels), F32)], n_in=1)(w)

    late_one, early_one = turn(weight_one)
    late_two, early_two = turn(weight_two)

    rows = tile_rows + 2
    spots = tile_rows * columns
    flops = 2 * 27 * wide * channels * spots

    def cached(pieces, early):
        return call(
            cached_body,
            shaped((2, spots, 128), F32),
            flops=flops,
            scratch=[pltpu.VMEM((2, rows, columns, 3 * wide), BF16)],
            n_in=5,
        )(*pieces, early)

    cached_one = cached(pieces_one, early_one)
    cached_two = cached(pieces_two, early_two)

    first, stat = call(
        first_body,
        (shaped((frames, rows, columns, wide), BF16), shaped((2, wide), F32)),
        flops=flops // 4,
        scratch=[
            pltpu.VMEM((rows + 2, frames + 2, 3 * lc, columns), BF16),
            pltpu.VMEM((27 * lc, wide), BF16),
            pltpu.SMEM((rows + 2,), jnp.int32),
        ],
        specs=[SMEM] + [VMEM] * 9,
    )(row_map, near, far, before, span, after, *w_in)

    def over_tiles(x):
        x = jnp.stack(xor_stage(x, "tile", [1]))
        stages = far_masks(tiles)
        for masks in stages[:-1]:
            x = jnp.concatenate(xor_stage(x, "tile", masks), axis=0)
        return xor_stage(x, "tile", stages[-1])

    count = frames * spots
    stats = over_tiles(stat)
    middle, stat_two = call(
        functools.partial(middle_body, len(stats), count),
        (shaped((frames, columns, tile_rows * channels), BF16), shaped((2, 128), F32)),
        flops=flops * 2,
        scratch=[
            pltpu.VMEM((frames, rows, columns, 3 * wide), BF16),
            pltpu.VMEM((frames, spots, 128), F32),
        ],
        n_in=len(stats) + 8,
    )(*stats, *got, first, cached_one, late_one, early_one)

    mids = xor_stage(middle, "src", others)
    stats = over_tiles(jnp.stack(xor_stage(stat_two, "src", others)))
    above, below = edges_of(mids, channels)
    part, scales = call(
        functools.partial(last_body, len(stats), count),
        (shaped((frames, spots, 128), F32), shaped((2, wide), F32)),
        flops=flops * 2,
        scratch=[pltpu.VMEM((frames, rows, columns, 3 * wide), BF16)],
        n_in=len(stats) + 11,
    )(*stats, *got, *mids, cached_two, late_two, early_two)
    decoded = call(
        edge_body,
        shaped((frames, tile_rows, columns, channels), BF16),
        flops=flops // 2,
        scratch=[
            pltpu.VMEM((frames, 2, columns, 3 * wide), BF16),
            pltpu.VMEM((frames, tile_rows, columns, channels), BF16),
            pltpu.SemaphoreType.DMA((frames,)),
        ],
        n_in=7,
        out_specs=HBM,
    )(part, scales, above, below, first, late_two, early_two)
    return decoded.transpose(0, 1, 3, 2)


def solution(mesh):
    placed = (
        P(None, ("src", "tile"), None, None),
        P(),
        P(None, "tile", None, None),
        P(None, "tile", "src", None),
        P(None, "tile", "src", None),
        P(None, None, None, None, "src"),
        P(None, None, None, "src", None),
        P(None, None, None, "src", None),
        P("src"),
        P("src"),
    )
    return jax.shard_map(
        window,
        mesh=mesh,
        in_specs=placed,
        out_specs=P(None, "tile", "src", None),
        check_vma=False,
    )
```

profile of v0, /device:TPU:1, one launch (start us, length us, event | category | flops | bytes accessed | tf_op | source)
XLA Modules:
  0.0 144.5 jit_solution(17827245097213185020)
XLA Ops:
  0.0 1.5 %shard_map.100.refs_4_ = f32[24,480]{1,0:T(8,128)} custom-call(bf16[3,1,16,160]{3,2,1,0:T(8,128)(2,1)} %refs_0_.1, f32[1,96]{1,0:T(1,128)} %bitcast.44, f32[1,96]{1,0:T(1,128)} %bitcast.45), custom_call_target="tpu_custom_call" | custom-call | bytes 1048576 | tf_op jit(solution)/shard_map/pallas_call | solution.py:416
  1.5 2.1 %collective-permute-start = (f32[24,480]{1,0:T(8,128)}, f32[24,480]{1,0:T(8,128)S(1)}, u32[]{:S(2)}, u32[]{:S(2)}) collective-permute-start(f32[24,480]{1,0:T(8,128)} %shard_map.100.refs_4_), channel_id=1, source_target_pairs={{0,8},{8,0},{16,24},{24,16},{1,9},{9,1},{17,25},{25,17},{2,10},{10... | collective-permute-start | bytes 138248 | tf_op jit(solution)/shard_map/ppermute | solution.py:33
  3.6 1.2 collective-permute-start.1
  6.8 2.1 %collective-permute-done.2.refs_7_ = f32[24,480]{1,0:T(8,128)S(1)} collective-permute-done((f32[24,480]{1,0:T(8,128)}, f32[24,480]{1,0:T(8,128)S(1)}, u32[]{:S(2)}, u32[]{:S(2)}) %collective-permute-start.2) | collective-permute-done | bytes 46112 | tf_op jit(solution)/shard_map/ppermute | solution.py:33
  8.9 1.4 collective-permute-start.3
  10.3 2.2 %shard_map.101 = (bf16[4,160,384]{2,1,0:T(8,128)(2,1)}, bf16[4,16,320]{2,1,0:T(8,128)(2,1)}, bf16[192,384]{1,0:T(8,128)(2,1)}, bf16[192,384]{1,0:T(8,128)(2,1)}) custom-call(bf16[2,4,160,96]{3,2,1,0:T(8,128)(2,1)} %bitcast.34, bf16[2,4,160,96]{3,2,1,0:T(8,128)(2,1)} %bitcast.35, bf16[2,4,16,160]{3,2,1,0:T(8,128)(2,1)} %refs_2_.1), custom_call_target="tpu_custom_call" | custom-call | bytes 1048576 | tf_op jit(solution)/shard_map/pallas_call | solution.py:437
  12.5 4.6 %collective-permute-start.7 = (bf16[192,384]{1,0:T(8,128)(2,1)}, bf16[192,384]{1,0:T(8,128)(2,1)S(1)}, u32[]{:S(2)}, u32[]{:S(2)}) collective-permute-start(bf16[192,384]{1,0:T(8,128)(2,1)} %get-tuple-element.21), channel_id=1, source_target_pairs={{0,1},{1,2},{2,3},{3,4},{4,5},{5,6},{6,7},{8,9},{9,10},{10,11},{11... | collective-permute-start | bytes 442376 | tf_op jit(solution)/shard_map/ppermute | solution.py:53
  17.1 1.9 %collective-permute-start.8 = (bf16[192,384]{1,0:T(8,128)(2,1)}, bf16[192,384]{1,0:T(8,128)(2,1)S(1)}, u32[]{:S(2)}, u32[]{:S(2)}) collective-permute-start(bf16[192,384]{1,0:T(8,128)(2,1)} %get-tuple-element.23), channel_id=1, source_target_pairs={{1,0},{2,1},{3,2},{4,3},{5,4},{6,5},{7,6},{9,8},{10,9},{11,10},{12... | collective-permute-start | bytes 442376 | tf_op jit(solution)/shard_map/ppermute | solution.py:57
  19.4 2.3 %collective-permute-start.4 = (bf16[4,16,480]{2,1,0:T(8,128)(2,1)S(1)}, bf16[4,16,480]{2,1,0:T(8,128)(2,1)S(1)}, u32[]{:S(2)}, u32[]{:S(2)}) collective-permute-start(bf16[4,16,480]{2,1,0:T(8,128)(2,1)S(1)} %pad_maximum_fusion.2), channel_id=1, source_target_pairs={{0,4},{1,5},{2,6},{3,7},{4,0},{5,1},{6,2},{7,3},{8,12},{9,13},{10,... | collective-permute-start | bytes 184328 | tf_op jit(solution)/shard_map/ppermute | solution.py:33
  21.7 2.2 %collective-permute-start.5 = (bf16[4,16,480]{2,1,0:T(8,128)(2,1)S(1)}, bf16[4,16,480]{2,1,0:T(8,128)(2,1)S(1)}, u32[]{:S(2)}, u32[]{:S(2)}) collective-permute-start(bf16[4,16,480]{2,1,0:T(8,128)(2,1)S(1)} %pad_maximum_fusion.2), channel_id=1, source_target_pairs={{0,6},{1,7},{2,4},{3,5},{4,2},{5,3},{6,0},{7,1},{8,14},{9,15},{10,... | collective-permute-start | bytes 184328 | tf_op jit(solution)/shard_map/ppermute | solution.py:33
  23.9 3.8 %collective-permute-done.5 = bf16[4,16,480]{2,1,0:T(8,128)(2,1)S(1)} collective-permute-done((bf16[4,16,480]{2,1,0:T(8,128)(2,1)S(1)}, bf16[4,16,480]{2,1,0:T(8,128)(2,1)S(1)}, u32[]{:S(2)}, u32[]{:S(2)}) %collective-permute-start.5) | collective-permute-done | bytes 61472 | tf_op jit(solution)/shard_map/ppermute | solution.py:33
  27.7 2.8 %collective-permute-start.6 = (bf16[16,16,480]{2,1,0:T(8,128)(2,1)S(1)}, bf16[16,16,480]{2,1,0:T(8,128)(2,1)S(1)}, u32[]{:S(2)}, u32[]{:S(2)}) collective-permute-start(bf16[16,16,480]{2,1,0:T(8,128)(2,1)S(1)} %constant_dynamic-update-slice_fusion.near_ref), channel_id=1, source_target_pairs={{0,1},{1,0},{2,3},{3,2},{4,5},{5,4},{6,7},{7,6},{8,9},{9,8},{10,11... | collective-permute-start | bytes 737288 | tf_op jit(solution)/shard_map/ppermute | solution.py:33
  32.8 1.6 %collective-permute-start.18 = (bf16[3,160,384]{2,1,0:T(8,128)(2,1)S(1)}, bf16[3,160,384]{2,1,0:T(8,128)(2,1)S(1)}, u32[]{:S(2)}, u32[]{:S(2)}) collective-permute-start(bf16[3,160,384]{2,1,0:T(8,128)(2,1)S(1)} %get-tuple-element.27.p0), channel_id=1, source_target_pairs={{0,24},{8,16},{16,8},{24,0},{1,25},{9,17},{17,9},{25,1},{2,26},{10... | collective-permute-start | bytes 1105928 | tf_op jit(solution)/shard_map/ppermute | solution.py:33
  34.7 18.0 %collective-permute-done.10.w2 = bf16[432,96]{1,0:T(8,128)(2,1)S(1)} collective-permute-done((bf16[432,96]{1,0:T(8,128)(2,1)S(1)}, bf16[432,96]{1,0:T(8,128)(2,1)S(1)}, u32[]{:S(2)}, u32[]{:S(2)}) %collective-permute-start.10) | collective-permute-done | bytes 82976 | tf_op jit(solution)/shard_map/ppermute | solution.py:33
  53.3 3.9 %collective-permute-done.11.w3 = bf16[432,96]{1,0:T(8,128)(2,1)S(1)} collective-permute-done((bf16[432,96]{1,0:T(8,128)(2,1)S(1)}, bf16[432,96]{1,0:T(8,128)(2,1)S(1)}, u32[]{:S(2)}, u32[]{:S(2)}) %collective-permute-start.11) | collective-permute-done | bytes 82976 | tf_op jit(solution)/shard_map/ppermute | solution.py:33
  58.0 4.2 %shard_map.102 = (bf16[3,6,160,384]{3,2,1,0:T(8,128)(2,1)S(1)}, f32[2,384]{1,0:T(2,128)S(1)}) custom-call(s32[32]{0:T(128)S(1)} %copy-done.6, bf16[16,16,480]{2,1,0:T(8,128)(2,1)S(1)} %constant_dynamic-update-slice_fusion.near_ref, bf16[16,16,480]{2,1,0:T(8,128)(2,1)S(1)} %collective-permute-done.6.far_ref, ...), custom_call_target="tpu_custom_call" | custom-call | flops 318504960 | bytes 1048576 | tf_op jit(solution)/shard_map/pallas_call | solution.py:474
  62.3 2.4 %collective-permute-start.12 = (f32[2,384]{1,0:T(2,128)S(1)}, f32[2,384]{1,0:T(2,128)S(1)}, u32[]{:S(2)}, u32[]{:S(2)}) collective-permute-start(f32[2,384]{1,0:T(2,128)S(1)} %get-tuple-element.24), channel_id=1, source_target_pairs={{0,1},{1,0},{2,3},{3,2},{4,5},{5,4},{6,7},{7,6},{8,9},{9,8},{10,11... | collective-permute-start | bytes 9224 | tf_op jit(solution)/shard_map/ppermute | solution.py:33
  64.6 2.5 %shard_map.104 = (bf16[9,384,256]{2,1,0:T(8,128)(2,1)S(1)}, bf16[9,384,256]{2,1,0:T(8,128)(2,1)S(1)}) custom-call(bf16[3,3,3,96,384]{4,3,2,1,0:T(8,128)(2,1)S(1)} %copy-done), custom_call_target="tpu_custom_call" | custom-call | bytes 1048576 | tf_op jit(solution)/shard_map/pallas_call | solution.py:453
  67.2 2.3 %shard_map.107 = (bf16[9,384,256]{2,1,0:T(8,128)(2,1)S(1)}, bf16[9,384,256]{2,1,0:T(8,128)(2,1)S(1)}) custom-call(bf16[3,3,3,96,384]{4,3,2,1,0:T(8,128)(2,1)S(1)} %copy-done.1), custom_call_target="tpu_custom_call" | custom-call | bytes 1048576 | tf_op jit(solution)/shard_map/pallas_call | solution.py:453
  71.2 2.6 %collective-permute-start.15 = (f32[2,2,384]{2,1,0:T(2,128)S(1)}, f32[2,2,384]{2,1,0:T(2,128)S(1)}, u32[]{:S(2)}, u32[]{:S(2)}) collective-permute-start(f32[2,2,384]{2,1,0:T(2,128)S(1)} %pad_maximum_fusion.4.refs_0_), channel_id=1, source_target_pairs={{0,6},{1,7},{2,4},{3,5},{4,2},{5,3},{6,0},{7,1},{8,14},{9,15},{10,... | collective-permute-start | bytes 18440 | tf_op jit(solution)/shard_map/ppermute | solution.py:33
  73.9 3.4 %shard_map.105.refs_9_ = f32[2,640,128]{2,1,0:T(8,128)S(1)} custom-call(bf16[3,160,384]{2,1,0:T(8,128)(2,1)S(1)} %get-tuple-element.27.p0, bf16[3,160,384]{2,1,0:T(8,128)(2,1)S(1)} %collective-permute-done.16.p1, bf16[3,160,384]{2,1,0:T(8,128)(2,1)S(1)} %collective-permute-done.17.p2, bf16[3,160,384]{2,1,0:T(8,128)(2,1)S(1)} %collective-permute-done.18.p3, ...), custom_call_target="tpu_custom_call" | custom-call | flops 1274019840 | bytes 1048576 | tf_op jit(solution)/shard_map/pallas_call | solution.py:463
  77.3 6.6 %shard_map.106 = (bf16[3,160,384]{2,1,0:T(8,128)(2,1)S(1)}, f32[2,128]{1,0:T(2,128)S(1)}) custom-call(f32[2,2,384]{2,1,0:T(2,128)S(1)} %pad_maximum_fusion.4.refs_0_, f32[2,2,384]{2,1,0:T(2,128)S(1)} %collective-permute-done.13.refs_1_, f32[2,2,384]{2,1,0:T(2,128)S(1)} %collective-permute-done.14.refs_2_, f32[2,2,384]{2,1,0:T(2,128)S(1)} %collective-permute-done.15.refs_3_, ...), custom_call_target="tpu_custom_call" | custom-call | flops 2548039680 | bytes 1048576 | tf_op jit(solution)/shard_map/pallas_call | solution.py:495
  87.5 1.2 collective-permute-start.30
  90.6 5.1 %collective-permute-done.28.refs_11_ = bf16[3,160,384]{2,1,0:T(8,128)(2,1)S(1)} collective-permute-done((bf16[3,160,384]{2,1,0:T(8,128)(2,1)S(1)}, bf16[3,160,384]{2,1,0:T(8,128)(2,1)S(1)}, u32[]{:S(2)}, u32[]{:S(2)}) %collective-permute-start.28) | collective-permute-done | bytes 368672 | tf_op jit(solution)/shard_map/ppermute | solution.py:33
  96.6 25.1 %collective-permute-done.27.refs_10_ = bf16[3,160,384]{2,1,0:T(8,128)(2,1)S(1)} collective-permute-done((bf16[3,160,384]{2,1,0:T(8,128)(2,1)S(1)}, bf16[3,160,384]{2,1,0:T(8,128)(2,1)S(1)}, u32[]{:S(2)}, u32[]{:S(2)}) %collective-permute-start.27) | collective-permute-done | bytes 368672 | tf_op jit(solution)/shard_map/ppermute | solution.py:33
  122.7 1.9 %collective-permute-start.32 = (bf16[3,160,384]{2,1,0:T(8,128)(2,1)S(1)}, bf16[3,160,384]{2,1,0:T(8,128)(2,1)S(1)}, u32[]{:S(2)}, u32[]{:S(2)}) collective-permute-start(bf16[3,160,384]{2,1,0:T(8,128)(2,1)S(1)} %pad_maximum_fusion), channel_id=1, source_target_pairs={{0,1},{1,2},{2,3},{3,4},{4,5},{5,6},{6,7},{8,9},{9,10},{10,11},{11... | collective-permute-start | bytes 1105928 | tf_op jit(solution)/shard_map/ppermute | solution.py:53
  124.9 2.6 %collective-permute-start.33 = (bf16[3,160,384]{2,1,0:T(8,128)(2,1)S(1)}, bf16[3,160,384]{2,1,0:T(8,128)(2,1)S(1)}, u32[]{:S(2)}, u32[]{:S(2)}) collective-permute-start(bf16[3,160,384]{2,1,0:T(8,128)(2,1)S(1)} %pad_maximum_fusion.1), channel_id=1, source_target_pairs={{1,0},{2,1},{3,2},{4,3},{5,4},{6,5},{7,6},{9,8},{10,9},{11,10},{12... | collective-permute-start | bytes 1105928 | tf_op jit(solution)/shard_map/ppermute | solution.py:57
  127.6 1.1 collective-permute-start.24
  128.8 2.4 %collective-permute-start.25 = (f32[2,4,2,128]{3,2,1,0:T(2,128)S(1)}, f32[2,4,2,128]{3,2,1,0:T(2,128)S(1)}, u32[]{:S(2)}, u32[]{:S(2)}) collective-permute-start(f32[2,4,2,128]{3,2,1,0:T(2,128)S(1)} %pad_maximum_fusion.3.refs_0_), channel_id=1, source_target_pairs={{0,6},{1,7},{2,4},{3,5},{4,2},{5,3},{6,0},{7,1},{8,14},{9,15},{10,... | collective-permute-start | bytes 24584 | tf_op jit(solution)/shard_map/ppermute | solution.py:33
  131.2 3.3 %shard_map.108.refs_12_ = f32[2,640,128]{2,1,0:T(8,128)S(1)} custom-call(bf16[3,160,384]{2,1,0:T(8,128)(2,1)S(1)} %get-tuple-element.32.p0, bf16[3,160,384]{2,1,0:T(8,128)(2,1)S(1)} %collective-permute-done.29.p1, bf16[3,160,384]{2,1,0:T(8,128)(2,1)S(1)} %collective-permute-done.30.p2, bf16[3,160,384]{2,1,0:T(8,128)(2,1)S(1)} %collective-permute-done.31.p3, ...), custom_call_target="tpu_custom_call" | custom-call | flops 1274019840 | bytes 1048576 | tf_op jit(solution)/shard_map/pallas_call | solution.py:463
  134.5 7.7 %shard_map.109 = (f32[3,640,128]{2,1,0:T(8,128)S(1)}, f32[2,384]{1,0:T(2,128)S(1)}) custom-call(f32[2,4,2,128]{3,2,1,0:T(2,128)S(1)} %pad_maximum_fusion.3.refs_0_, f32[2,4,2,128]{3,2,1,0:T(2,128)S(1)} %collective-permute-done.23.refs_1_, f32[2,4,2,128]{3,2,1,0:T(2,128)S(1)} %collective-permute-done.24.refs_2_, ...), custom_call_target="tpu_custom_call" | custom-call | flops 2548039680 | bytes 1048576 | tf_op jit(solution)/shard_map/pallas_call | solution.py:509
  142.3 2.1 %shard_map.110 = bf16[3,4,160,96]{3,2,1,0:T(8,128)(2,1)} custom-call(f32[3,640,128]{2,1,0:T(8,128)S(1)} %get-tuple-element.35.part_ref, f32[2,384]{1,0:T(2,128)S(1)} %get-tuple-element.36.scale_ref, bf16[3,160,384]{2,1,0:T(8,128)(2,1)S(1)} %collective-permute-done.32.up, bf16[3,160,384]{2,1,0:T(8,128)(2,1)S(1)} %collective-permute-done.33.down, ...), custom_call_target="tpu_custom_call" | custom-call | flops 637009920 | bytes 1048576 | tf_op jit(solution)/shard_map/pallas_call | solution.py:516
  (79 shorter events, 15.7 us)
Async XLA Ops:
  1.5 4.2 %collective-permute-start = (f32[24,480]{1,0:T(8,128)}, f32[24,480]{1,0:T(8,128)S(1)}, u32[]{:S(2)}, u32[]{:S(2)}) collective-permute-start(f32[24,480]{1,0:T(8,128)} %shard_map.100.refs_4_), channel_id=1, source_target_pairs={{0,8},{8,0},{16,24},{24,16},{1,9},{9,1},{17,25},{25,17},{2,10},{10... | collective-permute-start | bytes 138248 | tf_op jit(solution)/shard_map/ppermute | solution.py:33
  4.8 4.0 %collective-permute-start.2 = (f32[24,480]{1,0:T(8,128)}, f32[24,480]{1,0:T(8,128)S(1)}, u32[]{:S(2)}, u32[]{:S(2)}) collective-permute-start(f32[24,480]{1,0:T(8,128)} %shard_map.100.refs_4_), channel_id=1, source_target_pairs={{0,24},{8,16},{16,8},{24,0},{1,25},{9,17},{17,9},{25,1},{2,26},{10... | collective-permute-start | bytes 138248 | tf_op jit(solution)/shard_map/ppermute | solution.py:33
  8.9 12.8 %collective-permute-start.3 = (bf16[4,16,480]{2,1,0:T(8,128)(2,1)S(1)}, bf16[4,16,480]{2,1,0:T(8,128)(2,1)S(1)}, u32[]{:S(2)}, u32[]{:S(2)}) collective-permute-start(bf16[4,16,480]{2,1,0:T(8,128)(2,1)S(1)} %pad_maximum_fusion.2), channel_id=1, source_target_pairs={{0,2},{1,3},{2,0},{3,1},{4,6},{5,7},{6,4},{7,5},{8,10},{9,11},{10,... | collective-permute-start | bytes 184328 | tf_op jit(solution)/shard_map/ppermute | solution.py:33
  12.5 18.0 %collective-permute-start.7 = (bf16[192,384]{1,0:T(8,128)(2,1)}, bf16[192,384]{1,0:T(8,128)(2,1)S(1)}, u32[]{:S(2)}, u32[]{:S(2)}) collective-permute-start(bf16[192,384]{1,0:T(8,128)(2,1)} %get-tuple-element.21), channel_id=1, source_target_pairs={{0,1},{1,2},{2,3},{3,4},{4,5},{5,6},{6,7},{8,9},{9,10},{10,11},{11... | collective-permute-start | bytes 442376 | tf_op jit(solution)/shard_map/ppermute | solution.py:53
  17.1 13.4 %collective-permute-start.8 = (bf16[192,384]{1,0:T(8,128)(2,1)}, bf16[192,384]{1,0:T(8,128)(2,1)S(1)}, u32[]{:S(2)}, u32[]{:S(2)}) collective-permute-start(bf16[192,384]{1,0:T(8,128)(2,1)} %get-tuple-element.23), channel_id=1, source_target_pairs={{1,0},{2,1},{3,2},{4,3},{5,4},{6,5},{7,6},{9,8},{10,9},{11,10},{12... | collective-permute-start | bytes 442376 | tf_op jit(solution)/shard_map/ppermute | solution.py:57
  19.0 15.4 %collective-permute-start.9 = (bf16[432,96]{1,0:T(8,128)(2,1)}, bf16[432,96]{1,0:T(8,128)(2,1)S(1)}, u32[]{:S(2)}, u32[]{:S(2)}) collective-permute-start(bf16[432,96]{1,0:T(8,128)(2,1)} %bitcast.27), channel_id=1, source_target_pairs={{0,8},{8,0},{16,24},{24,16},{1,9},{9,1},{17,25},{25,17},{2,10},{10... | collective-permute-start | bytes 248840 | tf_op jit(solution)/shard_map/ppermute | solution.py:33
  19.4 4.5 %collective-permute-start.4 = (bf16[4,16,480]{2,1,0:T(8,128)(2,1)S(1)}, bf16[4,16,480]{2,1,0:T(8,128)(2,1)S(1)}, u32[]{:S(2)}, u32[]{:S(2)}) collective-permute-start(bf16[4,16,480]{2,1,0:T(8,128)(2,1)S(1)} %pad_maximum_fusion.2), channel_id=1, source_target_pairs={{0,4},{1,5},{2,6},{3,7},{4,0},{5,1},{6,2},{7,3},{8,12},{9,13},{10,... | collective-permute-start | bytes 184328 | tf_op jit(solution)/shard_map/ppermute | solution.py:33
  21.7 6.0 %collective-permute-start.5 = (bf16[4,16,480]{2,1,0:T(8,128)(2,1)S(1)}, bf16[4,16,480]{2,1,0:T(8,128)(2,1)S(1)}, u32[]{:S(2)}, u32[]{:S(2)}) collective-permute-start(bf16[4,16,480]{2,1,0:T(8,128)(2,1)S(1)} %pad_maximum_fusion.2), channel_id=1, source_target_pairs={{0,6},{1,7},{2,4},{3,5},{4,2},{5,3},{6,0},{7,1},{8,14},{9,15},{10,... | collective-permute-start | bytes 184328 | tf_op jit(solution)/shard_map/ppermute | solution.py:33
  27.7 29.5 %collective-permute-start.6 = (bf16[16,16,480]{2,1,0:T(8,128)(2,1)S(1)}, bf16[16,16,480]{2,1,0:T(8,128)(2,1)S(1)}, u32[]{:S(2)}, u32[]{:S(2)}) collective-permute-start(bf16[16,16,480]{2,1,0:T(8,128)(2,1)S(1)} %constant_dynamic-update-slice_fusion.near_ref), channel_id=1, source_target_pairs={{0,1},{1,0},{2,3},{3,2},{4,5},{5,4},{6,7},{7,6},{8,9},{9,8},{10,11... | collective-permute-start | bytes 737288 | tf_op jit(solution)/shard_map/ppermute | solution.py:33
  31.7 39.5 %collective-permute-start.16 = (bf16[3,160,384]{2,1,0:T(8,128)(2,1)S(1)}, bf16[3,160,384]{2,1,0:T(8,128)(2,1)S(1)}, u32[]{:S(2)}, u32[]{:S(2)}) collective-permute-start(bf16[3,160,384]{2,1,0:T(8,128)(2,1)S(1)} %get-tuple-element.27.p0), channel_id=1, source_target_pairs={{0,8},{8,0},{16,24},{24,16},{1,9},{9,1},{17,25},{25,17},{2,10},{10... | collective-permute-start | bytes 1105928 | tf_op jit(solution)/shard_map/ppermute | solution.py:33
  32.6 38.6 %collective-permute-start.17 = (bf16[3,160,384]{2,1,0:T(8,128)(2,1)S(1)}, bf16[3,160,384]{2,1,0:T(8,128)(2,1)S(1)}, u32[]{:S(2)}, u32[]{:S(2)}) collective-permute-start(bf16[3,160,384]{2,1,0:T(8,128)(2,1)S(1)} %get-tuple-element.27.p0), channel_id=1, source_target_pairs={{0,16},{8,24},{16,0},{24,8},{1,17},{9,25},{17,1},{25,9},{2,18},{10... | collective-permute-start | bytes 1105928 | tf_op jit(solution)/shard_map/ppermute | solution.py:33
  32.8 41.1 %collective-permute-start.18 = (bf16[3,160,384]{2,1,0:T(8,128)(2,1)S(1)}, bf16[3,160,384]{2,1,0:T(8,128)(2,1)S(1)}, u32[]{:S(2)}, u32[]{:S(2)}) collective-permute-start(bf16[3,160,384]{2,1,0:T(8,128)(2,1)S(1)} %get-tuple-element.27.p0), channel_id=1, source_target_pairs={{0,24},{8,16},{16,8},{24,0},{1,25},{9,17},{17,9},{25,1},{2,26},{10... | collective-permute-start | bytes 1105928 | tf_op jit(solution)/shard_map/ppermute | solution.py:33
  34.5 18.3 %collective-permute-start.10 = (bf16[432,96]{1,0:T(8,128)(2,1)S(1)}, bf16[432,96]{1,0:T(8,128)(2,1)S(1)}, u32[]{:S(2)}, u32[]{:S(2)}) collective-permute-start(bf16[432,96]{1,0:T(8,128)(2,1)S(1)} %bitcast.28), channel_id=1, source_target_pairs={{0,16},{8,24},{16,0},{24,8},{1,17},{9,25},{17,1},{25,9},{2,18},{10... | collective-permute-start | bytes 248840 | tf_op jit(solution)/shard_map/ppermute | solution.py:33
  52.7 4.5 %collective-permute-start.11 = (bf16[432,96]{1,0:T(8,128)(2,1)S(1)}, bf16[432,96]{1,0:T(8,128)(2,1)S(1)}, u32[]{:S(2)}, u32[]{:S(2)}) collective-permute-start(bf16[432,96]{1,0:T(8,128)(2,1)S(1)} %bitcast.29), channel_id=1, source_target_pairs={{0,24},{8,16},{16,8},{24,0},{1,25},{9,17},{17,9},{25,1},{2,26},{10... | collective-permute-start | bytes 248840 | tf_op jit(solution)/shard_map/ppermute | solution.py:33
  62.3 8.0 %collective-permute-start.12 = (f32[2,384]{1,0:T(2,128)S(1)}, f32[2,384]{1,0:T(2,128)S(1)}, u32[]{:S(2)}, u32[]{:S(2)}) collective-permute-start(f32[2,384]{1,0:T(2,128)S(1)} %get-tuple-element.24), channel_id=1, source_target_pairs={{0,1},{1,0},{2,3},{3,2},{4,5},{5,4},{6,7},{7,6},{8,9},{9,8},{10,11... | collective-permute-start | bytes 9224 | tf_op jit(solution)/shard_map/ppermute | solution.py:33
  69.5 58.0 %collective-permute-start.29 = (bf16[3,160,384]{2,1,0:T(8,128)(2,1)S(1)}, bf16[3,160,384]{2,1,0:T(8,128)(2,1)S(1)}, u32[]{:S(2)}, u32[]{:S(2)}) collective-permute-start(bf16[3,160,384]{2,1,0:T(8,128)(2,1)S(1)} %get-tuple-element.32.p0), channel_id=1, source_target_pairs={{0,8},{8,0},{16,24},{24,16},{1,9},{9,1},{17,25},{25,17},{2,10},{10... | collective-permute-start | bytes 1105928 | tf_op jit(solution)/shard_map/ppermute | solution.py:33
  70.3 7.0 %collective-permute-start.13 = (f32[2,2,384]{2,1,0:T(2,128)S(1)}, f32[2,2,384]{2,1,0:T(2,128)S(1)}, u32[]{:S(2)}, u32[]{:S(2)}) collective-permute-start(f32[2,2,384]{2,1,0:T(2,128)S(1)} %pad_maximum_fusion.4.refs_0_), channel_id=1, source_target_pairs={{0,2},{1,3},{2,0},{3,1},{4,6},{5,7},{6,4},{7,5},{8,10},{9,11},{10,... | collective-permute-start | bytes 18440 | tf_op jit(solution)/shard_map/ppermute | solution.py:33
  71.2 6.0 %collective-permute-start.14 = (f32[2,2,384]{2,1,0:T(2,128)S(1)}, f32[2,2,384]{2,1,0:T(2,128)S(1)}, u32[]{:S(2)}, u32[]{:S(2)}) collective-permute-start(f32[2,2,384]{2,1,0:T(2,128)S(1)} %pad_maximum_fusion.4.refs_0_), channel_id=1, source_target_pairs={{0,4},{1,5},{2,6},{3,7},{4,0},{5,1},{6,2},{7,3},{8,12},{9,13},{10,... | collective-permute-start | bytes 18440 | tf_op jit(solution)/shard_map/ppermute | solution.py:33
  71.2 6.0 %collective-permute-start.15 = (f32[2,2,384]{2,1,0:T(2,128)S(1)}, f32[2,2,384]{2,1,0:T(2,128)S(1)}, u32[]{:S(2)}, u32[]{:S(2)}) collective-permute-start(f32[2,2,384]{2,1,0:T(2,128)S(1)} %pad_maximum_fusion.4.refs_0_), channel_id=1, source_target_pairs={{0,6},{1,7},{2,4},{3,5},{4,2},{5,3},{6,0},{7,1},{8,14},{9,15},{10,... | collective-permute-start | bytes 18440 | tf_op jit(solution)/shard_map/ppermute | solution.py:33
  83.9 3.7 %collective-permute-start.21 = (f32[2,128]{1,0:T(2,128)S(1)}, f32[2,128]{1,0:T(2,128)S(1)}, u32[]{:S(2)}, u32[]{:S(2)}) collective-permute-start(f32[2,128]{1,0:T(2,128)S(1)} %get-tuple-element.30), channel_id=1, source_target_pairs={{0,24},{8,16},{16,8},{24,0},{1,25},{9,17},{17,9},{25,1},{2,26},{10... | collective-permute-start | bytes 3080 | tf_op jit(solution)/shard_map/ppermute | solution.py:33
  84.8 3.9 %collective-permute-start.20 = (f32[2,128]{1,0:T(2,128)S(1)}, f32[2,128]{1,0:T(2,128)S(1)}, u32[]{:S(2)}, u32[]{:S(2)}) collective-permute-start(f32[2,128]{1,0:T(2,128)S(1)} %get-tuple-element.30), channel_id=1, source_target_pairs={{0,16},{8,24},{16,0},{24,8},{1,17},{9,25},{17,1},{25,9},{2,18},{10... | collective-permute-start | bytes 3080 | tf_op jit(solution)/shard_map/ppermute | solution.py:33
  85.9 3.8 %collective-permute-start.19 = (f32[2,128]{1,0:T(2,128)S(1)}, f32[2,128]{1,0:T(2,128)S(1)}, u32[]{:S(2)}, u32[]{:S(2)}) collective-permute-start(f32[2,128]{1,0:T(2,128)S(1)} %get-tuple-element.30), channel_id=1, source_target_pairs={{0,8},{8,0},{16,24},{24,16},{1,9},{9,1},{17,25},{25,17},{2,10},{10... | collective-permute-start | bytes 3080 | tf_op jit(solution)/shard_map/ppermute | solution.py:33
  86.6 9.2 %collective-permute-start.28 = (bf16[3,160,384]{2,1,0:T(8,128)(2,1)S(1)}, bf16[3,160,384]{2,1,0:T(8,128)(2,1)S(1)}, u32[]{:S(2)}, u32[]{:S(2)}) collective-permute-start(bf16[3,160,384]{2,1,0:T(8,128)(2,1)S(1)} %get-tuple-element.31.refs_8_), channel_id=1, source_target_pairs={{0,24},{8,16},{16,8},{24,0},{1,25},{9,17},{17,9},{25,1},{2,26},{10... | collective-permute-start | bytes 1105928 | tf_op jit(solution)/shard_map/ppermute | solution.py:33
  87.5 40.1 %collective-permute-start.30 = (bf16[3,160,384]{2,1,0:T(8,128)(2,1)S(1)}, bf16[3,160,384]{2,1,0:T(8,128)(2,1)S(1)}, u32[]{:S(2)}, u32[]{:S(2)}) collective-permute-start(bf16[3,160,384]{2,1,0:T(8,128)(2,1)S(1)} %get-tuple-element.32.p0), channel_id=1, source_target_pairs={{0,16},{8,24},{16,0},{24,8},{1,17},{9,25},{17,1},{25,9},{2,18},{10... | collective-permute-start | bytes 1105928 | tf_op jit(solution)/shard_map/ppermute | solution.py:33
  88.7 40.0 %collective-permute-start.31 = (bf16[3,160,384]{2,1,0:T(8,128)(2,1)S(1)}, bf16[3,160,384]{2,1,0:T(8,128)(2,1)S(1)}, u32[]{:S(2)}, u32[]{:S(2)}) collective-permute-start(bf16[3,160,384]{2,1,0:T(8,128)(2,1)S(1)} %get-tuple-element.32.p0), channel_id=1, source_target_pairs={{0,24},{8,16},{16,8},{24,0},{1,25},{9,17},{17,9},{25,1},{2,26},{10... | collective-permute-start | bytes 1105928 | tf_op jit(solution)/shard_map/ppermute | solution.py:33
  89.7 32.0 %collective-permute-start.27 = (bf16[3,160,384]{2,1,0:T(8,128)(2,1)S(1)}, bf16[3,160,384]{2,1,0:T(8,128)(2,1)S(1)}, u32[]{:S(2)}, u32[]{:S(2)}) collective-permute-start(bf16[3,160,384]{2,1,0:T(8,128)(2,1)S(1)} %get-tuple-element.31.refs_8_), channel_id=1, source_target_pairs={{0,16},{8,24},{16,0},{24,8},{1,17},{9,25},{17,1},{25,9},{2,18},{10... | collective-permute-start | bytes 1105928 | tf_op jit(solution)/shard_map/ppermute | solution.py:33
  95.7 26.6 %collective-permute-start.26 = (bf16[3,160,384]{2,1,0:T(8,128)(2,1)S(1)}, bf16[3,160,384]{2,1,0:T(8,128)(2,1)S(1)}, u32[]{:S(2)}, u32[]{:S(2)}) collective-permute-start(bf16[3,160,384]{2,1,0:T(8,128)(2,1)S(1)} %get-tuple-element.31.refs_8_), channel_id=1, source_target_pairs={{0,8},{8,0},{16,24},{24,16},{1,9},{9,1},{17,25},{25,17},{2,10},{10... | collective-permute-start | bytes 1105928 | tf_op jit(solution)/shard_map/ppermute | solution.py:33
  122.7 19.6 %collective-permute-start.32 = (bf16[3,160,384]{2,1,0:T(8,128)(2,1)S(1)}, bf16[3,160,384]{2,1,0:T(8,128)(2,1)S(1)}, u32[]{:S(2)}, u32[]{:S(2)}) collective-permute-start(bf16[3,160,384]{2,1,0:T(8,128)(2,1)S(1)} %pad_maximum_fusion), channel_id=1, source_target_pairs={{0,1},{1,2},{2,3},{3,4},{4,5},{5,6},{6,7},{8,9},{9,10},{10,11},{11... | collective-permute-start | bytes 1105928 | tf_op jit(solution)/shard_map/ppermute | solution.py:53
  124.9 17.4 %collective-permute-start.33 = (bf16[3,160,384]{2,1,0:T(8,128)(2,1)S(1)}, bf16[3,160,384]{2,1,0:T(8,128)(2,1)S(1)}, u32[]{:S(2)}, u32[]{:S(2)}) collective-permute-start(bf16[3,160,384]{2,1,0:T(8,128)(2,1)S(1)} %pad_maximum_fusion.1), channel_id=1, source_target_pairs={{1,0},{2,1},{3,2},{4,3},{5,4},{6,5},{7,6},{9,8},{10,9},{11,10},{12... | collective-permute-start | bytes 1105928 | tf_op jit(solution)/shard_map/ppermute | solution.py:57
  127.5 7.0 %collective-permute-start.23 = (f32[2,4,2,128]{3,2,1,0:T(2,128)S(1)}, f32[2,4,2,128]{3,2,1,0:T(2,128)S(1)}, u32[]{:S(2)}, u32[]{:S(2)}) collective-permute-start(f32[2,4,2,128]{3,2,1,0:T(2,128)S(1)} %pad_maximum_fusion.3.refs_0_), channel_id=1, source_target_pairs={{0,2},{1,3},{2,0},{3,1},{4,6},{5,7},{6,4},{7,5},{8,10},{9,11},{10,... | collective-permute-start | bytes 24584 | tf_op jit(solution)/shard_map/ppermute | solution.py:33
  127.6 6.9 %collective-permute-start.24 = (f32[2,4,2,128]{3,2,1,0:T(2,128)S(1)}, f32[2,4,2,128]{3,2,1,0:T(2,128)S(1)}, u32[]{:S(2)}, u32[]{:S(2)}) collective-permute-start(f32[2,4,2,128]{3,2,1,0:T(2,128)S(1)} %pad_maximum_fusion.3.refs_0_), channel_id=1, source_target_pairs={{0,4},{1,5},{2,6},{3,7},{4,0},{5,1},{6,2},{7,3},{8,12},{9,13},{10,... | collective-permute-start | bytes 24584 | tf_op jit(solution)/shard_map/ppermute | solution.py:33
  128.8 5.8 %collective-permute-start.25 = (f32[2,4,2,128]{3,2,1,0:T(2,128)S(1)}, f32[2,4,2,128]{3,2,1,0:T(2,128)S(1)}, u32[]{:S(2)}, u32[]{:S(2)}) collective-permute-start(f32[2,4,2,128]{3,2,1,0:T(2,128)S(1)} %pad_maximum_fusion.3.refs_0_), channel_id=1, source_target_pairs={{0,6},{1,7},{2,4},{3,5},{4,2},{5,3},{6,0},{7,1},{8,14},{9,15},{10,... | collective-permute-start | bytes 24584 | tf_op jit(solution)/shard_map/ppermute | solution.py:33
  (9 other events, 197.6 us)
where the time goes:
time: 146 us; the launch traced here: 145 us
  waiting for transfers between devices  59.2 us (41%)
  starting transfers between devices  45.2 us (31%)
  Pallas kernels  36 us (25%)
  local copies, waits for them, and re-layouts  3.11 us (2%)
    ppermute x30, waiting for transfers between devices, xor_send(): lax.ppermute(x, axis, [(i, i ^ mask) for i in range(lax.axis_size(axis))])  59.2 us
    ppermute x30, starting transfers between devices, xor_send(): lax.ppermute(x, axis, [(i, i ^ mask) for i in range(lax.axis_size(axis))])  34 us
    pallas_call x1, Pallas kernels, window(): call(functools.partial(last_body, len(stats), count), (shaped((frames, sp...  7.7 us
    pallas_call x2, Pallas kernels, cached(): call(cached_body, shaped((2, spots, 128), F32), flops=flops, scratch=[plt...  6.69 us
    pallas_call x1, Pallas kernels, window(): call(functools.partial(middle_body, len(stats), count), (shaped((frames,...  6.56 us
    ppermute x2, starting transfers between devices, to_next(): lax.ppermute(x, 'tile', [(i, i + 1) for i in range(lax.axis_size('tile')...  6.55 us
    pallas_call x2, Pallas kernels, turn(): call(weights_body, (shape, shape), scratch=[pltpu.VMEM((wide, channels),...  4.84 us
    ppermute x2, starting transfers between devices, to_previous(): lax.ppermute(x, 'tile', [(i + 1, i) for i in range(lax.axis_size('tile')...  4.57 us
  transfers between devices with their start and end apart: 34, of which 7 were waited for; matrix products, arithmetic and copies ran while one was open for 1% of the time, Pallas kernels for 22%

commit v1 on v0

--- a/solution.py
+++ b/solution.py
@@ -17,13 +17,14 @@
 HBM = pl.BlockSpec(memory_space=pl.ANY)
 
 
-def call(body, outs, flops=0, scratch=(), specs=None, n_in=0, out_specs=None, limit=VMEM_LIMIT):
+def call(body, outs, flops=0, scratch=(), specs=None, n_in=0, out_specs=None, limit=VMEM_LIMIT, alias=None):
     return pl.pallas_call(
         body,
         out_shape=outs,
         in_specs=specs if specs is not None else [VMEM] * n_in,
         out_specs=out_specs if out_specs is not None else jax.tree.map(lambda _: VMEM, outs),
         scratch_shapes=list(scratch),
+        input_output_aliases=alias or {},
         cost_estimate=pl.CostEstimate(flops=flops, bytes_accessed=1 << 20, transcendentals=0),
         compiler_params=pltpu.CompilerParams(vmem_limit_bytes=limit),
     )
@@ -49,6 +50,10 @@
     return stages
 
 
+def stay(*arrays):
+    return [pltpu.with_memory_space_constraint(x, pltpu.HBM) for x in arrays]
+
+
 def to_next(x):
     return lax.ppermute(x, "tile", [(i, i + 1) for i in range(lax.axis_size("tile") - 1)])
 
@@ -65,19 +70,41 @@
         copy.wait()
 
 
+GROUP = 5
+
+
 def message_body(*refs):
-    out_ref, latent_ref, gain_a, gain_b, sems = refs[3:]
-    fetch(refs[:3], (latent_ref, gain_a, gain_b), sems)
+    out_ref, latent_ref, gain_a, gain_b, w_ref, sems = refs[4:]
+    fetch(refs[:4], (latent_ref, gain_a, gain_b, w_ref), sems)
     lc, channels = latent_ref.shape[2], gain_a.shape[1]
-    line = jnp.concatenate([latent_ref[f, 0].astype(F32) for f in range(latent_ref.shape[0])], axis=1)
+
+    def joined(parts):
+        return jnp.concatenate([part.astype(F32) for part in parts], axis=1).astype(BF16)
+
+    out_ref[0:lc, :] = joined([latent_ref[f, 0] for f in range(latent_ref.shape[0])])
+    taps = w_ref.shape[0] // lc
+    for n in range(0, taps, GROUP):
+        held = [w_ref[k * lc : (k + 1) * lc] for k in range(n, min(n + GROUP, taps))]
+        at = lc + n // GROUP * lc
+        out_ref[at : at + lc, 0 : len(held) * channels] = joined(held)
     gains = jnp.concatenate([gain_a[...], gain_b[...]], axis=1)
-    out_ref[0:lc, :] = line
-    out_ref[lc:, :] = jnp.zeros_like(out_ref[lc:, :])
-    out_ref[lc : lc + 1, 0 : 2 * channels] = gains
+    at = out_ref.shape[0] - 16
+    terms = []
+    for _ in range(3):
+        terms.append(gains.astype(BF16).astype(F32))
+        gains = gains - terms[-1]
+    rows = jnp.concatenate(terms + [jnp.zeros((13, gains.shape[1]), F32)], axis=0)
+    out_ref[at:, 0 : gains.shape[1]] = rows.astype(BF16)
+
+
+def near_body(*refs):
+    out_ref = refs[-1]
+    for n, ref in enumerate(refs[:-1]):
+        out_ref[n] = ref[0 : out_ref.shape[1], :]
 
 
 def pack_body(*refs):
-    packed_ref, own_ref, low_ref, high_ref, *here, sems = refs[3:]
+    own_one, own_two, span_out, low_ref, high_ref, *here, sems = refs[3:]
     fetch(refs[:3], here, sems)
     one_ref, two_ref, span_ref = here
     frames, rows = one_ref.shape[0], one_ref.shape[1]
@@ -86,9 +113,10 @@
     def joined(parts):
         return jnp.concatenate([part.astype(F32) for part in parts], axis=1).astype(BF16)
 
+    for ref, out in ((one_ref, own_one), (two_ref, own_two)):
+        for f in range(frames):
+            out[f] = joined([ref[f, h] for h in range(rows)])
     every = [ref.at[f] for ref in (one_ref, two_ref) for f in range(frames)]
-    for n, ref in enumerate(every):
-        packed_ref[n] = joined([ref[h] for h in range(rows)])
     low_ref[0:columns, :] = joined([ref[0] for ref in every])
     high_ref[0:columns, :] = joined([ref[rows - 1] for ref in every])
     width = span_ref.shape[3] * frames
@@ -96,7 +124,7 @@
         ref[columns:, :] = jnp.zeros_like(ref[columns:, :])
     for row in range(rows):
         both = joined([span_ref[f, row] for f in range(frames)])
-        own_ref[row] = both
+        span_out[row] = both
         if row < 2:
             low_ref[columns + row * lc : columns + (row + 1) * lc, 0:width] = both
         if row >= rows - 2:
@@ -104,45 +132,45 @@
             high_ref[at : at + lc, 0:width] = both
 
 
-def rim_body(packed_ref, before, after, one_ref, two_ref):
-    columns = packed_ref.shape[1]
-    channels = packed_ref.shape[2] // 4
-    for n, ref in enumerate((one_ref, two_ref)):
+def rim_body(one_in, two_in, before, after, one_out, two_out, held, sems):
+    columns = held.shape[1]
+    channels = held.shape[2] // 4
+    copies = []
+    for n, out in enumerate((one_out, two_out)):
         parts = []
         for f in range(2):
-            ref[f] = packed_ref[2 * n + f]
             lanes = slice((2 * n + f) * channels, (2 * n + f + 1) * channels)
             parts += [side[0:columns, lanes].astype(F32) for side in (before, after)]
-        ref[2] = jnp.concatenate(parts, axis=1).astype(BF16)
+        held[n] = jnp.concatenate(parts, axis=1).astype(BF16)
+        copies.append(pltpu.make_async_copy(held.at[n], out.at[2], sems.at[n]))
+        copies[-1].start()
+    for copy in copies:
+        copy.wait()
 
 
 def weights_body(w_ref, late_ref, early_ref, turned):
     outs, ins = w_ref.shape[3], w_ref.shape[4]
     mine = lax.axis_index("src")
-    late_ref[...] = jnp.zeros_like(late_ref)
-    early_ref[...] = jnp.zeros_like(early_ref)
+    turned[...] = jnp.zeros_like(turned)
 
     def tap(n, _):
         b, e = n // 3, n % 3
         for a in range(3):
-            turned[...] = w_ref[a, b, e].astype(F32).T
-            for slot in range(ins // outs):
-                start = pl.multiple_of(jnp.bitwise_xor(mine, slot) * outs, 8)
-                rows = turned[pl.ds(start, outs), :].astype(BF16)
-                here = pl.ds(slot * outs, outs)
-                if a == 2:
-                    late_ref[n, here, 0:outs] = rows
-                if a == 1:
-                    late_ref[n, here, 128 : 128 + outs] = rows
-                    early_ref[n, here, 0:outs] = rows
-                if a == 0:
-                    early_ref[n, here, 128 : 128 + outs] = rows
+            turned[a, :, 0:outs] = w_ref[a, b, e].astype(F32).T
+        for slot in range(ins // outs):
+            start = pl.multiple_of(jnp.bitwise_xor(mine, slot) * outs, 8)
+            here = pl.ds(slot * outs, outs)
+            early, middle, late = [turned[a, pl.ds(start, outs), :].astype(BF16) for a in range(3)]
+            late_ref[n, here, 0:128] = late
+            late_ref[n, here, 128:256] = middle
+            early_ref[n, here, 0:128] = middle
+            early_ref[n, here, 128:256] = early
         return 0
 
     lax.fori_loop(0, 9, tap, 0)
 
 
-def first_body(map_ref, near_ref, far_ref, before, own, after, w0, w1, w2, w3, first_ref, stat_ref, taps, wall, tab_ref):
+def first_body(map_ref, near_ref, far_ref, before, own, after, m0, m1, m2, m3, first_ref, stat_ref, taps, wall, tab_ref):
     half = near_ref.shape[0]
     rows = own.shape[0] + 4
     columns = own.shape[2] // 2
@@ -160,7 +188,11 @@
         def _():
             tab_ref[jnp.clip(at, 0, rows - 1)] = place
 
-    wall[...] = jnp.concatenate([w[...].astype(F32) for w in (w0, w1, w2, w3)], axis=1).astype(BF16)
+    wide = wall.shape[1]
+    for n in range(wall.shape[0] // 16):
+        at, lanes = 16 + n // GROUP * 16, slice(n % GROUP * wide // 4, (n % GROUP + 1) * wide // 4)
+        parts = [m[at : at + 16, lanes].astype(F32) for m in (m0, m1, m2, m3)]
+        wall[16 * n : 16 * n + 16, :] = jnp.concatenate(parts, axis=1).astype(BF16)
     for row in range(rows):
         place = tab_ref[row]
         kept = (place >= 0).astype(F32)
@@ -281,9 +313,10 @@
 
 
 def gain_of(refs, n, channels):
-    at = refs[0].shape[0] - 8
+    at = refs[0].shape[0] - 16
     lanes = slice(n * channels, (n + 1) * channels)
-    return jnp.concatenate([ref[at : at + 1, lanes] for ref in refs], axis=1)
+    terms = [ref[at : at + 16, lanes].astype(F32) for ref in refs]
+    return jnp.concatenate([(t[0:1] + t[1:2]) + t[2:3] for t in terms], axis=1)
 
 
 def inside():
@@ -413,44 +446,51 @@
     wide = channels * sources
     others = range(1, sources)
 
+    taps = 27 * lc
+    height = lc + -(-27 // GROUP) * lc + 16
     message = call(
         message_body,
-        shaped((lc + 8, frames * columns), F32),
+        shaped((height, frames * columns), BF16),
         scratch=[
             pltpu.VMEM(latent.shape, BF16),
             pltpu.VMEM((1, channels), F32),
             pltpu.VMEM((1, channels), F32),
-            pltpu.SemaphoreType.DMA((3,)),
+            pltpu.VMEM((taps, channels), BF16),
+            pltpu.SemaphoreType.DMA((4,)),
         ],
-        specs=[HBM] * 3,
-        limit=60 * 1024 * 1024,
-    )(latent, gain_one[None], gain_two[None])
+        specs=[HBM] * 4,
+    )(*stay(latent, gain_one[None], gain_two[None], conv_in_w.reshape(taps, channels)))
     got = xor_stage(message, "src", others)
-    near = jnp.stack([x[:lc].astype(BF16) for x in got])
+    near = call(near_body, shaped((sources, lc, frames * columns), BF16), n_in=sources)(*got)
     for masks in far_masks(tiles):
         near = jnp.concatenate(xor_stage(near, "tile", masks), axis=0)
     far = xor_send(near, "tile", 1)
 
-    w_in = xor_stage(conv_in_w.reshape(27 * lc, channels), "src", others)
     caches = (cache_one.transpose(0, 1, 3, 2), cache_two.transpose(0, 1, 3, 2), latent_cache)
     strip = shaped((columns + 2 * lc, tile_rows * channels), BF16)
-    packed, span, low, high = call(
+    rimmed = shaped((3, columns, tile_rows * channels), BF16)
+    own_one, own_two, span, low, high = call(
         pack_body,
-        (shaped((4, columns, tile_rows * channels), BF16), shaped((tile_rows, lc, 2 * columns), BF16), strip, strip),
+        (rimmed, rimmed, shaped((tile_rows, lc, 2 * columns), BF16), strip, strip),
         scratch=[pltpu.VMEM(x.shape, BF16) for x in caches] + [pltpu.SemaphoreType.DMA((3,))],
         specs=[HBM] * 3,
-        limit=60 * 1024 * 1024,
-    )(*caches)
+    )(*stay(*caches))
     before = to_next(high)
     after = to_previous(low)
-    rimmed = shaped((3, columns, tile_rows * channels), BF16)
-    rim_one, rim_two = call(rim_body, (rimmed, rimmed), n_in=3)(packed, before, after)
+    rim_one, rim_two = call(
+        rim_body,
+        (rimmed, rimmed),
+        scratch=[pltpu.VMEM((2, columns, tile_rows * channels), BF16), pltpu.SemaphoreType.DMA((2,))],
+        specs=[HBM, HBM, VMEM, VMEM],
+        out_specs=(HBM, HBM),
+        alias={0: 0, 1: 1},
+    )(own_one, own_two, before, after)
     pieces_one = xor_stage(rim_one, "src", others)
     pieces_two = xor_stage(rim_two, "src", others)
 
     def turn(w):
         shape = shaped((9, wide, 256), BF16)
-        return call(weights_body, (shape, shape), scratch=[pltpu.VMEM((wide, channels), F32)], n_in=1)(w)
+        return call(weights_body, (shape, shape), scratch=[pltpu.VMEM((3, wide, 128), F32)], n_in=1)(w)
 
     late_one, early_one = turn(weight_one)
     late_two, early_two = turn(weight_two)
@@ -481,7 +521,7 @@
             pltpu.SMEM((rows + 2,), jnp.int32),
         ],
         specs=[SMEM] + [VMEM] * 9,
-    )(row_map, near, far, before, span, after, *w_in)
+    )(row_map, near, far, before, span, after, *got)
 
     def over_tiles(x):
         x = jnp.stack(xor_stage(x, "tile", [1]))

time: 146 us -> 120 us (0.82)
  waiting for transfers between devices: 59.2 us -> 41.9 us
  starting transfers between devices: 45.2 us -> 39.7 us
  local copies, waits for them, and re-layouts: 3.11 us -> 0.43 us
    ppermute x30 -> x27, waiting for transfers between devices: 59.2 us -> 37.5 us  [xor_send(): lax.ppermute(x, axis, [(i, i ^ mask) for i in range(lax.axis_size(axis))])]
    ppermute x30 -> x27, starting transfers between devices: 34 us -> 25.6 us  [xor_send(): lax.ppermute(x, axis, [(i, i ^ mask) for i in range(lax.axis_size(axis))])]
    ppermute x2, waiting for transfers between devices: 0.01 us -> 4.36 us  [to_previous(): lax.ppermute(x, 'tile', [(i + 1, i) for i in range(lax.axis_size('tile')...]
    ppermute x2, starting transfers between devices: 6.55 us -> 10.1 us  [to_next(): lax.ppermute(x, 'tile', [(i, i + 1) for i in range(lax.axis_size('tile')...]
    unnamed x20 -> x6, local copies, waits for them, and re-layouts: 2.68 us -> 0.01 us
    pallas_call x5 -> x6, Pallas kernels: 8.71 us -> 7.9 us  [the longest x2 4.7 us: turn(): call(weights_body, (shape, shape), scratch=[pltpu.VMEM((3, wide, 128), F3...]
  transfers between devices with their start and end apart: 34 -> 31, of which waited for: 7 -> 9; matrix products, arithmetic and copies ran while one was open for 1% -> 1% of each run, Pallas kernels for 22% -> 27%
where the time goes in v1:
time: 120 us; the launch traced here: 118 us
  waiting for transfers between devices  41.9 us (35%)
  starting transfers between devices  39.7 us (33%)
  Pallas kernels  35.1 us (29%)
    ppermute x27, waiting for transfers between devices, xor_send(): lax.ppermute(x, axis, [(i, i ^ mask) for i in range(lax.axis_size(axis))])  37.5 us
    ppermute x27, starting transfers between devices, xor_send(): lax.ppermute(x, axis, [(i, i ^ mask) for i in range(lax.axis_size(axis))])  25.6 us
    ppermute x2, starting transfers between devices, to_next(): lax.ppermute(x, 'tile', [(i, i + 1) for i in range(lax.axis_size('tile')...  10.1 us
    pallas_call x1, Pallas kernels, window(): call(functools.partial(last_body, len(stats), count), (shaped((frames, sp...  7.69 us
    pallas_call x2, Pallas kernels, cached(): call(cached_body, shaped((2, spots, 128), F32), flops=flops, scratch=[plt...  6.69 us
    pallas_call x1, Pallas kernels, window(): call(functools.partial(middle_body, len(stats), count), (shaped((frames,...  6.54 us
    pallas_call x2, Pallas kernels, turn(): call(weights_body, (shape, shape), scratch=[pltpu.VMEM((3, wide, 128), F3...  4.7 us
    ppermute x2, waiting for transfers between devices, to_previous(): lax.ppermute(x, 'tile', [(i + 1, i) for i in range(lax.axis_size('tile')...  4.36 us
  transfers between devices with their start and end apart: 31, of which 9 were waited for; matrix products, arithmetic and copies ran while one was open for 1% of the time, Pallas kernels for 27%

profile of v1, /device:TPU:1, one launch (start us, length us, event | category | flops | bytes accessed | tf_op | source)
XLA Modules:
  0.0 118.2 jit_solution(249243616795523310)
XLA Ops:
  0.0 1.1 shard_map.100.refs_0_.m0.refs_4_
  1.1 2.1 %collective-permute-start = (bf16[128,480]{1,0:T(8,128)(2,1)S(1)}, bf16[128,480]{1,0:T(8,128)(2,1)S(1)}, u32[]{:S(2)}, u32[]{:S(2)}) collective-permute-start(bf16[128,480]{1,0:T(8,128)(2,1)S(1)} %shard_map.100.refs_0_.m0.refs_4_), channel_id=1, source_target_pairs={{0,8},{8,0},{16,24},{24,16},{1,9},{9,1},{17,25},{25,17},{2,10},{10... | collective-permute-start | bytes 368648 | tf_op jit(solution)/shard_map/ppermute | solution.py:34
  3.2 1.2 %collective-permute-start.1 = (bf16[128,480]{1,0:T(8,128)(2,1)S(1)}, bf16[128,480]{1,0:T(8,128)(2,1)S(1)}, u32[]{:S(2)}, u32[]{:S(2)}) collective-permute-start(bf16[128,480]{1,0:T(8,128)(2,1)S(1)} %shard_map.100.refs_0_.m0.refs_4_), channel_id=1, source_target_pairs={{0,16},{8,24},{16,0},{24,8},{1,17},{9,25},{17,1},{25,9},{2,18},{10... | collective-permute-start | bytes 368648 | tf_op jit(solution)/shard_map/ppermute | solution.py:34
  4.5 1.9 %collective-permute-done.refs_1_.m1.refs_5_ = bf16[128,480]{1,0:T(8,128)(2,1)S(1)} collective-permute-done((bf16[128,480]{1,0:T(8,128)(2,1)S(1)}, bf16[128,480]{1,0:T(8,128)(2,1)S(1)}, u32[]{:S(2)}, u32[]{:S(2)}) %collective-permute-start) | collective-permute-done | bytes 122912 | tf_op jit(solution)/shard_map/ppermute | solution.py:34
  7.3 2.7 %collective-permute-done.2.refs_3_.m3.refs_7_ = bf16[128,480]{1,0:T(8,128)(2,1)S(1)} collective-permute-done((bf16[128,480]{1,0:T(8,128)(2,1)S(1)}, bf16[128,480]{1,0:T(8,128)(2,1)S(1)}, u32[]{:S(2)}, u32[]{:S(2)}) %collective-permute-start.2) | collective-permute-done | bytes 122912 | tf_op jit(solution)/shard_map/ppermute | solution.py:34
  10.0 3.3 %collective-permute-start.5 = (bf16[4,16,480]{2,1,0:T(8,128)(2,1)S(1)}, bf16[4,16,480]{2,1,0:T(8,128)(2,1)S(1)}, u32[]{:S(2)}, u32[]{:S(2)}) collective-permute-start(bf16[4,16,480]{2,1,0:T(8,128)(2,1)S(1)} %shard_map.101), channel_id=1, source_target_pairs={{0,6},{1,7},{2,4},{3,5},{4,2},{5,3},{6,0},{7,1},{8,14},{9,15},{10,... | collective-permute-start | bytes 184328 | tf_op jit(solution)/shard_map/ppermute | solution.py:34
  13.7 1.5 %shard_map.102 = (bf16[3,160,384]{2,1,0:T(8,128)(2,1)S(1)}, bf16[3,160,384]{2,1,0:T(8,128)(2,1)S(1)}, bf16[4,16,320]{2,1,0:T(8,128)(2,1)S(1)}, bf16[192,384]{1,0:T(8,128)(2,1)S(1)}, bf16[192,384]{1,0:T(8,128)(2,1)S(1)}) custom-call(bf16[2,4,160,96]{3,2,1,0:T(8,128)(2,1)} %bitcast.18, bf16[2,4,160,96]{3,2,1,0:T(8,128)(2,1)} %bitcast.19, ...), custom_call_target="tpu_custom_call" | custom-call | bytes 1048576 | tf_op jit(solution)/shard_map/pallas_call | solution.py:472
  15.3 5.4 %collective-permute-start.7 = (bf16[192,384]{1,0:T(8,128)(2,1)S(1)}, bf16[192,384]{1,0:T(8,128)(2,1)S(1)}, u32[]{:S(2)}, u32[]{:S(2)}) collective-permute-start(bf16[192,384]{1,0:T(8,128)(2,1)S(1)} %get-tuple-element.22), channel_id=1, source_target_pairs={{0,1},{1,2},{2,3},{3,4},{4,5},{5,6},{6,7},{8,9},{9,10},{10,11},{11... | collective-permute-start | bytes 442376 | tf_op jit(solution)/shard_map/ppermute | solution.py:58
  20.7 1.9 %collective-permute-start.8 = (bf16[192,384]{1,0:T(8,128)(2,1)S(1)}, bf16[192,384]{1,0:T(8,128)(2,1)S(1)}, u32[]{:S(2)}, u32[]{:S(2)}) collective-permute-start(bf16[192,384]{1,0:T(8,128)(2,1)S(1)} %get-tuple-element.24), channel_id=1, source_target_pairs={{1,0},{2,1},{3,2},{4,3},{5,4},{6,5},{7,6},{9,8},{10,9},{11,10},{12... | collective-permute-start | bytes 442376 | tf_op jit(solution)/shard_map/ppermute | solution.py:62
  22.8 4.4 %collective-permute-done.8.after = bf16[192,384]{1,0:T(8,128)(2,1)S(1)} collective-permute-done((bf16[192,384]{1,0:T(8,128)(2,1)S(1)}, bf16[192,384]{1,0:T(8,128)(2,1)S(1)}, u32[]{:S(2)}, u32[]{:S(2)}) %collective-permute-start.8) | collective-permute-done | bytes 147488 | tf_op jit(solution)/shard_map/ppermute | solution.py:62
  27.8 0.9 collective-permute-start.13
  29.3 1.2 collective-permute-start.15
  30.5 4.2 %shard_map.103 = (bf16[3,6,160,384]{3,2,1,0:T(8,128)(2,1)S(1)}, f32[2,384]{1,0:T(2,128)S(1)}) custom-call(s32[32]{0:T(128)S(1)} %copy-done.2, bf16[16,16,480]{2,1,0:T(8,128)(2,1)S(1)} %pad_maximum_fusion.2.near_ref, bf16[16,16,480]{2,1,0:T(8,128)(2,1)S(1)} %collective-permute-done.6.far_ref, bf16[192,384]{1,0:T(8,128)(2,1)S(1)} %collective-permute-done.7.before, ...), custom_call_target="tpu_custom_call" | custom-call | flops 318504960 | bytes 1048576 | tf_op jit(solution)/shard_map/pallas_call | solution.py:514
  34.8 2.3 %shard_map.105 = (bf16[9,384,256]{2,1,0:T(8,128)(2,1)S(1)}, bf16[9,384,256]{2,1,0:T(8,128)(2,1)S(1)}) custom-call(bf16[3,3,3,96,384]{4,3,2,1,0:T(8,128)(2,1)S(1)} %copy-done), custom_call_target="tpu_custom_call" | custom-call | bytes 1048576 | tf_op jit(solution)/shard_map/pallas_call | solution.py:493
  37.1 2.4 %shard_map.108 = (bf16[9,384,256]{2,1,0:T(8,128)(2,1)S(1)}, bf16[9,384,256]{2,1,0:T(8,128)(2,1)S(1)}) custom-call(bf16[3,3,3,96,384]{4,3,2,1,0:T(8,128)(2,1)S(1)} %copy-done.1), custom_call_target="tpu_custom_call" | custom-call | bytes 1048576 | tf_op jit(solution)/shard_map/pallas_call | solution.py:493
  39.5 0.9 collective-permute-start.26
  40.5 1.3 %collective-permute-start.10 = (f32[2,2,384]{2,1,0:T(2,128)S(1)}, f32[2,2,384]{2,1,0:T(2,128)S(1)}, u32[]{:S(2)}, u32[]{:S(2)}) collective-permute-start(f32[2,2,384]{2,1,0:T(2,128)S(1)} %pad_maximum_fusion.4.refs_0_), channel_id=1, source_target_pairs={{0,2},{1,3},{2,0},{3,1},{4,6},{5,7},{6,4},{7,5},{8,10},{9,11},{10,... | collective-permute-start | bytes 18440 | tf_op jit(solution)/shard_map/ppermute | solution.py:34
  41.7 2.2 %collective-permute-start.11 = (f32[2,2,384]{2,1,0:T(2,128)S(1)}, f32[2,2,384]{2,1,0:T(2,128)S(1)}, u32[]{:S(2)}, u32[]{:S(2)}) collective-permute-start(f32[2,2,384]{2,1,0:T(2,128)S(1)} %pad_maximum_fusion.4.refs_0_), channel_id=1, source_target_pairs={{0,4},{1,5},{2,6},{3,7},{4,0},{5,1},{6,2},{7,3},{8,12},{9,13},{10,... | collective-permute-start | bytes 18440 | tf_op jit(solution)/shard_map/ppermute | solution.py:34
  44.7 3.3 %shard_map.106.refs_9_ = f32[2,640,128]{2,1,0:T(8,128)S(1)} custom-call(bf16[3,160,384]{2,1,0:T(8,128)(2,1)S(1)} %get-tuple-element.29.p0, bf16[3,160,384]{2,1,0:T(8,128)(2,1)S(1)} %collective-permute-done.13.p1, bf16[3,160,384]{2,1,0:T(8,128)(2,1)S(1)} %collective-permute-done.14.p2, bf16[3,160,384]{2,1,0:T(8,128)(2,1)S(1)} %collective-permute-done.15.p3, ...), custom_call_target="tpu_custom_call" | custom-call | flops 1274019840 | bytes 1048576 | tf_op jit(solution)/shard_map/pallas_call | solution.py:503
  48.8 6.5 %shard_map.107 = (bf16[3,160,384]{2,1,0:T(8,128)(2,1)S(1)}, f32[2,128]{1,0:T(2,128)S(1)}) custom-call(f32[2,2,384]{2,1,0:T(2,128)S(1)} %pad_maximum_fusion.4.refs_0_, f32[2,2,384]{2,1,0:T(2,128)S(1)} %collective-permute-done.10.refs_1_, f32[2,2,384]{2,1,0:T(2,128)S(1)} %collective-permute-done.11.refs_2_, f32[2,2,384]{2,1,0:T(2,128)S(1)} %collective-permute-done.12.refs_3_, ...), custom_call_target="tpu_custom_call" | custom-call | flops 2548039680 | bytes 1048576 | tf_op jit(solution)/shard_map/pallas_call | solution.py:535
  55.4 1.8 %collective-permute-start.18 = (f32[2,128]{1,0:T(2,128)S(1)}, f32[2,128]{1,0:T(2,128)S(1)}, u32[]{:S(2)}, u32[]{:S(2)}) collective-permute-start(f32[2,128]{1,0:T(2,128)S(1)} %get-tuple-element.32), channel_id=1, source_target_pairs={{0,24},{8,16},{16,8},{24,0},{1,25},{9,17},{17,9},{25,1},{2,26},{10... | collective-permute-start | bytes 3080 | tf_op jit(solution)/shard_map/ppermute | solution.py:34
  58.1 1.8 %collective-permute-start.25 = (bf16[3,160,384]{2,1,0:T(8,128)(2,1)S(1)}, bf16[3,160,384]{2,1,0:T(8,128)(2,1)S(1)}, u32[]{:S(2)}, u32[]{:S(2)}) collective-permute-start(bf16[3,160,384]{2,1,0:T(8,128)(2,1)S(1)} %get-tuple-element.33.refs_8_), channel_id=1, source_target_pairs={{0,24},{8,16},{16,8},{24,0},{1,25},{9,17},{17,9},{25,1},{2,26},{10... | collective-permute-start | bytes 1105928 | tf_op jit(solution)/shard_map/ppermute | solution.py:34
  60.3 1.2 %collective-permute-start.28 = (bf16[3,160,384]{2,1,0:T(8,128)(2,1)S(1)}, bf16[3,160,384]{2,1,0:T(8,128)(2,1)S(1)}, u32[]{:S(2)}, u32[]{:S(2)}) collective-permute-start(bf16[3,160,384]{2,1,0:T(8,128)(2,1)S(1)} %get-tuple-element.34.p0), channel_id=1, source_target_pairs={{0,24},{8,16},{16,8},{24,0},{1,25},{9,17},{17,9},{25,1},{2,26},{10... | collective-permute-start | bytes 1105928 | tf_op jit(solution)/shard_map/ppermute | solution.py:34
  62.1 4.8 %collective-permute-done.25.refs_11_ = bf16[3,160,384]{2,1,0:T(8,128)(2,1)S(1)} collective-permute-done((bf16[3,160,384]{2,1,0:T(8,128)(2,1)S(1)}, bf16[3,160,384]{2,1,0:T(8,128)(2,1)S(1)}, u32[]{:S(2)}, u32[]{:S(2)}) %collective-permute-start.25) | collective-permute-done | bytes 368672 | tf_op jit(solution)/shard_map/ppermute | solution.py:34
  67.5 25.7 %collective-permute-done.24.refs_10_ = bf16[3,160,384]{2,1,0:T(8,128)(2,1)S(1)} collective-permute-done((bf16[3,160,384]{2,1,0:T(8,128)(2,1)S(1)}, bf16[3,160,384]{2,1,0:T(8,128)(2,1)S(1)}, u32[]{:S(2)}, u32[]{:S(2)}) %collective-permute-start.24) | collective-permute-done | bytes 368672 | tf_op jit(solution)/shard_map/ppermute | solution.py:34
  94.2 4.6 %collective-permute-start.29 = (bf16[3,160,384]{2,1,0:T(8,128)(2,1)S(1)}, bf16[3,160,384]{2,1,0:T(8,128)(2,1)S(1)}, u32[]{:S(2)}, u32[]{:S(2)}) collective-permute-start(bf16[3,160,384]{2,1,0:T(8,128)(2,1)S(1)} %pad_maximum_fusion), channel_id=1, source_target_pairs={{0,1},{1,2},{2,3},{3,4},{4,5},{5,6},{6,7},{8,9},{9,10},{10,11},{11... | collective-permute-start | bytes 1105928 | tf_op jit(solution)/shard_map/ppermute | solution.py:58
  99.1 2.1 %collective-permute-start.30 = (bf16[3,160,384]{2,1,0:T(8,128)(2,1)S(1)}, bf16[3,160,384]{2,1,0:T(8,128)(2,1)S(1)}, u32[]{:S(2)}, u32[]{:S(2)}) collective-permute-start(bf16[3,160,384]{2,1,0:T(8,128)(2,1)S(1)} %pad_maximum_fusion.1), channel_id=1, source_target_pairs={{1,0},{2,1},{3,2},{4,3},{5,4},{6,5},{7,6},{9,8},{10,9},{11,10},{12... | collective-permute-start | bytes 1105928 | tf_op jit(solution)/shard_map/ppermute | solution.py:62
  101.2 1.3 %collective-permute-start.20 = (f32[2,4,2,128]{3,2,1,0:T(2,128)S(1)}, f32[2,4,2,128]{3,2,1,0:T(2,128)S(1)}, u32[]{:S(2)}, u32[]{:S(2)}) collective-permute-start(f32[2,4,2,128]{3,2,1,0:T(2,128)S(1)} %pad_maximum_fusion.3.refs_0_), channel_id=1, source_target_pairs={{0,2},{1,3},{2,0},{3,1},{4,6},{5,7},{6,4},{7,5},{8,10},{9,11},{10,... | collective-permute-start | bytes 24584 | tf_op jit(solution)/shard_map/ppermute | solution.py:34
  103.0 1.9 %collective-permute-start.22 = (f32[2,4,2,128]{3,2,1,0:T(2,128)S(1)}, f32[2,4,2,128]{3,2,1,0:T(2,128)S(1)}, u32[]{:S(2)}, u32[]{:S(2)}) collective-permute-start(f32[2,4,2,128]{3,2,1,0:T(2,128)S(1)} %pad_maximum_fusion.3.refs_0_), channel_id=1, source_target_pairs={{0,6},{1,7},{2,4},{3,5},{4,2},{5,3},{6,0},{7,1},{8,14},{9,15},{10,... | collective-permute-start | bytes 24584 | tf_op jit(solution)/shard_map/ppermute | solution.py:34
  104.8 3.3 %shard_map.109.refs_12_ = f32[2,640,128]{2,1,0:T(8,128)S(1)} custom-call(bf16[3,160,384]{2,1,0:T(8,128)(2,1)S(1)} %get-tuple-element.34.p0, bf16[3,160,384]{2,1,0:T(8,128)(2,1)S(1)} %collective-permute-done.26.p1, bf16[3,160,384]{2,1,0:T(8,128)(2,1)S(1)} %collective-permute-done.27.p2, bf16[3,160,384]{2,1,0:T(8,128)(2,1)S(1)} %collective-permute-done.28.p3, ...), custom_call_target="tpu_custom_call" | custom-call | flops 1274019840 | bytes 1048576 | tf_op jit(solution)/shard_map/pallas_call | solution.py:503
  108.2 7.7 %shard_map.110 = (f32[3,640,128]{2,1,0:T(8,128)S(1)}, f32[2,384]{1,0:T(2,128)S(1)}) custom-call(f32[2,4,2,128]{3,2,1,0:T(2,128)S(1)} %pad_maximum_fusion.3.refs_0_, f32[2,4,2,128]{3,2,1,0:T(2,128)S(1)} %collective-permute-done.20.refs_1_, f32[2,4,2,128]{3,2,1,0:T(2,128)S(1)} %collective-permute-done.21.refs_2_, ...), custom_call_target="tpu_custom_call" | custom-call | flops 2548039680 | bytes 1048576 | tf_op jit(solution)/shard_map/pallas_call | solution.py:549
  116.0 2.1 %shard_map.111 = bf16[3,4,160,96]{3,2,1,0:T(8,128)(2,1)} custom-call(f32[3,640,128]{2,1,0:T(8,128)S(1)} %get-tuple-element.37.part_ref, f32[2,384]{1,0:T(2,128)S(1)} %get-tuple-element.38.scale_ref, bf16[3,160,384]{2,1,0:T(8,128)(2,1)S(1)} %collective-permute-done.29.up, bf16[3,160,384]{2,1,0:T(8,128)(2,1)S(1)} %collective-permute-done.30.down, ...), custom_call_target="tpu_custom_call" | custom-call | flops 637009920 | bytes 1048576 | tf_op jit(solution)/shard_map/pallas_call | solution.py:556
  (59 shorter events, 8.3 us)
Async XLA Ops:
  0.0 30.5 %copy-start.2 = (s32[32]{0:T(128)S(1)}, s32[32]{0:T(128)}, u32[]{:S(2)}) copy-start(s32[32]{0:T(128)} %map_ref.1) | copy-start | bytes 388
  1.1 5.3 %collective-permute-start = (bf16[128,480]{1,0:T(8,128)(2,1)S(1)}, bf16[128,480]{1,0:T(8,128)(2,1)S(1)}, u32[]{:S(2)}, u32[]{:S(2)}) collective-permute-start(bf16[128,480]{1,0:T(8,128)(2,1)S(1)} %shard_map.100.refs_0_.m0.refs_4_), channel_id=1, source_target_pairs={{0,8},{8,0},{16,24},{24,16},{1,9},{9,1},{17,25},{25,17},{2,10},{10... | collective-permute-start | bytes 368648 | tf_op jit(solution)/shard_map/ppermute | solution.py:34
  3.2 4.1 %collective-permute-start.1 = (bf16[128,480]{1,0:T(8,128)(2,1)S(1)}, bf16[128,480]{1,0:T(8,128)(2,1)S(1)}, u32[]{:S(2)}, u32[]{:S(2)}) collective-permute-start(bf16[128,480]{1,0:T(8,128)(2,1)S(1)} %shard_map.100.refs_0_.m0.refs_4_), channel_id=1, source_target_pairs={{0,16},{8,24},{16,0},{24,8},{1,17},{9,25},{17,1},{25,9},{2,18},{10... | collective-permute-start | bytes 368648 | tf_op jit(solution)/shard_map/ppermute | solution.py:34
  4.4 5.6 %collective-permute-start.2 = (bf16[128,480]{1,0:T(8,128)(2,1)S(1)}, bf16[128,480]{1,0:T(8,128)(2,1)S(1)}, u32[]{:S(2)}, u32[]{:S(2)}) collective-permute-start(bf16[128,480]{1,0:T(8,128)(2,1)S(1)} %shard_map.100.refs_0_.m0.refs_4_), channel_id=1, source_target_pairs={{0,24},{8,16},{16,8},{24,0},{1,25},{9,17},{17,9},{25,1},{2,26},{10... | collective-permute-start | bytes 368648 | tf_op jit(solution)/shard_map/ppermute | solution.py:34
  10.0 12.6 %collective-permute-start.5 = (bf16[4,16,480]{2,1,0:T(8,128)(2,1)S(1)}, bf16[4,16,480]{2,1,0:T(8,128)(2,1)S(1)}, u32[]{:S(2)}, u32[]{:S(2)}) collective-permute-start(bf16[4,16,480]{2,1,0:T(8,128)(2,1)S(1)} %shard_map.101), channel_id=1, source_target_pairs={{0,6},{1,7},{2,4},{3,5},{4,2},{5,3},{6,0},{7,1},{8,14},{9,15},{10,... | collective-permute-start | bytes 184328 | tf_op jit(solution)/shard_map/ppermute | solution.py:34
  13.4 9.3 %collective-permute-start.4 = (bf16[4,16,480]{2,1,0:T(8,128)(2,1)S(1)}, bf16[4,16,480]{2,1,0:T(8,128)(2,1)S(1)}, u32[]{:S(2)}, u32[]{:S(2)}) collective-permute-start(bf16[4,16,480]{2,1,0:T(8,128)(2,1)S(1)} %shard_map.101), channel_id=1, source_target_pairs={{0,4},{1,5},{2,6},{3,7},{4,0},{5,1},{6,2},{7,3},{8,12},{9,13},{10,... | collective-permute-start | bytes 184328 | tf_op jit(solution)/shard_map/ppermute | solution.py:34
  13.4 9.3 %collective-permute-start.3 = (bf16[4,16,480]{2,1,0:T(8,128)(2,1)S(1)}, bf16[4,16,480]{2,1,0:T(8,128)(2,1)S(1)}, u32[]{:S(2)}, u32[]{:S(2)}) collective-permute-start(bf16[4,16,480]{2,1,0:T(8,128)(2,1)S(1)} %shard_map.101), channel_id=1, source_target_pairs={{0,2},{1,3},{2,0},{3,1},{4,6},{5,7},{6,4},{7,5},{8,10},{9,11},{10,... | collective-permute-start | bytes 184328 | tf_op jit(solution)/shard_map/ppermute | solution.py:34
  15.3 7.5 %collective-permute-start.7 = (bf16[192,384]{1,0:T(8,128)(2,1)S(1)}, bf16[192,384]{1,0:T(8,128)(2,1)S(1)}, u32[]{:S(2)}, u32[]{:S(2)}) collective-permute-start(bf16[192,384]{1,0:T(8,128)(2,1)S(1)} %get-tuple-element.22), channel_id=1, source_target_pairs={{0,1},{1,2},{2,3},{3,4},{4,5},{5,6},{6,7},{8,9},{9,10},{10,11},{11... | collective-permute-start | bytes 442376 | tf_op jit(solution)/shard_map/ppermute | solution.py:58
  20.7 6.5 %collective-permute-start.8 = (bf16[192,384]{1,0:T(8,128)(2,1)S(1)}, bf16[192,384]{1,0:T(8,128)(2,1)S(1)}, u32[]{:S(2)}, u32[]{:S(2)}) collective-permute-start(bf16[192,384]{1,0:T(8,128)(2,1)S(1)} %get-tuple-element.24), channel_id=1, source_target_pairs={{1,0},{2,1},{3,2},{4,3},{5,4},{6,5},{7,6},{9,8},{10,9},{11,10},{12... | collective-permute-start | bytes 442376 | tf_op jit(solution)/shard_map/ppermute | solution.py:62
  22.7 7.8 %collective-permute-start.6 = (bf16[16,16,480]{2,1,0:T(8,128)(2,1)S(1)}, bf16[16,16,480]{2,1,0:T(8,128)(2,1)S(1)}, u32[]{:S(2)}, u32[]{:S(2)}) collective-permute-start(bf16[16,16,480]{2,1,0:T(8,128)(2,1)S(1)} %pad_maximum_fusion.2.near_ref), channel_id=1, source_target_pairs={{0,1},{1,0},{2,3},{3,2},{4,5},{5,4},{6,7},{7,6},{8,9},{9,8},{10,11... | collective-permute-start | bytes 737288 | tf_op jit(solution)/shard_map/ppermute | solution.py:34
  27.8 14.0 %collective-permute-start.13 = (bf16[3,160,384]{2,1,0:T(8,128)(2,1)S(1)}, bf16[3,160,384]{2,1,0:T(8,128)(2,1)S(1)}, u32[]{:S(2)}, u32[]{:S(2)}) collective-permute-start(bf16[3,160,384]{2,1,0:T(8,128)(2,1)S(1)} %get-tuple-element.29.p0), channel_id=1, source_target_pairs={{0,8},{8,0},{16,24},{24,16},{1,9},{9,1},{17,25},{25,17},{2,10},{10... | collective-permute-start | bytes 1105928 | tf_op jit(solution)/shard_map/ppermute | solution.py:34
  28.7 15.8 %collective-permute-start.14 = (bf16[3,160,384]{2,1,0:T(8,128)(2,1)S(1)}, bf16[3,160,384]{2,1,0:T(8,128)(2,1)S(1)}, u32[]{:S(2)}, u32[]{:S(2)}) collective-permute-start(bf16[3,160,384]{2,1,0:T(8,128)(2,1)S(1)} %get-tuple-element.29.p0), channel_id=1, source_target_pairs={{0,16},{8,24},{16,0},{24,8},{1,17},{9,25},{17,1},{25,9},{2,18},{10... | collective-permute-start | bytes 1105928 | tf_op jit(solution)/shard_map/ppermute | solution.py:34
  29.3 15.4 %collective-permute-start.15 = (bf16[3,160,384]{2,1,0:T(8,128)(2,1)S(1)}, bf16[3,160,384]{2,1,0:T(8,128)(2,1)S(1)}, u32[]{:S(2)}, u32[]{:S(2)}) collective-permute-start(bf16[3,160,384]{2,1,0:T(8,128)(2,1)S(1)} %get-tuple-element.29.p0), channel_id=1, source_target_pairs={{0,24},{8,16},{16,8},{24,0},{1,25},{9,17},{17,9},{25,1},{2,26},{10... | collective-permute-start | bytes 1105928 | tf_op jit(solution)/shard_map/ppermute | solution.py:34
  34.7 5.8 %collective-permute-start.9 = (f32[2,384]{1,0:T(2,128)S(1)}, f32[2,384]{1,0:T(2,128)S(1)}, u32[]{:S(2)}, u32[]{:S(2)}) collective-permute-start(f32[2,384]{1,0:T(2,128)S(1)} %get-tuple-element.25), channel_id=1, source_target_pairs={{0,1},{1,0},{2,3},{3,2},{4,5},{5,4},{6,7},{7,6},{8,9},{9,8},{10,11... | collective-permute-start | bytes 9224 | tf_op jit(solution)/shard_map/ppermute | solution.py:34
  39.5 61.7 %collective-permute-start.26 = (bf16[3,160,384]{2,1,0:T(8,128)(2,1)S(1)}, bf16[3,160,384]{2,1,0:T(8,128)(2,1)S(1)}, u32[]{:S(2)}, u32[]{:S(2)}) collective-permute-start(bf16[3,160,384]{2,1,0:T(8,128)(2,1)S(1)} %get-tuple-element.34.p0), channel_id=1, source_target_pairs={{0,8},{8,0},{16,24},{24,16},{1,9},{9,1},{17,25},{25,17},{2,10},{10... | collective-permute-start | bytes 1105928 | tf_op jit(solution)/shard_map/ppermute | solution.py:34
  40.5 7.6 %collective-permute-start.10 = (f32[2,2,384]{2,1,0:T(2,128)S(1)}, f32[2,2,384]{2,1,0:T(2,128)S(1)}, u32[]{:S(2)}, u32[]{:S(2)}) collective-permute-start(f32[2,2,384]{2,1,0:T(2,128)S(1)} %pad_maximum_fusion.4.refs_0_), channel_id=1, source_target_pairs={{0,2},{1,3},{2,0},{3,1},{4,6},{5,7},{6,4},{7,5},{8,10},{9,11},{10,... | collective-permute-start | bytes 18440 | tf_op jit(solution)/shard_map/ppermute | solution.py:34
  41.7 6.3 %collective-permute-start.11 = (f32[2,2,384]{2,1,0:T(2,128)S(1)}, f32[2,2,384]{2,1,0:T(2,128)S(1)}, u32[]{:S(2)}, u32[]{:S(2)}) collective-permute-start(f32[2,2,384]{2,1,0:T(2,128)S(1)} %pad_maximum_fusion.4.refs_0_), channel_id=1, source_target_pairs={{0,4},{1,5},{2,6},{3,7},{4,0},{5,1},{6,2},{7,3},{8,12},{9,13},{10,... | collective-permute-start | bytes 18440 | tf_op jit(solution)/shard_map/ppermute | solution.py:34
  44.5 4.3 %collective-permute-start.12 = (f32[2,2,384]{2,1,0:T(2,128)S(1)}, f32[2,2,384]{2,1,0:T(2,128)S(1)}, u32[]{:S(2)}, u32[]{:S(2)}) collective-permute-start(f32[2,2,384]{2,1,0:T(2,128)S(1)} %pad_maximum_fusion.4.refs_0_), channel_id=1, source_target_pairs={{0,6},{1,7},{2,4},{3,5},{4,2},{5,3},{6,0},{7,1},{8,14},{9,15},{10,... | collective-permute-start | bytes 18440 | tf_op jit(solution)/shard_map/ppermute | solution.py:34
  55.4 4.6 %collective-permute-start.18 = (f32[2,128]{1,0:T(2,128)S(1)}, f32[2,128]{1,0:T(2,128)S(1)}, u32[]{:S(2)}, u32[]{:S(2)}) collective-permute-start(f32[2,128]{1,0:T(2,128)S(1)} %get-tuple-element.32), channel_id=1, source_target_pairs={{0,24},{8,16},{16,8},{24,0},{1,25},{9,17},{17,9},{25,1},{2,26},{10... | collective-permute-start | bytes 3080 | tf_op jit(solution)/shard_map/ppermute | solution.py:34
  57.2 3.1 %collective-permute-start.17 = (f32[2,128]{1,0:T(2,128)S(1)}, f32[2,128]{1,0:T(2,128)S(1)}, u32[]{:S(2)}, u32[]{:S(2)}) collective-permute-start(f32[2,128]{1,0:T(2,128)S(1)} %get-tuple-element.32), channel_id=1, source_target_pairs={{0,16},{8,24},{16,0},{24,8},{1,17},{9,25},{17,1},{25,9},{2,18},{10... | collective-permute-start | bytes 3080 | tf_op jit(solution)/shard_map/ppermute | solution.py:34
  57.4 4.0 %collective-permute-start.16 = (f32[2,128]{1,0:T(2,128)S(1)}, f32[2,128]{1,0:T(2,128)S(1)}, u32[]{:S(2)}, u32[]{:S(2)}) collective-permute-start(f32[2,128]{1,0:T(2,128)S(1)} %get-tuple-element.32), channel_id=1, source_target_pairs={{0,8},{8,0},{16,24},{24,16},{1,9},{9,1},{17,25},{25,17},{2,10},{10... | collective-permute-start | bytes 3080 | tf_op jit(solution)/shard_map/ppermute | solution.py:34
  58.1 8.8 %collective-permute-start.25 = (bf16[3,160,384]{2,1,0:T(8,128)(2,1)S(1)}, bf16[3,160,384]{2,1,0:T(8,128)(2,1)S(1)}, u32[]{:S(2)}, u32[]{:S(2)}) collective-permute-start(bf16[3,160,384]{2,1,0:T(8,128)(2,1)S(1)} %get-tuple-element.33.refs_8_), channel_id=1, source_target_pairs={{0,24},{8,16},{16,8},{24,0},{1,25},{9,17},{17,9},{25,1},{2,26},{10... | collective-permute-start | bytes 1105928 | tf_op jit(solution)/shard_map/ppermute | solution.py:34
  60.0 42.6 %collective-permute-start.27 = (bf16[3,160,384]{2,1,0:T(8,128)(2,1)S(1)}, bf16[3,160,384]{2,1,0:T(8,128)(2,1)S(1)}, u32[]{:S(2)}, u32[]{:S(2)}) collective-permute-start(bf16[3,160,384]{2,1,0:T(8,128)(2,1)S(1)} %get-tuple-element.34.p0), channel_id=1, source_target_pairs={{0,16},{8,24},{16,0},{24,8},{1,17},{9,25},{17,1},{25,9},{2,18},{10... | collective-permute-start | bytes 1105928 | tf_op jit(solution)/shard_map/ppermute | solution.py:34
  60.3 42.7 %collective-permute-start.28 = (bf16[3,160,384]{2,1,0:T(8,128)(2,1)S(1)}, bf16[3,160,384]{2,1,0:T(8,128)(2,1)S(1)}, u32[]{:S(2)}, u32[]{:S(2)}) collective-permute-start(bf16[3,160,384]{2,1,0:T(8,128)(2,1)S(1)} %get-tuple-element.34.p0), channel_id=1, source_target_pairs={{0,24},{8,16},{16,8},{24,0},{1,25},{9,17},{17,9},{25,1},{2,26},{10... | collective-permute-start | bytes 1105928 | tf_op jit(solution)/shard_map/ppermute | solution.py:34
  61.5 31.7 %collective-permute-start.24 = (bf16[3,160,384]{2,1,0:T(8,128)(2,1)S(1)}, bf16[3,160,384]{2,1,0:T(8,128)(2,1)S(1)}, u32[]{:S(2)}, u32[]{:S(2)}) collective-permute-start(bf16[3,160,384]{2,1,0:T(8,128)(2,1)S(1)} %get-tuple-element.33.refs_8_), channel_id=1, source_target_pairs={{0,16},{8,24},{16,0},{24,8},{1,17},{9,25},{17,1},{25,9},{2,18},{10... | collective-permute-start | bytes 1105928 | tf_op jit(solution)/shard_map/ppermute | solution.py:34
  66.9 26.9 %collective-permute-start.23 = (bf16[3,160,384]{2,1,0:T(8,128)(2,1)S(1)}, bf16[3,160,384]{2,1,0:T(8,128)(2,1)S(1)}, u32[]{:S(2)}, u32[]{:S(2)}) collective-permute-start(bf16[3,160,384]{2,1,0:T(8,128)(2,1)S(1)} %get-tuple-element.33.refs_8_), channel_id=1, source_target_pairs={{0,8},{8,0},{16,24},{24,16},{1,9},{9,1},{17,25},{25,17},{2,10},{10... | collective-permute-start | bytes 1105928 | tf_op jit(solution)/shard_map/ppermute | solution.py:34
  93.2 5.8 %collective-permute-start.19 = (f32[4,2,128]{2,1,0:T(2,128)S(1)}, f32[4,2,128]{2,1,0:T(2,128)S(1)}, u32[]{:S(2)}, u32[]{:S(2)}) collective-permute-start(f32[4,2,128]{2,1,0:T(2,128)S(1)} %pad_maximum_fusion.5), channel_id=1, source_target_pairs={{0,1},{1,0},{2,3},{3,2},{4,5},{5,4},{6,7},{7,6},{8,9},{9,8},{10,11... | collective-permute-start | bytes 12296 | tf_op jit(solution)/shard_map/ppermute | solution.py:34
  94.2 21.8 %collective-permute-start.29 = (bf16[3,160,384]{2,1,0:T(8,128)(2,1)S(1)}, bf16[3,160,384]{2,1,0:T(8,128)(2,1)S(1)}, u32[]{:S(2)}, u32[]{:S(2)}) collective-permute-start(bf16[3,160,384]{2,1,0:T(8,128)(2,1)S(1)} %pad_maximum_fusion), channel_id=1, source_target_pairs={{0,1},{1,2},{2,3},{3,4},{4,5},{5,6},{6,7},{8,9},{9,10},{10,11},{11... | collective-permute-start | bytes 1105928 | tf_op jit(solution)/shard_map/ppermute | solution.py:58
  99.1 16.9 %collective-permute-start.30 = (bf16[3,160,384]{2,1,0:T(8,128)(2,1)S(1)}, bf16[3,160,384]{2,1,0:T(8,128)(2,1)S(1)}, u32[]{:S(2)}, u32[]{:S(2)}) collective-permute-start(bf16[3,160,384]{2,1,0:T(8,128)(2,1)S(1)} %pad_maximum_fusion.1), channel_id=1, source_target_pairs={{1,0},{2,1},{3,2},{4,3},{5,4},{6,5},{7,6},{9,8},{10,9},{11,10},{12... | collective-permute-start | bytes 1105928 | tf_op jit(solution)/shard_map/ppermute | solution.py:62
  101.2 7.0 %collective-permute-start.20 = (f32[2,4,2,128]{3,2,1,0:T(2,128)S(1)}, f32[2,4,2,128]{3,2,1,0:T(2,128)S(1)}, u32[]{:S(2)}, u32[]{:S(2)}) collective-permute-start(f32[2,4,2,128]{3,2,1,0:T(2,128)S(1)} %pad_maximum_fusion.3.refs_0_), channel_id=1, source_target_pairs={{0,2},{1,3},{2,0},{3,1},{4,6},{5,7},{6,4},{7,5},{8,10},{9,11},{10,... | collective-permute-start | bytes 24584 | tf_op jit(solution)/shard_map/ppermute | solution.py:34
  102.5 5.7 %collective-permute-start.21 = (f32[2,4,2,128]{3,2,1,0:T(2,128)S(1)}, f32[2,4,2,128]{3,2,1,0:T(2,128)S(1)}, u32[]{:S(2)}, u32[]{:S(2)}) collective-permute-start(f32[2,4,2,128]{3,2,1,0:T(2,128)S(1)} %pad_maximum_fusion.3.refs_0_), channel_id=1, source_target_pairs={{0,4},{1,5},{2,6},{3,7},{4,0},{5,1},{6,2},{7,3},{8,12},{9,13},{10,... | collective-permute-start | bytes 24584 | tf_op jit(solution)/shard_map/ppermute | solution.py:34
  103.0 5.3 %collective-permute-start.22 = (f32[2,4,2,128]{3,2,1,0:T(2,128)S(1)}, f32[2,4,2,128]{3,2,1,0:T(2,128)S(1)}, u32[]{:S(2)}, u32[]{:S(2)}) collective-permute-start(f32[2,4,2,128]{3,2,1,0:T(2,128)S(1)} %pad_maximum_fusion.3.refs_0_), channel_id=1, source_target_pairs={{0,6},{1,7},{2,4},{3,5},{4,2},{5,3},{6,0},{7,1},{8,14},{9,15},{10,... | collective-permute-start | bytes 24584 | tf_op jit(solution)/shard_map/ppermute | solution.py:34
  (2 other events, 30.4 us)

commit v2 on v1

--- a/solution.py
+++ b/solution.py
@@ -156,11 +156,11 @@
     def tap(n, _):
         b, e = n // 3, n % 3
         for a in range(3):
-            turned[a, :, 0:outs] = w_ref[a, b, e].astype(F32).T
+            turned[a, :, 0:outs] = w_ref[a, b, e].T
         for slot in range(ins // outs):
-            start = pl.multiple_of(jnp.bitwise_xor(mine, slot) * outs, 8)
+            start = pl.multiple_of(jnp.bitwise_xor(mine, slot) * outs, 16)
             here = pl.ds(slot * outs, outs)
-            early, middle, late = [turned[a, pl.ds(start, outs), :].astype(BF16) for a in range(3)]
+            early, middle, late = [turned[a, pl.ds(start, outs), :] for a in range(3)]
             late_ref[n, here, 0:128] = late
             late_ref[n, here, 128:256] = middle
             early_ref[n, here, 0:128] = middle
@@ -192,7 +192,9 @@
     for n in range(wall.shape[0] // 16):
         at, lanes = 16 + n // GROUP * 16, slice(n % GROUP * wide // 4, (n % GROUP + 1) * wide // 4)
         parts = [m[at : at + 16, lanes].astype(F32) for m in (m0, m1, m2, m3)]
-        wall[16 * n : 16 * n + 16, :] = jnp.concatenate(parts, axis=1).astype(BF16)
+        a, b, e = n // 9, n // 3 % 3, n % 3
+        put = 16 * (9 * b + 3 * a + e)
+        wall[put : put + 16, :] = jnp.concatenate(parts, axis=1).astype(BF16)
     for row in range(rows):
         place = tab_ref[row]
         kept = (place >= 0).astype(F32)
@@ -203,17 +205,19 @@
         else:
             at = columns + 16 * (row if row < 2 else row - rows + 2)
             old = (before if row < 2 else after)[at : at + 16, 0 : 2 * columns].astype(F32)
-        for f in range(frames + 2):
-            v = old[:, f * columns : (f + 1) * columns] if f < 2 else new[:, (f - 2) * columns : (f - 1) * columns]
-            zero = jnp.zeros((16, 1), F32)
-            left = jnp.concatenate([zero, v[:, : columns - 1]], axis=1)
-            right = jnp.concatenate([v[:, 1:], zero], axis=1)
-            taps[row, f] = jnp.concatenate([left, v, right], axis=0).astype(BF16)
+        line = [old[:, f * columns : (f + 1) * columns] for f in range(2)]
+        line += [new[:, f * columns : (f + 1) * columns] for f in range(frames)]
+        v = jnp.concatenate(line, axis=0)
+        zero = jnp.zeros((v.shape[0], 1), F32)
+        left = jnp.concatenate([zero, v[:, : columns - 1]], axis=1)
+        right = jnp.concatenate([v[:, 1:], zero], axis=1)
+        parts = [x[16 * f : 16 * f + 16] for f in range(frames + 2) for x in (left, v, right)]
+        taps[row] = jnp.concatenate(parts, axis=0).astype(BF16).T
     total = jnp.zeros((8, wall.shape[1]), F32)
     for t in range(frames):
         for r in range(rows - 2):
-            patch = jnp.concatenate([taps[r + b, t + a] for a in range(3) for b in range(3)], axis=0)
-            got = lax.dot_general(patch, wall[...], (((0,), (0,)), ((), ())), preferred_element_type=F32).astype(BF16)
+            patch = jnp.concatenate([taps[r + b, :, 48 * t : 48 * t + 144] for b in range(3)], axis=1)
+            got = jnp.dot(patch, wall[...], preferred_element_type=F32).astype(BF16)
             first_ref[t, r] = got
             if 0 < r < rows - 3:
                 total += jnp.sum(got.astype(F32).reshape(columns // 8, 8, -1), axis=0)
@@ -263,15 +267,52 @@
     return (0.5 * y) * (1.0 + jnp.tanh(0.5 * y))
 
 
-def tap_product(taps, f, w_ref, lanes):
+def row_sum(got, columns, inner):
+    if not inner:
+        return got[0] + got[1] + got[2]
+    above, here, below = got
+    head = here[:columns] + below[:columns]
+    tail = here[-columns:] + above[-columns:]
+    return jnp.concatenate([head, here[columns:-columns] + above[:-columns] + below[columns:], tail], axis=0)
+
+
+def row_span(b, rows, inner):
+    return (max(1, b), min(rows - 1, b + rows - 2)) if inner else (b, b + rows - 2)
+
+
+def tap_product(taps, f, w_ref, lanes, inner=False):
     _, rows, columns, depth = taps.shape
-    summed = None
+    got = []
     for b in range(3):
-        x = taps[f, b : b + rows - 2].reshape((rows - 2) * columns, depth)
+        first, end = row_span(b, rows, inner)
+        x = taps[f, first:end].reshape((end - first) * columns, depth)
         w = w_ref[3 * b : 3 * b + 3, :, lanes].reshape(depth, lanes.stop - lanes.start)
-        got = jnp.dot(x, w, preferred_element_type=F32)
-        summed = got if summed is None else summed + got
-    return summed
+        got.append(jnp.dot(x, w, preferred_element_type=F32))
+    return row_sum(got, columns, inner)
+
+
+def lone_product(taps, f, w_ref, lanes, inner=False):
+    _, rows, columns, depth = taps.shape
+    depth //= 3
+    outer, centre = [], []
+    if not inner:
+        x = [taps[f, b : b + rows - 2, :, depth : 2 * depth].reshape((rows - 2) * columns, depth) for b in range(3)]
+        x = jnp.concatenate(x, axis=1)
+        w = [jnp.concatenate([w_ref[3 * b + e, :, lanes] for b in range(3)], axis=0) for e in range(3)]
+        outer = [jnp.dot(x, jnp.concatenate([w[0], w[2]], axis=1), preferred_element_type=F32), 0.0, 0.0]
+        centre = [jnp.dot(x, w[1], preferred_element_type=F32), 0.0, 0.0]
+    for b in range(0 if not inner else 3):
+        first, end = row_span(b, rows, inner)
+        x = taps[f, first:end, :, depth : 2 * depth].reshape((end - first) * columns, depth)
+        pair = jnp.concatenate([w_ref[3 * b, :, lanes], w_ref[3 * b + 2, :, lanes]], axis=1)
+        outer.append(jnp.dot(x, pair, preferred_element_type=F32))
+        centre.append(jnp.dot(x, w_ref[3 * b + 1, :, lanes], preferred_element_type=F32))
+    outer, centre = row_sum(outer, columns, inner), row_sum(centre, columns, inner)
+    left, right = outer[:, 0:128], outer[:, 128:256]
+    at = lax.broadcasted_iota(jnp.int32, left.shape, 0) % columns
+    left = jnp.where(at == 0, 0.0, pltpu.roll(left, 1, axis=0))
+    right = jnp.where(at == columns - 1, 0.0, pltpu.roll(right, left.shape[0] - 1, axis=0))
+    return centre + left + right
 
 
 def spread_rows(own, up, down, f, r, rows, channels):
@@ -295,21 +336,21 @@
                 at = (2 * f + (r > 0)) * channels
                 v = jnp.concatenate([piece[2, :, at : at + channels].astype(F32) for piece in pieces], axis=1)
             put_row(taps, f, r, v)
-    one = tap_product(taps, 0, early_ref, slice(128, 256))
+    one = lone_product(taps, 0, early_ref, slice(128, 256))
     both = tap_product(taps, 1, early_ref, slice(0, 256))
     out_ref[0] = one + both[:, 0:128]
     out_ref[1] = both[:, 128:256]
 
 
-def conv_current(taps, late_ref, early_ref, cached_ref):
-    both = tap_product(taps, 0, late_ref, slice(0, 256))
+def conv_current(taps, late_ref, early_ref, cached_ref, inner=False):
+    both = tap_product(taps, 0, late_ref, slice(0, 256), inner)
     yield cached_ref[0] + both[:, 0:128]
     middle = cached_ref[1] + both[:, 128:256]
-    last = tap_product(taps, 0, early_ref, slice(128, 256))
-    both = tap_product(taps, 1, late_ref, slice(0, 256))
+    last = lone_product(taps, 0, early_ref, slice(128, 256), inner)
+    both = tap_product(taps, 1, late_ref, slice(0, 256), inner)
     yield middle + both[:, 0:128]
     last = last + both[:, 128:256]
-    yield last + tap_product(taps, 2, late_ref, slice(0, 128))
+    yield last + lone_product(taps, 2, late_ref, slice(0, 128), inner)
 
 
 def gain_of(refs, n, channels):
@@ -359,8 +400,8 @@
 
 def last_body(n_stats, count, *refs):
     stats = refs[:n_stats]
-    gains, (p0, p1, p2, p3) = refs[n_stats : n_stats + 4], refs[n_stats + 4 : n_stats + 8]
-    cached_ref, late_ref, early_ref, out_ref, scale_ref, taps = refs[n_stats + 8 :]
+    gains, (p0, p1, p2, *p3) = refs[n_stats : n_stats + 4], refs[n_stats + 4 : n_stats + 9]
+    cached_ref, late_ref, early_ref, out_ref, scale_ref, taps = refs[n_stats + 9 :]
     frames, rows, _, _ = taps.shape
     channels = p0.shape[2] // (rows - 2)
 
@@ -373,12 +414,12 @@
     scale_ref[0:1, :] = mean
     scale_ref[1:2, :] = scale
     for f in range(frames):
-        taps[f, 0] = jnp.zeros_like(taps[f, 0])
-        taps[f, rows - 1] = jnp.zeros_like(taps[f, rows - 1])
         for r in range(1, rows - 1):
-            v = spread_rows((p0, p1, p2, p3), None, None, f, r, rows, channels)
+            at = slice((r - 1) * channels, r * channels)
+            far = jnp.concatenate([piece[f, :, at].astype(F32) for piece in p3], axis=0)
+            v = jnp.concatenate([piece[f, :, at].astype(F32) for piece in (p0, p1, p2)] + [far], axis=1)
             put_row(taps, f, r, activate(v, mean, scale))
-    for f, got in enumerate(conv_current(taps, late_ref, early_ref, cached_ref)):
+    for f, got in enumerate(conv_current(taps, late_ref, early_ref, cached_ref, True)):
         out_ref[f] = got
 
 
@@ -490,7 +531,7 @@
 
     def turn(w):
         shape = shaped((9, wide, 256), BF16)
-        return call(weights_body, (shape, shape), scratch=[pltpu.VMEM((3, wide, 128), F32)], n_in=1)(w)
+        return call(weights_body, (shape, shape), scratch=[pltpu.VMEM((3, wide, 128), BF16)], n_in=1)(w)
 
     late_one, early_one = turn(weight_one)
     late_two, early_two = turn(weight_two)
@@ -516,22 +557,22 @@
         (shaped((frames, rows, columns, wide), BF16), shaped((2, wide), F32)),
         flops=flops // 4,
         scratch=[
-            pltpu.VMEM((rows + 2, frames + 2, 3 * lc, columns), BF16),
+            pltpu.VMEM((rows + 2, columns, (frames + 2) * 3 * lc), BF16),
             pltpu.VMEM((27 * lc, wide), BF16),
             pltpu.SMEM((rows + 2,), jnp.int32),
         ],
         specs=[SMEM] + [VMEM] * 9,
     )(row_map, near, far, before, span, after, *got)
 
-    def over_tiles(x):
+    def over_tiles(x, stages):
         x = jnp.stack(xor_stage(x, "tile", [1]))
-        stages = far_masks(tiles)
         for masks in stages[:-1]:
             x = jnp.concatenate(xor_stage(x, "tile", masks), axis=0)
         return xor_stage(x, "tile", stages[-1])
 
+    doubling = [[1 << n] for n in range(1, tiles.bit_length() - 1)]
     count = frames * spots
-    stats = over_tiles(stat)
+    stats = over_tiles(stat, doubling)
     middle, stat_two = call(
         functools.partial(middle_body, len(stats), count),
         (shaped((frames, columns, tile_rows * channels), BF16), shaped((2, 128), F32)),
@@ -543,15 +584,17 @@
         n_in=len(stats) + 8,
     )(*stats, *got, first, cached_one, late_one, early_one)
 
-    mids = xor_stage(middle, "src", others)
-    stats = over_tiles(jnp.stack(xor_stage(stat_two, "src", others)))
-    above, below = edges_of(mids, channels)
+    mids = xor_stage(middle, "src", [1, 2])
+    cut = columns // 2
+    mids += [xor_send(mids[1][:, :cut], "src", 2), xor_send(mids[2][:, cut:], "src", 1)]
+    stats = over_tiles(jnp.stack(xor_stage(stat_two, "src", others)), far_masks(tiles))
+    above, below = edges_of(mids[:3] + [jnp.concatenate(mids[3:], axis=1)], channels)
     part, scales = call(
         functools.partial(last_body, len(stats), count),
         (shaped((frames, spots, 128), F32), shaped((2, wide), F32)),
         flops=flops * 2,
         scratch=[pltpu.VMEM((frames, rows, columns, 3 * wide), BF16)],
-        n_in=len(stats) + 11,
+        n_in=len(stats) + 12,
     )(*stats, *got, *mids, cached_two, late_two, early_two)
     decoded = call(
         edge_body,

time: 120 us -> 113 us (0.942)
  the two profiles are of different devices: /device:TPU:1 before, /device:TPU:0 now
where the time goes in v2:
time: 113 us
  starting transfers between devices  48.1 us (43%)
  Pallas kernels  31.8 us (28%)
  waiting for transfers between devices  31.4 us (28%)
    ppermute x27, starting transfers between devices, xor_send(): lax.ppermute(x, axis, [(i, i ^ mask) for i in range(lax.axis_size(axis))])  41.6 us
    ppermute x27, waiting for transfers between devices, xor_send(): lax.ppermute(x, axis, [(i, i ^ mask) for i in range(lax.axis_size(axis))])  30.7 us
    pallas_call x1, Pallas kernels, window(): call(functools.partial(last_body, len(stats), count), (shaped((frames, sp...  6.39 us
    pallas_call x1, Pallas kernels, window(): call(functools.partial(middle_body, len(stats), count), (shaped((frames,...  5.84 us
    pallas_call x2, Pallas kernels, cached(): call(cached_body, shaped((2, spots, 128), F32), flops=flops, scratch=[plt...  5.73 us
    pallas_call x1, Pallas kernels, window(): call(first_body, (shaped((frames, rows, columns, wide), BF16), shaped((2,...  4.47 us
    pallas_call x2, Pallas kernels, turn(): call(weights_body, (shape, shape), scratch=[pltpu.VMEM((3, wide, 128), BF...  4.14 us
    ppermute x2, starting transfers between devices, to_next(): lax.ppermute(x, 'tile', [(i, i + 1) for i in range(lax.axis_size('tile')...  3.73 us
  transfers between devices with their start and end apart: 31, of which 9 were waited for; matrix products, arithmetic and copies ran while one was open for 1% of the time, Pallas kernels for 20%

profile of v2, /device:TPU:0, one launch (start us, length us, event | category | flops | bytes accessed | tf_op | source)
XLA Modules:
  0.0 112.9 jit_solution(7194556939748176768)
XLA Ops:
  1.1 3.0 %collective-permute-start = (bf16[128,480]{1,0:T(8,128)(2,1)S(1)}, bf16[128,480]{1,0:T(8,128)(2,1)S(1)}, u32[]{:S(2)}, u32[]{:S(2)}) collective-permute-start(bf16[128,480]{1,0:T(8,128)(2,1)S(1)} %shard_map.100.refs_0_.m0.refs_2_.refs_4_), channel_id=1, source_target_pairs={{0,8},{8,0},{16,24},{24,16},{1,9},{9,1},{17,25},{25,17},{2,10},{10... | collective-permute-start | bytes 368648 | tf_op jit(solution)/shard_map/ppermute | solution.py:34
  4.1 1.5 %collective-permute-start.1 = (bf16[128,480]{1,0:T(8,128)(2,1)S(1)}, bf16[128,480]{1,0:T(8,128)(2,1)S(1)}, u32[]{:S(2)}, u32[]{:S(2)}) collective-permute-start(bf16[128,480]{1,0:T(8,128)(2,1)S(1)} %shard_map.100.refs_0_.m0.refs_2_.refs_4_), channel_id=1, source_target_pairs={{0,16},{8,24},{16,0},{24,8},{1,17},{9,25},{17,1},{25,9},{2,18},{10... | collective-permute-start | bytes 368648 | tf_op jit(solution)/shard_map/ppermute | solution.py:34
  5.7 2.3 %collective-permute-done.refs_1_.m1.refs_3_.refs_5_ = bf16[128,480]{1,0:T(8,128)(2,1)S(1)} collective-permute-done((bf16[128,480]{1,0:T(8,128)(2,1)S(1)}, bf16[128,480]{1,0:T(8,128)(2,1)S(1)}, u32[]{:S(2)}, u32[]{:S(2)}) %collective-permute-start) | collective-permute-done | bytes 122912 | tf_op jit(solution)/shard_map/ppermute | solution.py:34
  8.0 3.9 %collective-permute-done.1.refs_2_.m2.refs_4_.refs_6_ = bf16[128,480]{1,0:T(8,128)(2,1)S(1)} collective-permute-done((bf16[128,480]{1,0:T(8,128)(2,1)S(1)}, bf16[128,480]{1,0:T(8,128)(2,1)S(1)}, u32[]{:S(2)}, u32[]{:S(2)}) %collective-permute-start.1) | collective-permute-done | bytes 122912 | tf_op jit(solution)/shard_map/ppermute | solution.py:34
  11.9 3.7 %collective-permute-start.5 = (bf16[4,16,480]{2,1,0:T(8,128)(2,1)S(1)}, bf16[4,16,480]{2,1,0:T(8,128)(2,1)S(1)}, u32[]{:S(2)}, u32[]{:S(2)}) collective-permute-start(bf16[4,16,480]{2,1,0:T(8,128)(2,1)S(1)} %shard_map.101), channel_id=1, source_target_pairs={{0,6},{1,7},{2,4},{3,5},{4,2},{5,3},{6,0},{7,1},{8,14},{9,15},{10,... | collective-permute-start | bytes 184328 | tf_op jit(solution)/shard_map/ppermute | solution.py:34
  16.4 1.5 %shard_map.102 = (bf16[3,160,384]{2,1,0:T(8,128)(2,1)S(1)}, bf16[3,160,384]{2,1,0:T(8,128)(2,1)S(1)}, bf16[4,16,320]{2,1,0:T(8,128)(2,1)S(1)}, bf16[192,384]{1,0:T(8,128)(2,1)S(1)}, bf16[192,384]{1,0:T(8,128)(2,1)S(1)}) custom-call(bf16[2,4,160,96]{3,2,1,0:T(8,128)(2,1)} %bitcast.19, bf16[2,4,160,96]{3,2,1,0:T(8,128)(2,1)} %bitcast.20, ...), custom_call_target="tpu_custom_call" | custom-call | bytes 1048576 | tf_op jit(solution)/shard_map/pallas_call | solution.py:513
  17.9 1.3 %collective-permute-start.7 = (bf16[192,384]{1,0:T(8,128)(2,1)S(1)}, bf16[192,384]{1,0:T(8,128)(2,1)S(1)}, u32[]{:S(2)}, u32[]{:S(2)}) collective-permute-start(bf16[192,384]{1,0:T(8,128)(2,1)S(1)} %get-tuple-element.22), channel_id=1, source_target_pairs={{0,1},{1,2},{2,3},{3,4},{4,5},{5,6},{6,7},{8,9},{9,10},{10,11},{11... | collective-permute-start | bytes 442376 | tf_op jit(solution)/shard_map/ppermute | solution.py:58
  19.2 1.3 %collective-permute-start.8 = (bf16[192,384]{1,0:T(8,128)(2,1)S(1)}, bf16[192,384]{1,0:T(8,128)(2,1)S(1)}, u32[]{:S(2)}, u32[]{:S(2)}) collective-permute-start(bf16[192,384]{1,0:T(8,128)(2,1)S(1)} %get-tuple-element.24), channel_id=1, source_target_pairs={{1,0},{2,1},{3,2},{4,3},{5,4},{6,5},{7,6},{9,8},{10,9},{11,10},{12... | collective-permute-start | bytes 442376 | tf_op jit(solution)/shard_map/ppermute | solution.py:62
  20.8 2.5 %collective-permute-start.6 = (bf16[16,16,480]{2,1,0:T(8,128)(2,1)S(1)}, bf16[16,16,480]{2,1,0:T(8,128)(2,1)S(1)}, u32[]{:S(2)}, u32[]{:S(2)}) collective-permute-start(bf16[16,16,480]{2,1,0:T(8,128)(2,1)S(1)} %pad_maximum_fusion.2.near_ref), channel_id=1, source_target_pairs={{0,1},{1,0},{2,3},{3,2},{4,5},{5,4},{6,7},{7,6},{8,9},{9,8},{10,11... | collective-permute-start | bytes 737288 | tf_op jit(solution)/shard_map/ppermute | solution.py:34
  26.7 1.4 %collective-permute-start.14 = (bf16[3,160,384]{2,1,0:T(8,128)(2,1)S(1)}, bf16[3,160,384]{2,1,0:T(8,128)(2,1)S(1)}, u32[]{:S(2)}, u32[]{:S(2)}) collective-permute-start(bf16[3,160,384]{2,1,0:T(8,128)(2,1)S(1)} %get-tuple-element.29.p0), channel_id=1, source_target_pairs={{0,24},{8,16},{16,8},{24,0},{1,25},{9,17},{17,9},{25,1},{2,26},{10... | collective-permute-start | bytes 1105928 | tf_op jit(solution)/shard_map/ppermute | solution.py:34
  28.1 4.5 %shard_map.103 = (bf16[3,6,160,384]{3,2,1,0:T(8,128)(2,1)S(1)}, f32[2,384]{1,0:T(2,128)S(1)}) custom-call(s32[32]{0:T(128)S(1)} %copy-done.2, bf16[16,16,480]{2,1,0:T(8,128)(2,1)S(1)} %pad_maximum_fusion.2.near_ref, bf16[16,16,480]{2,1,0:T(8,128)(2,1)S(1)} %collective-permute-done.6.far_ref, bf16[192,384]{1,0:T(8,128)(2,1)S(1)} %collective-permute-done.7.before, ...), custom_call_target="tpu_custom_call" | custom-call | flops 318504960 | bytes 1048576 | tf_op jit(solution)/shard_map/pallas_call | solution.py:555
  32.6 2.9 %collective-permute-start.9 = (f32[2,384]{1,0:T(2,128)S(1)}, f32[2,384]{1,0:T(2,128)S(1)}, u32[]{:S(2)}, u32[]{:S(2)}) collective-permute-start(f32[2,384]{1,0:T(2,128)S(1)} %get-tuple-element.25), channel_id=1, source_target_pairs={{0,1},{1,0},{2,3},{3,2},{4,5},{5,4},{6,7},{7,6},{8,9},{9,8},{10,11... | collective-permute-start | bytes 9224 | tf_op jit(solution)/shard_map/ppermute | solution.py:34
  36.3 1.5 %collective-permute-start.10 = (f32[2,2,384]{2,1,0:T(2,128)S(1)}, f32[2,2,384]{2,1,0:T(2,128)S(1)}, u32[]{:S(2)}, u32[]{:S(2)}) collective-permute-start(f32[2,2,384]{2,1,0:T(2,128)S(1)} %pad_maximum_fusion.5), channel_id=1, source_target_pairs={{0,2},{1,3},{2,0},{3,1},{4,6},{5,7},{6,4},{7,5},{8,10},{9,11},{10,... | collective-permute-start | bytes 18440 | tf_op jit(solution)/shard_map/ppermute | solution.py:34
  37.8 2.0 %shard_map.105 = (bf16[9,384,256]{2,1,0:T(8,128)(2,1)S(1)}, bf16[9,384,256]{2,1,0:T(8,128)(2,1)S(1)}) custom-call(bf16[3,3,3,96,384]{4,3,2,1,0:T(8,128)(2,1)S(1)} %copy-done), custom_call_target="tpu_custom_call" | custom-call | bytes 1048576 | tf_op jit(solution)/shard_map/pallas_call | solution.py:534
  39.8 2.2 %shard_map.108 = (bf16[9,384,256]{2,1,0:T(8,128)(2,1)S(1)}, bf16[9,384,256]{2,1,0:T(8,128)(2,1)S(1)}) custom-call(bf16[3,3,3,96,384]{4,3,2,1,0:T(8,128)(2,1)S(1)} %copy-done.1), custom_call_target="tpu_custom_call" | custom-call | bytes 1048576 | tf_op jit(solution)/shard_map/pallas_call | solution.py:534
  42.0 2.4 %collective-permute-start.11 = (f32[4,2,384]{2,1,0:T(2,128)S(1)}, f32[4,2,384]{2,1,0:T(2,128)S(1)}, u32[]{:S(2)}, u32[]{:S(2)}) collective-permute-start(f32[4,2,384]{2,1,0:T(2,128)S(1)} %pad_maximum_fusion.3.refs_0_), channel_id=1, source_target_pairs={{0,4},{1,5},{2,6},{3,7},{4,0},{5,1},{6,2},{7,3},{8,12},{9,13},{10,... | collective-permute-start | bytes 36872 | tf_op jit(solution)/shard_map/ppermute | solution.py:34
  44.5 2.9 %shard_map.106.refs_7_ = f32[2,640,128]{2,1,0:T(8,128)S(1)} custom-call(bf16[3,160,384]{2,1,0:T(8,128)(2,1)S(1)} %get-tuple-element.29.p0, bf16[3,160,384]{2,1,0:T(8,128)(2,1)S(1)} %collective-permute-done.12.p1, bf16[3,160,384]{2,1,0:T(8,128)(2,1)S(1)} %collective-permute-done.13.p2, bf16[3,160,384]{2,1,0:T(8,128)(2,1)S(1)} %collective-permute-done.14.p3, ...), custom_call_target="tpu_custom_call" | custom-call | flops 1274019840 | bytes 1048576 | tf_op jit(solution)/shard_map/pallas_call | solution.py:544
  47.4 5.8 %shard_map.107 = (bf16[3,160,384]{2,1,0:T(8,128)(2,1)S(1)}, f32[2,128]{1,0:T(2,128)S(1)}) custom-call(f32[4,2,384]{2,1,0:T(2,128)S(1)} %pad_maximum_fusion.3.refs_0_, f32[4,2,384]{2,1,0:T(2,128)S(1)} %collective-permute-done.11.refs_1_, bf16[128,480]{1,0:T(8,128)(2,1)S(1)} %shard_map.100.refs_0_.m0.refs_2_.refs_4_, ...), custom_call_target="tpu_custom_call" | custom-call | flops 2548039680 | bytes 1048576 | tf_op jit(solution)/shard_map/pallas_call | solution.py:576
  53.2 1.8 %collective-permute-start.17 = (f32[2,128]{1,0:T(2,128)S(1)}, f32[2,128]{1,0:T(2,128)S(1)}, u32[]{:S(2)}, u32[]{:S(2)}) collective-permute-start(f32[2,128]{1,0:T(2,128)S(1)} %get-tuple-element.32), channel_id=1, source_target_pairs={{0,24},{8,16},{16,8},{24,0},{1,25},{9,17},{17,9},{25,1},{2,26},{10... | collective-permute-start | bytes 3080 | tf_op jit(solution)/shard_map/ppermute | solution.py:34
  59.1 1.3 %collective-permute-start.26 = (bf16[3,160,384]{2,1,0:T(8,128)(2,1)S(1)}, bf16[3,160,384]{2,1,0:T(8,128)(2,1)S(1)}, u32[]{:S(2)}, u32[]{:S(2)}) collective-permute-start(bf16[3,160,384]{2,1,0:T(8,128)(2,1)S(1)} %get-tuple-element.34.p0), channel_id=1, source_target_pairs={{0,8},{8,0},{16,24},{24,16},{1,9},{9,1},{17,25},{25,17},{2,10},{10... | collective-permute-start | bytes 1105928 | tf_op jit(solution)/shard_map/ppermute | solution.py:34
  61.0 1.7 %collective-permute-start.28 = (bf16[3,160,384]{2,1,0:T(8,128)(2,1)S(1)}, bf16[3,160,384]{2,1,0:T(8,128)(2,1)S(1)}, u32[]{:S(2)}, u32[]{:S(2)}) collective-permute-start(bf16[3,160,384]{2,1,0:T(8,128)(2,1)S(1)} %get-tuple-element.34.p0), channel_id=1, source_target_pairs={{0,24},{8,16},{16,8},{24,0},{1,25},{9,17},{17,9},{25,1},{2,26},{10... | collective-permute-start | bytes 1105928 | tf_op jit(solution)/shard_map/ppermute | solution.py:34
  62.7 5.5 %collective-permute-done.22.refs_9_ = bf16[3,160,384]{2,1,0:T(8,128)(2,1)S(1)} collective-permute-done((bf16[3,160,384]{2,1,0:T(8,128)(2,1)S(1)}, bf16[3,160,384]{2,1,0:T(8,128)(2,1)S(1)}, u32[]{:S(2)}, u32[]{:S(2)}) %collective-permute-start.22) | collective-permute-done | bytes 368672 | tf_op jit(solution)/shard_map/ppermute | solution.py:34
  68.2 1.6 %collective-permute-start.24 = (bf16[3,80,384]{2,1,0:T(8,128)(2,1)S(1)}, bf16[3,80,384]{2,1,0:T(8,128)(2,1)S(1)}, u32[]{:S(2)}, u32[]{:S(2)}) collective-permute-start(bf16[3,80,384]{2,1,0:T(8,128)(2,1)S(1)} %slice.40), channel_id=1, source_target_pairs={{0,16},{8,24},{16,0},{24,8},{1,17},{9,25},{17,1},{25,9},{2,18},{10... | collective-permute-start | bytes 552968 | tf_op jit(solution)/shard_map/ppermute | solution.py:34
  70.9 16.4 %collective-permute-done.24.refs_11_ = bf16[3,80,384]{2,1,0:T(8,128)(2,1)S(1)} collective-permute-done((bf16[3,80,384]{2,1,0:T(8,128)(2,1)S(1)}, bf16[3,80,384]{2,1,0:T(8,128)(2,1)S(1)}, u32[]{:S(2)}, u32[]{:S(2)}) %collective-permute-start.24) | collective-permute-done | bytes 184352 | tf_op jit(solution)/shard_map/ppermute | solution.py:34
  87.7 2.4 %collective-permute-start.29 = (bf16[3,160,384]{2,1,0:T(8,128)(2,1)S(1)}, bf16[3,160,384]{2,1,0:T(8,128)(2,1)S(1)}, u32[]{:S(2)}, u32[]{:S(2)}) collective-permute-start(bf16[3,160,384]{2,1,0:T(8,128)(2,1)S(1)} %pad_maximum_fusion), channel_id=1, source_target_pairs={{0,1},{1,2},{2,3},{3,4},{4,5},{5,6},{6,7},{8,9},{9,10},{10,11},{11... | collective-permute-start | bytes 1105928 | tf_op jit(solution)/shard_map/ppermute | solution.py:58
  90.4 1.5 %collective-permute-start.30 = (bf16[3,160,384]{2,1,0:T(8,128)(2,1)S(1)}, bf16[3,160,384]{2,1,0:T(8,128)(2,1)S(1)}, u32[]{:S(2)}, u32[]{:S(2)}) collective-permute-start(bf16[3,160,384]{2,1,0:T(8,128)(2,1)S(1)} %pad_maximum_fusion.1), channel_id=1, source_target_pairs={{1,0},{2,1},{3,2},{4,3},{5,4},{6,5},{7,6},{9,8},{10,9},{11,10},{12... | collective-permute-start | bytes 1105928 | tf_op jit(solution)/shard_map/ppermute | solution.py:62
  91.9 5.3 %collective-permute-start.19 = (f32[2,4,2,128]{3,2,1,0:T(2,128)S(1)}, f32[2,4,2,128]{3,2,1,0:T(2,128)S(1)}, u32[]{:S(2)}, u32[]{:S(2)}) collective-permute-start(f32[2,4,2,128]{3,2,1,0:T(2,128)S(1)} %pad_maximum_fusion.4.refs_0_), channel_id=1, source_target_pairs={{0,2},{1,3},{2,0},{3,1},{4,6},{5,7},{6,4},{7,5},{8,10},{9,11},{10,... | collective-permute-start | bytes 24584 | tf_op jit(solution)/shard_map/ppermute | solution.py:34
  97.3 1.5 %collective-permute-start.20 = (f32[2,4,2,128]{3,2,1,0:T(2,128)S(1)}, f32[2,4,2,128]{3,2,1,0:T(2,128)S(1)}, u32[]{:S(2)}, u32[]{:S(2)}) collective-permute-start(f32[2,4,2,128]{3,2,1,0:T(2,128)S(1)} %pad_maximum_fusion.4.refs_0_), channel_id=1, source_target_pairs={{0,4},{1,5},{2,6},{3,7},{4,0},{5,1},{6,2},{7,3},{8,12},{9,13},{10,... | collective-permute-start | bytes 24584 | tf_op jit(solution)/shard_map/ppermute | solution.py:34
  99.9 2.9 %shard_map.109.refs_13_ = f32[2,640,128]{2,1,0:T(8,128)S(1)} custom-call(bf16[3,160,384]{2,1,0:T(8,128)(2,1)S(1)} %get-tuple-element.34.p0, bf16[3,160,384]{2,1,0:T(8,128)(2,1)S(1)} %collective-permute-done.26.p1, bf16[3,160,384]{2,1,0:T(8,128)(2,1)S(1)} %collective-permute-done.27.p2, bf16[3,160,384]{2,1,0:T(8,128)(2,1)S(1)} %collective-permute-done.28.p3, ...), custom_call_target="tpu_custom_call" | custom-call | flops 1274019840 | bytes 1048576 | tf_op jit(solution)/shard_map/pallas_call | solution.py:544
  102.8 1.3 %collective-permute-done.20.refs_2_ = f32[2,4,2,128]{3,2,1,0:T(2,128)S(1)} collective-permute-done((f32[2,4,2,128]{3,2,1,0:T(2,128)S(1)}, f32[2,4,2,128]{3,2,1,0:T(2,128)S(1)}, u32[]{:S(2)}, u32[]{:S(2)}) %collective-permute-start.20) | collective-permute-done | bytes 8224 | tf_op jit(solution)/shard_map/ppermute | solution.py:34
  104.2 6.4 %shard_map.110 = (f32[3,640,128]{2,1,0:T(8,128)S(1)}, f32[2,384]{1,0:T(2,128)S(1)}) custom-call(f32[2,4,2,128]{3,2,1,0:T(2,128)S(1)} %pad_maximum_fusion.4.refs_0_, f32[2,4,2,128]{3,2,1,0:T(2,128)S(1)} %collective-permute-done.19.refs_1_, f32[2,4,2,128]{3,2,1,0:T(2,128)S(1)} %collective-permute-done.20.refs_2_, ...), custom_call_target="tpu_custom_call" | custom-call | flops 2548039680 | bytes 1048576 | tf_op jit(solution)/shard_map/pallas_call | solution.py:592
  110.6 2.1 %shard_map.111 = bf16[3,4,160,96]{3,2,1,0:T(8,128)(2,1)} custom-call(f32[3,640,128]{2,1,0:T(8,128)S(1)} %get-tuple-element.37.part_ref, f32[2,384]{1,0:T(2,128)S(1)} %get-tuple-element.38.scale_ref, bf16[3,160,384]{2,1,0:T(8,128)(2,1)S(1)} %collective-permute-done.29.up, bf16[3,160,384]{2,1,0:T(8,128)(2,1)S(1)} %collective-permute-done.30.down, ...), custom_call_target="tpu_custom_call" | custom-call | flops 637009920 | bytes 1048576 | tf_op jit(solution)/shard_map/pallas_call | solution.py:599
  (64 shorter events, 14.2 us)
Async XLA Ops:
  0.0 28.1 %copy-start.2 = (s32[32]{0:T(128)S(1)}, s32[32]{0:T(128)}, u32[]{:S(2)}) copy-start(s32[32]{0:T(128)} %map_ref.1) | copy-start | bytes 388
  1.1 6.9 %collective-permute-start = (bf16[128,480]{1,0:T(8,128)(2,1)S(1)}, bf16[128,480]{1,0:T(8,128)(2,1)S(1)}, u32[]{:S(2)}, u32[]{:S(2)}) collective-permute-start(bf16[128,480]{1,0:T(8,128)(2,1)S(1)} %shard_map.100.refs_0_.m0.refs_2_.refs_4_), channel_id=1, source_target_pairs={{0,8},{8,0},{16,24},{24,16},{1,9},{9,1},{17,25},{25,17},{2,10},{10... | collective-permute-start | bytes 368648 | tf_op jit(solution)/shard_map/ppermute | solution.py:34
  4.1 7.8 %collective-permute-start.1 = (bf16[128,480]{1,0:T(8,128)(2,1)S(1)}, bf16[128,480]{1,0:T(8,128)(2,1)S(1)}, u32[]{:S(2)}, u32[]{:S(2)}) collective-permute-start(bf16[128,480]{1,0:T(8,128)(2,1)S(1)} %shard_map.100.refs_0_.m0.refs_2_.refs_4_), channel_id=1, source_target_pairs={{0,16},{8,24},{16,0},{24,8},{1,17},{9,25},{17,1},{25,9},{2,18},{10... | collective-permute-start | bytes 368648 | tf_op jit(solution)/shard_map/ppermute | solution.py:34
  5.7 6.3 %collective-permute-start.2 = (bf16[128,480]{1,0:T(8,128)(2,1)S(1)}, bf16[128,480]{1,0:T(8,128)(2,1)S(1)}, u32[]{:S(2)}, u32[]{:S(2)}) collective-permute-start(bf16[128,480]{1,0:T(8,128)(2,1)S(1)} %shard_map.100.refs_0_.m0.refs_2_.refs_4_), channel_id=1, source_target_pairs={{0,24},{8,16},{16,8},{24,0},{1,25},{9,17},{17,9},{25,1},{2,26},{10... | collective-permute-start | bytes 368648 | tf_op jit(solution)/shard_map/ppermute | solution.py:34
  11.9 8.6 %collective-permute-start.5 = (bf16[4,16,480]{2,1,0:T(8,128)(2,1)S(1)}, bf16[4,16,480]{2,1,0:T(8,128)(2,1)S(1)}, u32[]{:S(2)}, u32[]{:S(2)}) collective-permute-start(bf16[4,16,480]{2,1,0:T(8,128)(2,1)S(1)} %shard_map.101), channel_id=1, source_target_pairs={{0,6},{1,7},{2,4},{3,5},{4,2},{5,3},{6,0},{7,1},{8,14},{9,15},{10,... | collective-permute-start | bytes 184328 | tf_op jit(solution)/shard_map/ppermute | solution.py:34
  15.6 5.2 %collective-permute-start.4 = (bf16[4,16,480]{2,1,0:T(8,128)(2,1)S(1)}, bf16[4,16,480]{2,1,0:T(8,128)(2,1)S(1)}, u32[]{:S(2)}, u32[]{:S(2)}) collective-permute-start(bf16[4,16,480]{2,1,0:T(8,128)(2,1)S(1)} %shard_map.101), channel_id=1, source_target_pairs={{0,4},{1,5},{2,6},{3,7},{4,0},{5,1},{6,2},{7,3},{8,12},{9,13},{10,... | collective-permute-start | bytes 184328 | tf_op jit(solution)/shard_map/ppermute | solution.py:34
  15.6 5.2 %collective-permute-start.3 = (bf16[4,16,480]{2,1,0:T(8,128)(2,1)S(1)}, bf16[4,16,480]{2,1,0:T(8,128)(2,1)S(1)}, u32[]{:S(2)}, u32[]{:S(2)}) collective-permute-start(bf16[4,16,480]{2,1,0:T(8,128)(2,1)S(1)} %shard_map.101), channel_id=1, source_target_pairs={{0,2},{1,3},{2,0},{3,1},{4,6},{5,7},{6,4},{7,5},{8,10},{9,11},{10,... | collective-permute-start | bytes 184328 | tf_op jit(solution)/shard_map/ppermute | solution.py:34
  17.9 5.4 %collective-permute-start.7 = (bf16[192,384]{1,0:T(8,128)(2,1)S(1)}, bf16[192,384]{1,0:T(8,128)(2,1)S(1)}, u32[]{:S(2)}, u32[]{:S(2)}) collective-permute-start(bf16[192,384]{1,0:T(8,128)(2,1)S(1)} %get-tuple-element.22), channel_id=1, source_target_pairs={{0,1},{1,2},{2,3},{3,4},{4,5},{5,6},{6,7},{8,9},{9,10},{10,11},{11... | collective-permute-start | bytes 442376 | tf_op jit(solution)/shard_map/ppermute | solution.py:58
  19.2 4.7 %collective-permute-start.8 = (bf16[192,384]{1,0:T(8,128)(2,1)S(1)}, bf16[192,384]{1,0:T(8,128)(2,1)S(1)}, u32[]{:S(2)}, u32[]{:S(2)}) collective-permute-start(bf16[192,384]{1,0:T(8,128)(2,1)S(1)} %get-tuple-element.24), channel_id=1, source_target_pairs={{1,0},{2,1},{3,2},{4,3},{5,4},{6,5},{7,6},{9,8},{10,9},{11,10},{12... | collective-permute-start | bytes 442376 | tf_op jit(solution)/shard_map/ppermute | solution.py:62
  20.8 7.3 %collective-permute-start.6 = (bf16[16,16,480]{2,1,0:T(8,128)(2,1)S(1)}, bf16[16,16,480]{2,1,0:T(8,128)(2,1)S(1)}, u32[]{:S(2)}, u32[]{:S(2)}) collective-permute-start(bf16[16,16,480]{2,1,0:T(8,128)(2,1)S(1)} %pad_maximum_fusion.2.near_ref), channel_id=1, source_target_pairs={{0,1},{1,0},{2,3},{3,2},{4,5},{5,4},{6,7},{7,6},{8,9},{9,8},{10,11... | collective-permute-start | bytes 737288 | tf_op jit(solution)/shard_map/ppermute | solution.py:34
  24.6 19.9 %collective-permute-start.12 = (bf16[3,160,384]{2,1,0:T(8,128)(2,1)S(1)}, bf16[3,160,384]{2,1,0:T(8,128)(2,1)S(1)}, u32[]{:S(2)}, u32[]{:S(2)}) collective-permute-start(bf16[3,160,384]{2,1,0:T(8,128)(2,1)S(1)} %get-tuple-element.29.p0), channel_id=1, source_target_pairs={{0,8},{8,0},{16,24},{24,16},{1,9},{9,1},{17,25},{25,17},{2,10},{10... | collective-permute-start | bytes 1105928 | tf_op jit(solution)/shard_map/ppermute | solution.py:34
  25.8 18.7 %collective-permute-start.13 = (bf16[3,160,384]{2,1,0:T(8,128)(2,1)S(1)}, bf16[3,160,384]{2,1,0:T(8,128)(2,1)S(1)}, u32[]{:S(2)}, u32[]{:S(2)}) collective-permute-start(bf16[3,160,384]{2,1,0:T(8,128)(2,1)S(1)} %get-tuple-element.29.p0), channel_id=1, source_target_pairs={{0,16},{8,24},{16,0},{24,8},{1,17},{9,25},{17,1},{25,9},{2,18},{10... | collective-permute-start | bytes 1105928 | tf_op jit(solution)/shard_map/ppermute | solution.py:34
  26.7 17.8 %collective-permute-start.14 = (bf16[3,160,384]{2,1,0:T(8,128)(2,1)S(1)}, bf16[3,160,384]{2,1,0:T(8,128)(2,1)S(1)}, u32[]{:S(2)}, u32[]{:S(2)}) collective-permute-start(bf16[3,160,384]{2,1,0:T(8,128)(2,1)S(1)} %get-tuple-element.29.p0), channel_id=1, source_target_pairs={{0,24},{8,16},{16,8},{24,0},{1,25},{9,17},{17,9},{25,1},{2,26},{10... | collective-permute-start | bytes 1105928 | tf_op jit(solution)/shard_map/ppermute | solution.py:34
  32.6 3.7 %collective-permute-start.9 = (f32[2,384]{1,0:T(2,128)S(1)}, f32[2,384]{1,0:T(2,128)S(1)}, u32[]{:S(2)}, u32[]{:S(2)}) collective-permute-start(f32[2,384]{1,0:T(2,128)S(1)} %get-tuple-element.25), channel_id=1, source_target_pairs={{0,1},{1,0},{2,3},{3,2},{4,5},{5,4},{6,7},{7,6},{8,9},{9,8},{10,11... | collective-permute-start | bytes 9224 | tf_op jit(solution)/shard_map/ppermute | solution.py:34
  36.3 5.6 %collective-permute-start.10 = (f32[2,2,384]{2,1,0:T(2,128)S(1)}, f32[2,2,384]{2,1,0:T(2,128)S(1)}, u32[]{:S(2)}, u32[]{:S(2)}) collective-permute-start(f32[2,2,384]{2,1,0:T(2,128)S(1)} %pad_maximum_fusion.5), channel_id=1, source_target_pairs={{0,2},{1,3},{2,0},{3,1},{4,6},{5,7},{6,4},{7,5},{8,10},{9,11},{10,... | collective-permute-start | bytes 18440 | tf_op jit(solution)/shard_map/ppermute | solution.py:34
  42.0 5.3 %collective-permute-start.11 = (f32[4,2,384]{2,1,0:T(2,128)S(1)}, f32[4,2,384]{2,1,0:T(2,128)S(1)}, u32[]{:S(2)}, u32[]{:S(2)}) collective-permute-start(f32[4,2,384]{2,1,0:T(2,128)S(1)} %pad_maximum_fusion.3.refs_0_), channel_id=1, source_target_pairs={{0,4},{1,5},{2,6},{3,7},{4,0},{5,1},{6,2},{7,3},{8,12},{9,13},{10,... | collective-permute-start | bytes 36872 | tf_op jit(solution)/shard_map/ppermute | solution.py:34
  53.2 5.9 %collective-permute-start.17 = (f32[2,128]{1,0:T(2,128)S(1)}, f32[2,128]{1,0:T(2,128)S(1)}, u32[]{:S(2)}, u32[]{:S(2)}) collective-permute-start(f32[2,128]{1,0:T(2,128)S(1)} %get-tuple-element.32), channel_id=1, source_target_pairs={{0,24},{8,16},{16,8},{24,0},{1,25},{9,17},{17,9},{25,1},{2,26},{10... | collective-permute-start | bytes 3080 | tf_op jit(solution)/shard_map/ppermute | solution.py:34
  55.0 5.5 %collective-permute-start.16 = (f32[2,128]{1,0:T(2,128)S(1)}, f32[2,128]{1,0:T(2,128)S(1)}, u32[]{:S(2)}, u32[]{:S(2)}) collective-permute-start(f32[2,128]{1,0:T(2,128)S(1)} %get-tuple-element.32), channel_id=1, source_target_pairs={{0,16},{8,24},{16,0},{24,8},{1,17},{9,25},{17,1},{25,9},{2,18},{10... | collective-permute-start | bytes 3080 | tf_op jit(solution)/shard_map/ppermute | solution.py:34
  55.9 5.1 %collective-permute-start.15 = (f32[2,128]{1,0:T(2,128)S(1)}, f32[2,128]{1,0:T(2,128)S(1)}, u32[]{:S(2)}, u32[]{:S(2)}) collective-permute-start(f32[2,128]{1,0:T(2,128)S(1)} %get-tuple-element.32), channel_id=1, source_target_pairs={{0,8},{8,0},{16,24},{24,16},{1,9},{9,1},{17,25},{25,17},{2,10},{10... | collective-permute-start | bytes 3080 | tf_op jit(solution)/shard_map/ppermute | solution.py:34
  56.8 11.5 %collective-permute-start.22 = (bf16[3,160,384]{2,1,0:T(8,128)(2,1)S(1)}, bf16[3,160,384]{2,1,0:T(8,128)(2,1)S(1)}, u32[]{:S(2)}, u32[]{:S(2)}) collective-permute-start(bf16[3,160,384]{2,1,0:T(8,128)(2,1)S(1)} %get-tuple-element.33.refs_8_), channel_id=1, source_target_pairs={{0,8},{8,0},{16,24},{24,16},{1,9},{9,1},{17,25},{25,17},{2,10},{10... | collective-permute-start | bytes 1105928 | tf_op jit(solution)/shard_map/ppermute | solution.py:34
  57.9 11.9 %collective-permute-start.23 = (bf16[3,160,384]{2,1,0:T(8,128)(2,1)S(1)}, bf16[3,160,384]{2,1,0:T(8,128)(2,1)S(1)}, u32[]{:S(2)}, u32[]{:S(2)}) collective-permute-start(bf16[3,160,384]{2,1,0:T(8,128)(2,1)S(1)} %get-tuple-element.33.refs_8_), channel_id=1, source_target_pairs={{0,16},{8,24},{16,0},{24,8},{1,17},{9,25},{17,1},{25,9},{2,18},{10... | collective-permute-start | bytes 1105928 | tf_op jit(solution)/shard_map/ppermute | solution.py:34
  59.1 32.8 %collective-permute-start.26 = (bf16[3,160,384]{2,1,0:T(8,128)(2,1)S(1)}, bf16[3,160,384]{2,1,0:T(8,128)(2,1)S(1)}, u32[]{:S(2)}, u32[]{:S(2)}) collective-permute-start(bf16[3,160,384]{2,1,0:T(8,128)(2,1)S(1)} %get-tuple-element.34.p0), channel_id=1, source_target_pairs={{0,8},{8,0},{16,24},{24,16},{1,9},{9,1},{17,25},{25,17},{2,10},{10... | collective-permute-start | bytes 1105928 | tf_op jit(solution)/shard_map/ppermute | solution.py:34
  60.5 36.8 %collective-permute-start.27 = (bf16[3,160,384]{2,1,0:T(8,128)(2,1)S(1)}, bf16[3,160,384]{2,1,0:T(8,128)(2,1)S(1)}, u32[]{:S(2)}, u32[]{:S(2)}) collective-permute-start(bf16[3,160,384]{2,1,0:T(8,128)(2,1)S(1)} %get-tuple-element.34.p0), channel_id=1, source_target_pairs={{0,16},{8,24},{16,0},{24,8},{1,17},{9,25},{17,1},{25,9},{2,18},{10... | collective-permute-start | bytes 1105928 | tf_op jit(solution)/shard_map/ppermute | solution.py:34
  61.0 37.7 %collective-permute-start.28 = (bf16[3,160,384]{2,1,0:T(8,128)(2,1)S(1)}, bf16[3,160,384]{2,1,0:T(8,128)(2,1)S(1)}, u32[]{:S(2)}, u32[]{:S(2)}) collective-permute-start(bf16[3,160,384]{2,1,0:T(8,128)(2,1)S(1)} %get-tuple-element.34.p0), channel_id=1, source_target_pairs={{0,24},{8,16},{16,8},{24,0},{1,25},{9,17},{17,9},{25,1},{2,26},{10... | collective-permute-start | bytes 1105928 | tf_op jit(solution)/shard_map/ppermute | solution.py:34
  68.2 19.0 %collective-permute-start.24 = (bf16[3,80,384]{2,1,0:T(8,128)(2,1)S(1)}, bf16[3,80,384]{2,1,0:T(8,128)(2,1)S(1)}, u32[]{:S(2)}, u32[]{:S(2)}) collective-permute-start(bf16[3,80,384]{2,1,0:T(8,128)(2,1)S(1)} %slice.40), channel_id=1, source_target_pairs={{0,16},{8,24},{16,0},{24,8},{1,17},{9,25},{17,1},{25,9},{2,18},{10... | collective-permute-start | bytes 552968 | tf_op jit(solution)/shard_map/ppermute | solution.py:34
  69.8 17.4 %collective-permute-start.25 = (bf16[3,80,384]{2,1,0:T(8,128)(2,1)S(1)}, bf16[3,80,384]{2,1,0:T(8,128)(2,1)S(1)}, u32[]{:S(2)}, u32[]{:S(2)}) collective-permute-start(bf16[3,80,384]{2,1,0:T(8,128)(2,1)S(1)} %slice.41), channel_id=1, source_target_pairs={{0,8},{8,0},{16,24},{24,16},{1,9},{9,1},{17,25},{25,17},{2,10},{10... | collective-permute-start | bytes 552968 | tf_op jit(solution)/shard_map/ppermute | solution.py:34
  87.3 3.1 %collective-permute-start.18 = (f32[4,2,128]{2,1,0:T(2,128)S(1)}, f32[4,2,128]{2,1,0:T(2,128)S(1)}, u32[]{:S(2)}, u32[]{:S(2)}) collective-permute-start(f32[4,2,128]{2,1,0:T(2,128)S(1)} %pad_maximum_fusion.6), channel_id=1, source_target_pairs={{0,1},{1,0},{2,3},{3,2},{4,5},{5,4},{6,7},{7,6},{8,9},{9,8},{10,11... | collective-permute-start | bytes 12296 | tf_op jit(solution)/shard_map/ppermute | solution.py:34
  87.7 22.9 %collective-permute-start.29 = (bf16[3,160,384]{2,1,0:T(8,128)(2,1)S(1)}, bf16[3,160,384]{2,1,0:T(8,128)(2,1)S(1)}, u32[]{:S(2)}, u32[]{:S(2)}) collective-permute-start(bf16[3,160,384]{2,1,0:T(8,128)(2,1)S(1)} %pad_maximum_fusion), channel_id=1, source_target_pairs={{0,1},{1,2},{2,3},{3,4},{4,5},{5,6},{6,7},{8,9},{9,10},{10,11},{11... | collective-permute-start | bytes 1105928 | tf_op jit(solution)/shard_map/ppermute | solution.py:58
  90.4 20.2 %collective-permute-start.30 = (bf16[3,160,384]{2,1,0:T(8,128)(2,1)S(1)}, bf16[3,160,384]{2,1,0:T(8,128)(2,1)S(1)}, u32[]{:S(2)}, u32[]{:S(2)}) collective-permute-start(bf16[3,160,384]{2,1,0:T(8,128)(2,1)S(1)} %pad_maximum_fusion.1), channel_id=1, source_target_pairs={{1,0},{2,1},{3,2},{4,3},{5,4},{6,5},{7,6},{9,8},{10,9},{11,10},{12... | collective-permute-start | bytes 1105928 | tf_op jit(solution)/shard_map/ppermute | solution.py:62
  91.9 10.8 %collective-permute-start.19 = (f32[2,4,2,128]{3,2,1,0:T(2,128)S(1)}, f32[2,4,2,128]{3,2,1,0:T(2,128)S(1)}, u32[]{:S(2)}, u32[]{:S(2)}) collective-permute-start(f32[2,4,2,128]{3,2,1,0:T(2,128)S(1)} %pad_maximum_fusion.4.refs_0_), channel_id=1, source_target_pairs={{0,2},{1,3},{2,0},{3,1},{4,6},{5,7},{6,4},{7,5},{8,10},{9,11},{10,... | collective-permute-start | bytes 24584 | tf_op jit(solution)/shard_map/ppermute | solution.py:34
  97.3 6.7 %collective-permute-start.20 = (f32[2,4,2,128]{3,2,1,0:T(2,128)S(1)}, f32[2,4,2,128]{3,2,1,0:T(2,128)S(1)}, u32[]{:S(2)}, u32[]{:S(2)}) collective-permute-start(f32[2,4,2,128]{3,2,1,0:T(2,128)S(1)} %pad_maximum_fusion.4.refs_0_), channel_id=1, source_target_pairs={{0,4},{1,5},{2,6},{3,7},{4,0},{5,1},{6,2},{7,3},{8,12},{9,13},{10,... | collective-permute-start | bytes 24584 | tf_op jit(solution)/shard_map/ppermute | solution.py:34
  98.8 5.4 %collective-permute-start.21 = (f32[2,4,2,128]{3,2,1,0:T(2,128)S(1)}, f32[2,4,2,128]{3,2,1,0:T(2,128)S(1)}, u32[]{:S(2)}, u32[]{:S(2)}) collective-permute-start(f32[2,4,2,128]{3,2,1,0:T(2,128)S(1)} %pad_maximum_fusion.4.refs_0_), channel_id=1, source_target_pairs={{0,6},{1,7},{2,4},{3,5},{4,2},{5,3},{6,0},{7,1},{8,14},{9,15},{10,... | collective-permute-start | bytes 24584 | tf_op jit(solution)/shard_map/ppermute | solution.py:34
  (2 other events, 36.7 us)

commit v3 on v2

--- a/solution.py
+++ b/solution.py
@@ -94,7 +94,8 @@
         terms.append(gains.astype(BF16).astype(F32))
         gains = gains - terms[-1]
     rows = jnp.concatenate(terms + [jnp.zeros((13, gains.shape[1]), F32)], axis=0)
-    out_ref[at:, 0 : gains.shape[1]] = rows.astype(BF16)
+    lane = taps % GROUP * channels
+    out_ref[at:, lane : lane + gains.shape[1]] = rows.astype(BF16)
 
 
 def near_body(*refs):
@@ -355,6 +356,7 @@
 
 def gain_of(refs, n, channels):
     at = refs[0].shape[0] - 16
+    n += 27 % GROUP
     lanes = slice(n * channels, (n + 1) * channels)
     terms = [ref[at : at + 16, lanes].astype(F32) for ref in refs]
     return jnp.concatenate([(t[0:1] + t[1:2]) + t[2:3] for t in terms], axis=1)
@@ -488,7 +490,7 @@
     others = range(1, sources)
 
     taps = 27 * lc
-    height = lc + -(-27 // GROUP) * lc + 16
+    height = lc + -(-27 // GROUP) * lc
     message = call(
         message_body,
         shaped((height, frames * columns), BF16),

time: 113 us -> 112 us (level)
  transfers between devices with their start and end apart: 31 -> 31, of which waited for: 9 -> 10; matrix products, arithmetic and copies ran while one was open for 1% -> 1% of each run, Pallas kernels for 20% -> 20%
where the time goes in v3:
time: 112 us
  starting transfers between devices  47.7 us (43%)
  Pallas kernels  31.9 us (28%)
  waiting for transfers between devices  31.1 us (28%)
    ppermute x27, starting transfers between devices, xor_send(): lax.ppermute(x, axis, [(i, i ^ mask) for i in range(lax.axis_size(axis))])  41.1 us
    ppermute x27, waiting for transfers between devices, xor_send(): lax.ppermute(x, axis, [(i, i ^ mask) for i in range(lax.axis_size(axis))])  30.4 us
    pallas_call x1, Pallas kernels, window(): call(functools.partial(last_body, len(stats), count), (shaped((frames, sp...  6.42 us
    pallas_call x1, Pallas kernels, window(): call(functools.partial(middle_body, len(stats), count), (shaped((frames,...  5.85 us
    pallas_call x2, Pallas kernels, cached(): call(cached_body, shaped((2, spots, 128), F32), flops=flops, scratch=[plt...  5.72 us
    pallas_call x1, Pallas kernels, window(): call(first_body, (shaped((frames, rows, columns, wide), BF16), shaped((2,...  4.47 us
    pallas_call x2, Pallas kernels, turn(): call(weights_body, (shape, shape), scratch=[pltpu.VMEM((3, wide, 128), BF...  4.14 us
    ppermute x2, starting transfers between devices, to_next(): lax.ppermute(x, 'tile', [(i, i + 1) for i in range(lax.axis_size('tile')...  3.73 us
  transfers between devices with their start and end apart: 31, of which 10 were waited for; matrix products, arithmetic and copies ran while one was open for 1% of the time, Pallas kernels for 20%

profile of v3, /device:TPU:0, one launch (start us, length us, event | category | flops | bytes accessed | tf_op | source)
XLA Modules:
  0.0 112.3 jit_solution(4760687028692664350)
XLA Ops:
  1.2 3.0 %collective-permute-start = (bf16[112,480]{1,0:T(8,128)(2,1)S(1)}, bf16[112,480]{1,0:T(8,128)(2,1)S(1)}, u32[]{:S(2)}, u32[]{:S(2)}) collective-permute-start(bf16[112,480]{1,0:T(8,128)(2,1)S(1)} %shard_map.100.refs_0_.m0.refs_2_.refs_4_), channel_id=1, source_target_pairs={{0,8},{8,0},{16,24},{24,16},{1,9},{9,1},{17,25},{25,17},{2,10},{10... | collective-permute-start | bytes 322568 | tf_op jit(solution)/shard_map/ppermute | solution.py:34
  4.2 1.5 %collective-permute-start.1 = (bf16[112,480]{1,0:T(8,128)(2,1)S(1)}, bf16[112,480]{1,0:T(8,128)(2,1)S(1)}, u32[]{:S(2)}, u32[]{:S(2)}) collective-permute-start(bf16[112,480]{1,0:T(8,128)(2,1)S(1)} %shard_map.100.refs_0_.m0.refs_2_.refs_4_), channel_id=1, source_target_pairs={{0,16},{8,24},{16,0},{24,8},{1,17},{9,25},{17,1},{25,9},{2,18},{10... | collective-permute-start | bytes 322568 | tf_op jit(solution)/shard_map/ppermute | solution.py:34
  5.7 2.0 %collective-permute-done.refs_1_.m1.refs_3_.refs_5_ = bf16[112,480]{1,0:T(8,128)(2,1)S(1)} collective-permute-done((bf16[112,480]{1,0:T(8,128)(2,1)S(1)}, bf16[112,480]{1,0:T(8,128)(2,1)S(1)}, u32[]{:S(2)}, u32[]{:S(2)}) %collective-permute-start) | collective-permute-done | bytes 107552 | tf_op jit(solution)/shard_map/ppermute | solution.py:34
  7.7 3.7 %collective-permute-done.1.refs_2_.m2.refs_4_.refs_6_ = bf16[112,480]{1,0:T(8,128)(2,1)S(1)} collective-permute-done((bf16[112,480]{1,0:T(8,128)(2,1)S(1)}, bf16[112,480]{1,0:T(8,128)(2,1)S(1)}, u32[]{:S(2)}, u32[]{:S(2)}) %collective-permute-start.1) | collective-permute-done | bytes 107552 | tf_op jit(solution)/shard_map/ppermute | solution.py:34
  11.4 3.7 %collective-permute-start.5 = (bf16[4,16,480]{2,1,0:T(8,128)(2,1)S(1)}, bf16[4,16,480]{2,1,0:T(8,128)(2,1)S(1)}, u32[]{:S(2)}, u32[]{:S(2)}) collective-permute-start(bf16[4,16,480]{2,1,0:T(8,128)(2,1)S(1)} %shard_map.101), channel_id=1, source_target_pairs={{0,6},{1,7},{2,4},{3,5},{4,2},{5,3},{6,0},{7,1},{8,14},{9,15},{10,... | collective-permute-start | bytes 184328 | tf_op jit(solution)/shard_map/ppermute | solution.py:34
  15.9 1.5 %shard_map.102 = (bf16[3,160,384]{2,1,0:T(8,128)(2,1)S(1)}, bf16[3,160,384]{2,1,0:T(8,128)(2,1)S(1)}, bf16[4,16,320]{2,1,0:T(8,128)(2,1)S(1)}, bf16[192,384]{1,0:T(8,128)(2,1)S(1)}, bf16[192,384]{1,0:T(8,128)(2,1)S(1)}) custom-call(bf16[2,4,160,96]{3,2,1,0:T(8,128)(2,1)} %bitcast.19, bf16[2,4,160,96]{3,2,1,0:T(8,128)(2,1)} %bitcast.20, ...), custom_call_target="tpu_custom_call" | custom-call | bytes 1048576 | tf_op jit(solution)/shard_map/pallas_call | solution.py:515
  17.4 1.3 %collective-permute-start.7 = (bf16[192,384]{1,0:T(8,128)(2,1)S(1)}, bf16[192,384]{1,0:T(8,128)(2,1)S(1)}, u32[]{:S(2)}, u32[]{:S(2)}) collective-permute-start(bf16[192,384]{1,0:T(8,128)(2,1)S(1)} %get-tuple-element.22), channel_id=1, source_target_pairs={{0,1},{1,2},{2,3},{3,4},{4,5},{5,6},{6,7},{8,9},{9,10},{10,11},{11... | collective-permute-start | bytes 442376 | tf_op jit(solution)/shard_map/ppermute | solution.py:58
  18.7 1.3 %collective-permute-start.8 = (bf16[192,384]{1,0:T(8,128)(2,1)S(1)}, bf16[192,384]{1,0:T(8,128)(2,1)S(1)}, u32[]{:S(2)}, u32[]{:S(2)}) collective-permute-start(bf16[192,384]{1,0:T(8,128)(2,1)S(1)} %get-tuple-element.24), channel_id=1, source_target_pairs={{1,0},{2,1},{3,2},{4,3},{5,4},{6,5},{7,6},{9,8},{10,9},{11,10},{12... | collective-permute-start | bytes 442376 | tf_op jit(solution)/shard_map/ppermute | solution.py:62
  20.3 2.5 %collective-permute-start.6 = (bf16[16,16,480]{2,1,0:T(8,128)(2,1)S(1)}, bf16[16,16,480]{2,1,0:T(8,128)(2,1)S(1)}, u32[]{:S(2)}, u32[]{:S(2)}) collective-permute-start(bf16[16,16,480]{2,1,0:T(8,128)(2,1)S(1)} %pad_maximum_fusion.2.near_ref), channel_id=1, source_target_pairs={{0,1},{1,0},{2,3},{3,2},{4,5},{5,4},{6,7},{7,6},{8,9},{9,8},{10,11... | collective-permute-start | bytes 737288 | tf_op jit(solution)/shard_map/ppermute | solution.py:34
  26.1 1.6 %collective-permute-start.14 = (bf16[3,160,384]{2,1,0:T(8,128)(2,1)S(1)}, bf16[3,160,384]{2,1,0:T(8,128)(2,1)S(1)}, u32[]{:S(2)}, u32[]{:S(2)}) collective-permute-start(bf16[3,160,384]{2,1,0:T(8,128)(2,1)S(1)} %get-tuple-element.29.p0), channel_id=1, source_target_pairs={{0,24},{8,16},{16,8},{24,0},{1,25},{9,17},{17,9},{25,1},{2,26},{10... | collective-permute-start | bytes 1105928 | tf_op jit(solution)/shard_map/ppermute | solution.py:34
  27.6 4.5 %shard_map.103 = (bf16[3,6,160,384]{3,2,1,0:T(8,128)(2,1)S(1)}, f32[2,384]{1,0:T(2,128)S(1)}) custom-call(s32[32]{0:T(128)S(1)} %copy-done.2, bf16[16,16,480]{2,1,0:T(8,128)(2,1)S(1)} %pad_maximum_fusion.2.near_ref, bf16[16,16,480]{2,1,0:T(8,128)(2,1)S(1)} %collective-permute-done.6.far_ref, bf16[192,384]{1,0:T(8,128)(2,1)S(1)} %collective-permute-done.7.before, ...), custom_call_target="tpu_custom_call" | custom-call | flops 318504960 | bytes 1048576 | tf_op jit(solution)/shard_map/pallas_call | solution.py:557
  32.1 2.9 %collective-permute-start.9 = (f32[2,384]{1,0:T(2,128)S(1)}, f32[2,384]{1,0:T(2,128)S(1)}, u32[]{:S(2)}, u32[]{:S(2)}) collective-permute-start(f32[2,384]{1,0:T(2,128)S(1)} %get-tuple-element.25), channel_id=1, source_target_pairs={{0,1},{1,0},{2,3},{3,2},{4,5},{5,4},{6,7},{7,6},{8,9},{9,8},{10,11... | collective-permute-start | bytes 9224 | tf_op jit(solution)/shard_map/ppermute | solution.py:34
  35.9 1.5 %collective-permute-start.10 = (f32[2,2,384]{2,1,0:T(2,128)S(1)}, f32[2,2,384]{2,1,0:T(2,128)S(1)}, u32[]{:S(2)}, u32[]{:S(2)}) collective-permute-start(f32[2,2,384]{2,1,0:T(2,128)S(1)} %pad_maximum_fusion.5), channel_id=1, source_target_pairs={{0,2},{1,3},{2,0},{3,1},{4,6},{5,7},{6,4},{7,5},{8,10},{9,11},{10,... | collective-permute-start | bytes 18440 | tf_op jit(solution)/shard_map/ppermute | solution.py:34
  37.3 2.0 %shard_map.105 = (bf16[9,384,256]{2,1,0:T(8,128)(2,1)S(1)}, bf16[9,384,256]{2,1,0:T(8,128)(2,1)S(1)}) custom-call(bf16[3,3,3,96,384]{4,3,2,1,0:T(8,128)(2,1)S(1)} %copy-done), custom_call_target="tpu_custom_call" | custom-call | bytes 1048576 | tf_op jit(solution)/shard_map/pallas_call | solution.py:536
  39.3 2.2 %shard_map.108 = (bf16[9,384,256]{2,1,0:T(8,128)(2,1)S(1)}, bf16[9,384,256]{2,1,0:T(8,128)(2,1)S(1)}) custom-call(bf16[3,3,3,96,384]{4,3,2,1,0:T(8,128)(2,1)S(1)} %copy-done.1), custom_call_target="tpu_custom_call" | custom-call | bytes 1048576 | tf_op jit(solution)/shard_map/pallas_call | solution.py:536
  41.5 2.4 %collective-permute-start.11 = (f32[4,2,384]{2,1,0:T(2,128)S(1)}, f32[4,2,384]{2,1,0:T(2,128)S(1)}, u32[]{:S(2)}, u32[]{:S(2)}) collective-permute-start(f32[4,2,384]{2,1,0:T(2,128)S(1)} %pad_maximum_fusion.3.refs_0_), channel_id=1, source_target_pairs={{0,4},{1,5},{2,6},{3,7},{4,0},{5,1},{6,2},{7,3},{8,12},{9,13},{10,... | collective-permute-start | bytes 36872 | tf_op jit(solution)/shard_map/ppermute | solution.py:34
  44.0 2.9 %shard_map.106.refs_7_ = f32[2,640,128]{2,1,0:T(8,128)S(1)} custom-call(bf16[3,160,384]{2,1,0:T(8,128)(2,1)S(1)} %get-tuple-element.29.p0, bf16[3,160,384]{2,1,0:T(8,128)(2,1)S(1)} %collective-permute-done.12.p1, bf16[3,160,384]{2,1,0:T(8,128)(2,1)S(1)} %collective-permute-done.13.p2, bf16[3,160,384]{2,1,0:T(8,128)(2,1)S(1)} %collective-permute-done.14.p3, ...), custom_call_target="tpu_custom_call" | custom-call | flops 1274019840 | bytes 1048576 | tf_op jit(solution)/shard_map/pallas_call | solution.py:546
  46.9 5.8 %shard_map.107 = (bf16[3,160,384]{2,1,0:T(8,128)(2,1)S(1)}, f32[2,128]{1,0:T(2,128)S(1)}) custom-call(f32[4,2,384]{2,1,0:T(2,128)S(1)} %pad_maximum_fusion.3.refs_0_, f32[4,2,384]{2,1,0:T(2,128)S(1)} %collective-permute-done.11.refs_1_, bf16[112,480]{1,0:T(8,128)(2,1)S(1)} %shard_map.100.refs_0_.m0.refs_2_.refs_4_, ...), custom_call_target="tpu_custom_call" | custom-call | flops 2548039680 | bytes 1048576 | tf_op jit(solution)/shard_map/pallas_call | solution.py:578
  52.7 1.6 %collective-permute-start.17 = (f32[2,128]{1,0:T(2,128)S(1)}, f32[2,128]{1,0:T(2,128)S(1)}, u32[]{:S(2)}, u32[]{:S(2)}) collective-permute-start(f32[2,128]{1,0:T(2,128)S(1)} %get-tuple-element.32), channel_id=1, source_target_pairs={{0,24},{8,16},{16,8},{24,0},{1,25},{9,17},{17,9},{25,1},{2,26},{10... | collective-permute-start | bytes 3080 | tf_op jit(solution)/shard_map/ppermute | solution.py:34
  58.5 1.3 %collective-permute-start.26 = (bf16[3,160,384]{2,1,0:T(8,128)(2,1)S(1)}, bf16[3,160,384]{2,1,0:T(8,128)(2,1)S(1)}, u32[]{:S(2)}, u32[]{:S(2)}) collective-permute-start(bf16[3,160,384]{2,1,0:T(8,128)(2,1)S(1)} %get-tuple-element.34.p0), channel_id=1, source_target_pairs={{0,8},{8,0},{16,24},{24,16},{1,9},{9,1},{17,25},{25,17},{2,10},{10... | collective-permute-start | bytes 1105928 | tf_op jit(solution)/shard_map/ppermute | solution.py:34
  60.5 1.6 %collective-permute-start.28 = (bf16[3,160,384]{2,1,0:T(8,128)(2,1)S(1)}, bf16[3,160,384]{2,1,0:T(8,128)(2,1)S(1)}, u32[]{:S(2)}, u32[]{:S(2)}) collective-permute-start(bf16[3,160,384]{2,1,0:T(8,128)(2,1)S(1)} %get-tuple-element.34.p0), channel_id=1, source_target_pairs={{0,24},{8,16},{16,8},{24,0},{1,25},{9,17},{17,9},{25,1},{2,26},{10... | collective-permute-start | bytes 1105928 | tf_op jit(solution)/shard_map/ppermute | solution.py:34
  62.1 5.6 %collective-permute-done.22.refs_9_ = bf16[3,160,384]{2,1,0:T(8,128)(2,1)S(1)} collective-permute-done((bf16[3,160,384]{2,1,0:T(8,128)(2,1)S(1)}, bf16[3,160,384]{2,1,0:T(8,128)(2,1)S(1)}, u32[]{:S(2)}, u32[]{:S(2)}) %collective-permute-start.22) | collective-permute-done | bytes 368672 | tf_op jit(solution)/shard_map/ppermute | solution.py:34
  67.8 1.4 %collective-permute-start.24 = (bf16[3,80,384]{2,1,0:T(8,128)(2,1)S(1)}, bf16[3,80,384]{2,1,0:T(8,128)(2,1)S(1)}, u32[]{:S(2)}, u32[]{:S(2)}) collective-permute-start(bf16[3,80,384]{2,1,0:T(8,128)(2,1)S(1)} %slice.40), channel_id=1, source_target_pairs={{0,16},{8,24},{16,0},{24,8},{1,17},{9,25},{17,1},{25,9},{2,18},{10... | collective-permute-start | bytes 552968 | tf_op jit(solution)/shard_map/ppermute | solution.py:34
  70.3 16.5 %collective-permute-done.24.refs_11_ = bf16[3,80,384]{2,1,0:T(8,128)(2,1)S(1)} collective-permute-done((bf16[3,80,384]{2,1,0:T(8,128)(2,1)S(1)}, bf16[3,80,384]{2,1,0:T(8,128)(2,1)S(1)}, u32[]{:S(2)}, u32[]{:S(2)}) %collective-permute-start.24) | collective-permute-done | bytes 184352 | tf_op jit(solution)/shard_map/ppermute | solution.py:34
  87.2 2.4 %collective-permute-start.29 = (bf16[3,160,384]{2,1,0:T(8,128)(2,1)S(1)}, bf16[3,160,384]{2,1,0:T(8,128)(2,1)S(1)}, u32[]{:S(2)}, u32[]{:S(2)}) collective-permute-start(bf16[3,160,384]{2,1,0:T(8,128)(2,1)S(1)} %pad_maximum_fusion), channel_id=1, source_target_pairs={{0,1},{1,2},{2,3},{3,4},{4,5},{5,6},{6,7},{8,9},{9,10},{10,11},{11... | collective-permute-start | bytes 1105928 | tf_op jit(solution)/shard_map/ppermute | solution.py:58
  89.9 1.5 %collective-permute-start.30 = (bf16[3,160,384]{2,1,0:T(8,128)(2,1)S(1)}, bf16[3,160,384]{2,1,0:T(8,128)(2,1)S(1)}, u32[]{:S(2)}, u32[]{:S(2)}) collective-permute-start(bf16[3,160,384]{2,1,0:T(8,128)(2,1)S(1)} %pad_maximum_fusion.1), channel_id=1, source_target_pairs={{1,0},{2,1},{3,2},{4,3},{5,4},{6,5},{7,6},{9,8},{10,9},{11,10},{12... | collective-permute-start | bytes 1105928 | tf_op jit(solution)/shard_map/ppermute | solution.py:62
  91.5 5.3 %collective-permute-start.19 = (f32[2,4,2,128]{3,2,1,0:T(2,128)S(1)}, f32[2,4,2,128]{3,2,1,0:T(2,128)S(1)}, u32[]{:S(2)}, u32[]{:S(2)}) collective-permute-start(f32[2,4,2,128]{3,2,1,0:T(2,128)S(1)} %pad_maximum_fusion.4.refs_0_), channel_id=1, source_target_pairs={{0,2},{1,3},{2,0},{3,1},{4,6},{5,7},{6,4},{7,5},{8,10},{9,11},{10,... | collective-permute-start | bytes 24584 | tf_op jit(solution)/shard_map/ppermute | solution.py:34
  96.8 1.3 %collective-permute-start.20 = (f32[2,4,2,128]{3,2,1,0:T(2,128)S(1)}, f32[2,4,2,128]{3,2,1,0:T(2,128)S(1)}, u32[]{:S(2)}, u32[]{:S(2)}) collective-permute-start(f32[2,4,2,128]{3,2,1,0:T(2,128)S(1)} %pad_maximum_fusion.4.refs_0_), channel_id=1, source_target_pairs={{0,4},{1,5},{2,6},{3,7},{4,0},{5,1},{6,2},{7,3},{8,12},{9,13},{10,... | collective-permute-start | bytes 24584 | tf_op jit(solution)/shard_map/ppermute | solution.py:34
  99.3 2.9 %shard_map.109.refs_13_ = f32[2,640,128]{2,1,0:T(8,128)S(1)} custom-call(bf16[3,160,384]{2,1,0:T(8,128)(2,1)S(1)} %get-tuple-element.34.p0, bf16[3,160,384]{2,1,0:T(8,128)(2,1)S(1)} %collective-permute-done.26.p1, bf16[3,160,384]{2,1,0:T(8,128)(2,1)S(1)} %collective-permute-done.27.p2, bf16[3,160,384]{2,1,0:T(8,128)(2,1)S(1)} %collective-permute-done.28.p3, ...), custom_call_target="tpu_custom_call" | custom-call | flops 1274019840 | bytes 1048576 | tf_op jit(solution)/shard_map/pallas_call | solution.py:546
  102.2 1.2 %collective-permute-done.20.refs_2_ = f32[2,4,2,128]{3,2,1,0:T(2,128)S(1)} collective-permute-done((f32[2,4,2,128]{3,2,1,0:T(2,128)S(1)}, f32[2,4,2,128]{3,2,1,0:T(2,128)S(1)}, u32[]{:S(2)}, u32[]{:S(2)}) %collective-permute-start.20) | collective-permute-done | bytes 8224 | tf_op jit(solution)/shard_map/ppermute | solution.py:34
  103.6 6.4 %shard_map.110 = (f32[3,640,128]{2,1,0:T(8,128)S(1)}, f32[2,384]{1,0:T(2,128)S(1)}) custom-call(f32[2,4,2,128]{3,2,1,0:T(2,128)S(1)} %pad_maximum_fusion.4.refs_0_, f32[2,4,2,128]{3,2,1,0:T(2,128)S(1)} %collective-permute-done.19.refs_1_, f32[2,4,2,128]{3,2,1,0:T(2,128)S(1)} %collective-permute-done.20.refs_2_, ...), custom_call_target="tpu_custom_call" | custom-call | flops 2548039680 | bytes 1048576 | tf_op jit(solution)/shard_map/pallas_call | solution.py:594
  110.0 2.1 %shard_map.111 = bf16[3,4,160,96]{3,2,1,0:T(8,128)(2,1)} custom-call(f32[3,640,128]{2,1,0:T(8,128)S(1)} %get-tuple-element.37.part_ref, f32[2,384]{1,0:T(2,128)S(1)} %get-tuple-element.38.scale_ref, bf16[3,160,384]{2,1,0:T(8,128)(2,1)S(1)} %collective-permute-done.29.up, bf16[3,160,384]{2,1,0:T(8,128)(2,1)S(1)} %collective-permute-done.30.down, ...), custom_call_target="tpu_custom_call" | custom-call | flops 637009920 | bytes 1048576 | tf_op jit(solution)/shard_map/pallas_call | solution.py:601
  (64 shorter events, 14.4 us)
Async XLA Ops:
  0.0 27.6 %copy-start.2 = (s32[32]{0:T(128)S(1)}, s32[32]{0:T(128)}, u32[]{:S(2)}) copy-start(s32[32]{0:T(128)} %map_ref.1) | copy-start | bytes 388
  1.2 6.6 %collective-permute-start = (bf16[112,480]{1,0:T(8,128)(2,1)S(1)}, bf16[112,480]{1,0:T(8,128)(2,1)S(1)}, u32[]{:S(2)}, u32[]{:S(2)}) collective-permute-start(bf16[112,480]{1,0:T(8,128)(2,1)S(1)} %shard_map.100.refs_0_.m0.refs_2_.refs_4_), channel_id=1, source_target_pairs={{0,8},{8,0},{16,24},{24,16},{1,9},{9,1},{17,25},{25,17},{2,10},{10... | collective-permute-start | bytes 322568 | tf_op jit(solution)/shard_map/ppermute | solution.py:34
  4.2 7.2 %collective-permute-start.1 = (bf16[112,480]{1,0:T(8,128)(2,1)S(1)}, bf16[112,480]{1,0:T(8,128)(2,1)S(1)}, u32[]{:S(2)}, u32[]{:S(2)}) collective-permute-start(bf16[112,480]{1,0:T(8,128)(2,1)S(1)} %shard_map.100.refs_0_.m0.refs_2_.refs_4_), channel_id=1, source_target_pairs={{0,16},{8,24},{16,0},{24,8},{1,17},{9,25},{17,1},{25,9},{2,18},{10... | collective-permute-start | bytes 322568 | tf_op jit(solution)/shard_map/ppermute | solution.py:34
  5.7 5.7 %collective-permute-start.2 = (bf16[112,480]{1,0:T(8,128)(2,1)S(1)}, bf16[112,480]{1,0:T(8,128)(2,1)S(1)}, u32[]{:S(2)}, u32[]{:S(2)}) collective-permute-start(bf16[112,480]{1,0:T(8,128)(2,1)S(1)} %shard_map.100.refs_0_.m0.refs_2_.refs_4_), channel_id=1, source_target_pairs={{0,24},{8,16},{16,8},{24,0},{1,25},{9,17},{17,9},{25,1},{2,26},{10... | collective-permute-start | bytes 322568 | tf_op jit(solution)/shard_map/ppermute | solution.py:34
  11.4 8.6 %collective-permute-start.5 = (bf16[4,16,480]{2,1,0:T(8,128)(2,1)S(1)}, bf16[4,16,480]{2,1,0:T(8,128)(2,1)S(1)}, u32[]{:S(2)}, u32[]{:S(2)}) collective-permute-start(bf16[4,16,480]{2,1,0:T(8,128)(2,1)S(1)} %shard_map.101), channel_id=1, source_target_pairs={{0,6},{1,7},{2,4},{3,5},{4,2},{5,3},{6,0},{7,1},{8,14},{9,15},{10,... | collective-permute-start | bytes 184328 | tf_op jit(solution)/shard_map/ppermute | solution.py:34
  15.1 5.2 %collective-permute-start.4 = (bf16[4,16,480]{2,1,0:T(8,128)(2,1)S(1)}, bf16[4,16,480]{2,1,0:T(8,128)(2,1)S(1)}, u32[]{:S(2)}, u32[]{:S(2)}) collective-permute-start(bf16[4,16,480]{2,1,0:T(8,128)(2,1)S(1)} %shard_map.101), channel_id=1, source_target_pairs={{0,4},{1,5},{2,6},{3,7},{4,0},{5,1},{6,2},{7,3},{8,12},{9,13},{10,... | collective-permute-start | bytes 184328 | tf_op jit(solution)/shard_map/ppermute | solution.py:34
  15.1 5.2 %collective-permute-start.3 = (bf16[4,16,480]{2,1,0:T(8,128)(2,1)S(1)}, bf16[4,16,480]{2,1,0:T(8,128)(2,1)S(1)}, u32[]{:S(2)}, u32[]{:S(2)}) collective-permute-start(bf16[4,16,480]{2,1,0:T(8,128)(2,1)S(1)} %shard_map.101), channel_id=1, source_target_pairs={{0,2},{1,3},{2,0},{3,1},{4,6},{5,7},{6,4},{7,5},{8,10},{9,11},{10,... | collective-permute-start | bytes 184328 | tf_op jit(solution)/shard_map/ppermute | solution.py:34
  17.4 5.4 %collective-permute-start.7 = (bf16[192,384]{1,0:T(8,128)(2,1)S(1)}, bf16[192,384]{1,0:T(8,128)(2,1)S(1)}, u32[]{:S(2)}, u32[]{:S(2)}) collective-permute-start(bf16[192,384]{1,0:T(8,128)(2,1)S(1)} %get-tuple-element.22), channel_id=1, source_target_pairs={{0,1},{1,2},{2,3},{3,4},{4,5},{5,6},{6,7},{8,9},{9,10},{10,11},{11... | collective-permute-start | bytes 442376 | tf_op jit(solution)/shard_map/ppermute | solution.py:58
  18.7 4.7 %collective-permute-start.8 = (bf16[192,384]{1,0:T(8,128)(2,1)S(1)}, bf16[192,384]{1,0:T(8,128)(2,1)S(1)}, u32[]{:S(2)}, u32[]{:S(2)}) collective-permute-start(bf16[192,384]{1,0:T(8,128)(2,1)S(1)} %get-tuple-element.24), channel_id=1, source_target_pairs={{1,0},{2,1},{3,2},{4,3},{5,4},{6,5},{7,6},{9,8},{10,9},{11,10},{12... | collective-permute-start | bytes 442376 | tf_op jit(solution)/shard_map/ppermute | solution.py:62
  20.3 7.3 %collective-permute-start.6 = (bf16[16,16,480]{2,1,0:T(8,128)(2,1)S(1)}, bf16[16,16,480]{2,1,0:T(8,128)(2,1)S(1)}, u32[]{:S(2)}, u32[]{:S(2)}) collective-permute-start(bf16[16,16,480]{2,1,0:T(8,128)(2,1)S(1)} %pad_maximum_fusion.2.near_ref), channel_id=1, source_target_pairs={{0,1},{1,0},{2,3},{3,2},{4,5},{5,4},{6,7},{7,6},{8,9},{9,8},{10,11... | collective-permute-start | bytes 737288 | tf_op jit(solution)/shard_map/ppermute | solution.py:34
  24.1 19.9 %collective-permute-start.12 = (bf16[3,160,384]{2,1,0:T(8,128)(2,1)S(1)}, bf16[3,160,384]{2,1,0:T(8,128)(2,1)S(1)}, u32[]{:S(2)}, u32[]{:S(2)}) collective-permute-start(bf16[3,160,384]{2,1,0:T(8,128)(2,1)S(1)} %get-tuple-element.29.p0), channel_id=1, source_target_pairs={{0,8},{8,0},{16,24},{24,16},{1,9},{9,1},{17,25},{25,17},{2,10},{10... | collective-permute-start | bytes 1105928 | tf_op jit(solution)/shard_map/ppermute | solution.py:34
  25.1 18.9 %collective-permute-start.13 = (bf16[3,160,384]{2,1,0:T(8,128)(2,1)S(1)}, bf16[3,160,384]{2,1,0:T(8,128)(2,1)S(1)}, u32[]{:S(2)}, u32[]{:S(2)}) collective-permute-start(bf16[3,160,384]{2,1,0:T(8,128)(2,1)S(1)} %get-tuple-element.29.p0), channel_id=1, source_target_pairs={{0,16},{8,24},{16,0},{24,8},{1,17},{9,25},{17,1},{25,9},{2,18},{10... | collective-permute-start | bytes 1105928 | tf_op jit(solution)/shard_map/ppermute | solution.py:34
  26.1 17.9 %collective-permute-start.14 = (bf16[3,160,384]{2,1,0:T(8,128)(2,1)S(1)}, bf16[3,160,384]{2,1,0:T(8,128)(2,1)S(1)}, u32[]{:S(2)}, u32[]{:S(2)}) collective-permute-start(bf16[3,160,384]{2,1,0:T(8,128)(2,1)S(1)} %get-tuple-element.29.p0), channel_id=1, source_target_pairs={{0,24},{8,16},{16,8},{24,0},{1,25},{9,17},{17,9},{25,1},{2,26},{10... | collective-permute-start | bytes 1105928 | tf_op jit(solution)/shard_map/ppermute | solution.py:34
  32.1 3.7 %collective-permute-start.9 = (f32[2,384]{1,0:T(2,128)S(1)}, f32[2,384]{1,0:T(2,128)S(1)}, u32[]{:S(2)}, u32[]{:S(2)}) collective-permute-start(f32[2,384]{1,0:T(2,128)S(1)} %get-tuple-element.25), channel_id=1, source_target_pairs={{0,1},{1,0},{2,3},{3,2},{4,5},{5,4},{6,7},{7,6},{8,9},{9,8},{10,11... | collective-permute-start | bytes 9224 | tf_op jit(solution)/shard_map/ppermute | solution.py:34
  35.9 5.6 %collective-permute-start.10 = (f32[2,2,384]{2,1,0:T(2,128)S(1)}, f32[2,2,384]{2,1,0:T(2,128)S(1)}, u32[]{:S(2)}, u32[]{:S(2)}) collective-permute-start(f32[2,2,384]{2,1,0:T(2,128)S(1)} %pad_maximum_fusion.5), channel_id=1, source_target_pairs={{0,2},{1,3},{2,0},{3,1},{4,6},{5,7},{6,4},{7,5},{8,10},{9,11},{10,... | collective-permute-start | bytes 18440 | tf_op jit(solution)/shard_map/ppermute | solution.py:34
  41.5 5.3 %collective-permute-start.11 = (f32[4,2,384]{2,1,0:T(2,128)S(1)}, f32[4,2,384]{2,1,0:T(2,128)S(1)}, u32[]{:S(2)}, u32[]{:S(2)}) collective-permute-start(f32[4,2,384]{2,1,0:T(2,128)S(1)} %pad_maximum_fusion.3.refs_0_), channel_id=1, source_target_pairs={{0,4},{1,5},{2,6},{3,7},{4,0},{5,1},{6,2},{7,3},{8,12},{9,13},{10,... | collective-permute-start | bytes 36872 | tf_op jit(solution)/shard_map/ppermute | solution.py:34
  52.7 5.8 %collective-permute-start.17 = (f32[2,128]{1,0:T(2,128)S(1)}, f32[2,128]{1,0:T(2,128)S(1)}, u32[]{:S(2)}, u32[]{:S(2)}) collective-permute-start(f32[2,128]{1,0:T(2,128)S(1)} %get-tuple-element.32), channel_id=1, source_target_pairs={{0,24},{8,16},{16,8},{24,0},{1,25},{9,17},{17,9},{25,1},{2,26},{10... | collective-permute-start | bytes 3080 | tf_op jit(solution)/shard_map/ppermute | solution.py:34
  54.4 5.5 %collective-permute-start.16 = (f32[2,128]{1,0:T(2,128)S(1)}, f32[2,128]{1,0:T(2,128)S(1)}, u32[]{:S(2)}, u32[]{:S(2)}) collective-permute-start(f32[2,128]{1,0:T(2,128)S(1)} %get-tuple-element.32), channel_id=1, source_target_pairs={{0,16},{8,24},{16,0},{24,8},{1,17},{9,25},{17,1},{25,9},{2,18},{10... | collective-permute-start | bytes 3080 | tf_op jit(solution)/shard_map/ppermute | solution.py:34
  55.3 5.3 %collective-permute-start.15 = (f32[2,128]{1,0:T(2,128)S(1)}, f32[2,128]{1,0:T(2,128)S(1)}, u32[]{:S(2)}, u32[]{:S(2)}) collective-permute-start(f32[2,128]{1,0:T(2,128)S(1)} %get-tuple-element.32), channel_id=1, source_target_pairs={{0,8},{8,0},{16,24},{24,16},{1,9},{9,1},{17,25},{25,17},{2,10},{10... | collective-permute-start | bytes 3080 | tf_op jit(solution)/shard_map/ppermute | solution.py:34
  56.3 11.5 %collective-permute-start.22 = (bf16[3,160,384]{2,1,0:T(8,128)(2,1)S(1)}, bf16[3,160,384]{2,1,0:T(8,128)(2,1)S(1)}, u32[]{:S(2)}, u32[]{:S(2)}) collective-permute-start(bf16[3,160,384]{2,1,0:T(8,128)(2,1)S(1)} %get-tuple-element.33.refs_8_), channel_id=1, source_target_pairs={{0,8},{8,0},{16,24},{24,16},{1,9},{9,1},{17,25},{25,17},{2,10},{10... | collective-permute-start | bytes 1105928 | tf_op jit(solution)/shard_map/ppermute | solution.py:34
  57.3 11.9 %collective-permute-start.23 = (bf16[3,160,384]{2,1,0:T(8,128)(2,1)S(1)}, bf16[3,160,384]{2,1,0:T(8,128)(2,1)S(1)}, u32[]{:S(2)}, u32[]{:S(2)}) collective-permute-start(bf16[3,160,384]{2,1,0:T(8,128)(2,1)S(1)} %get-tuple-element.33.refs_8_), channel_id=1, source_target_pairs={{0,16},{8,24},{16,0},{24,8},{1,17},{9,25},{17,1},{25,9},{2,18},{10... | collective-permute-start | bytes 1105928 | tf_op jit(solution)/shard_map/ppermute | solution.py:34
  58.5 32.9 %collective-permute-start.26 = (bf16[3,160,384]{2,1,0:T(8,128)(2,1)S(1)}, bf16[3,160,384]{2,1,0:T(8,128)(2,1)S(1)}, u32[]{:S(2)}, u32[]{:S(2)}) collective-permute-start(bf16[3,160,384]{2,1,0:T(8,128)(2,1)S(1)} %get-tuple-element.34.p0), channel_id=1, source_target_pairs={{0,8},{8,0},{16,24},{24,16},{1,9},{9,1},{17,25},{25,17},{2,10},{10... | collective-permute-start | bytes 1105928 | tf_op jit(solution)/shard_map/ppermute | solution.py:34
  59.8 37.0 %collective-permute-start.27 = (bf16[3,160,384]{2,1,0:T(8,128)(2,1)S(1)}, bf16[3,160,384]{2,1,0:T(8,128)(2,1)S(1)}, u32[]{:S(2)}, u32[]{:S(2)}) collective-permute-start(bf16[3,160,384]{2,1,0:T(8,128)(2,1)S(1)} %get-tuple-element.34.p0), channel_id=1, source_target_pairs={{0,16},{8,24},{16,0},{24,8},{1,17},{9,25},{17,1},{25,9},{2,18},{10... | collective-permute-start | bytes 1105928 | tf_op jit(solution)/shard_map/ppermute | solution.py:34
  60.5 37.6 %collective-permute-start.28 = (bf16[3,160,384]{2,1,0:T(8,128)(2,1)S(1)}, bf16[3,160,384]{2,1,0:T(8,128)(2,1)S(1)}, u32[]{:S(2)}, u32[]{:S(2)}) collective-permute-start(bf16[3,160,384]{2,1,0:T(8,128)(2,1)S(1)} %get-tuple-element.34.p0), channel_id=1, source_target_pairs={{0,24},{8,16},{16,8},{24,0},{1,25},{9,17},{17,9},{25,1},{2,26},{10... | collective-permute-start | bytes 1105928 | tf_op jit(solution)/shard_map/ppermute | solution.py:34
  67.8 19.0 %collective-permute-start.24 = (bf16[3,80,384]{2,1,0:T(8,128)(2,1)S(1)}, bf16[3,80,384]{2,1,0:T(8,128)(2,1)S(1)}, u32[]{:S(2)}, u32[]{:S(2)}) collective-permute-start(bf16[3,80,384]{2,1,0:T(8,128)(2,1)S(1)} %slice.40), channel_id=1, source_target_pairs={{0,16},{8,24},{16,0},{24,8},{1,17},{9,25},{17,1},{25,9},{2,18},{10... | collective-permute-start | bytes 552968 | tf_op jit(solution)/shard_map/ppermute | solution.py:34
  69.2 17.6 %collective-permute-start.25 = (bf16[3,80,384]{2,1,0:T(8,128)(2,1)S(1)}, bf16[3,80,384]{2,1,0:T(8,128)(2,1)S(1)}, u32[]{:S(2)}, u32[]{:S(2)}) collective-permute-start(bf16[3,80,384]{2,1,0:T(8,128)(2,1)S(1)} %slice.41), channel_id=1, source_target_pairs={{0,8},{8,0},{16,24},{24,16},{1,9},{9,1},{17,25},{25,17},{2,10},{10... | collective-permute-start | bytes 552968 | tf_op jit(solution)/shard_map/ppermute | solution.py:34
  86.8 3.1 %collective-permute-start.18 = (f32[4,2,128]{2,1,0:T(2,128)S(1)}, f32[4,2,128]{2,1,0:T(2,128)S(1)}, u32[]{:S(2)}, u32[]{:S(2)}) collective-permute-start(f32[4,2,128]{2,1,0:T(2,128)S(1)} %pad_maximum_fusion.6), channel_id=1, source_target_pairs={{0,1},{1,0},{2,3},{3,2},{4,5},{5,4},{6,7},{7,6},{8,9},{9,8},{10,11... | collective-permute-start | bytes 12296 | tf_op jit(solution)/shard_map/ppermute | solution.py:34
  87.2 22.8 %collective-permute-start.29 = (bf16[3,160,384]{2,1,0:T(8,128)(2,1)S(1)}, bf16[3,160,384]{2,1,0:T(8,128)(2,1)S(1)}, u32[]{:S(2)}, u32[]{:S(2)}) collective-permute-start(bf16[3,160,384]{2,1,0:T(8,128)(2,1)S(1)} %pad_maximum_fusion), channel_id=1, source_target_pairs={{0,1},{1,2},{2,3},{3,4},{4,5},{5,6},{6,7},{8,9},{9,10},{10,11},{11... | collective-permute-start | bytes 1105928 | tf_op jit(solution)/shard_map/ppermute | solution.py:58
  89.9 20.1 %collective-permute-start.30 = (bf16[3,160,384]{2,1,0:T(8,128)(2,1)S(1)}, bf16[3,160,384]{2,1,0:T(8,128)(2,1)S(1)}, u32[]{:S(2)}, u32[]{:S(2)}) collective-permute-start(bf16[3,160,384]{2,1,0:T(8,128)(2,1)S(1)} %pad_maximum_fusion.1), channel_id=1, source_target_pairs={{1,0},{2,1},{3,2},{4,3},{5,4},{6,5},{7,6},{9,8},{10,9},{11,10},{12... | collective-permute-start | bytes 1105928 | tf_op jit(solution)/shard_map/ppermute | solution.py:62
  91.5 10.8 %collective-permute-start.19 = (f32[2,4,2,128]{3,2,1,0:T(2,128)S(1)}, f32[2,4,2,128]{3,2,1,0:T(2,128)S(1)}, u32[]{:S(2)}, u32[]{:S(2)}) collective-permute-start(f32[2,4,2,128]{3,2,1,0:T(2,128)S(1)} %pad_maximum_fusion.4.refs_0_), channel_id=1, source_target_pairs={{0,2},{1,3},{2,0},{3,1},{4,6},{5,7},{6,4},{7,5},{8,10},{9,11},{10,... | collective-permute-start | bytes 24584 | tf_op jit(solution)/shard_map/ppermute | solution.py:34
  96.8 6.6 %collective-permute-start.20 = (f32[2,4,2,128]{3,2,1,0:T(2,128)S(1)}, f32[2,4,2,128]{3,2,1,0:T(2,128)S(1)}, u32[]{:S(2)}, u32[]{:S(2)}) collective-permute-start(f32[2,4,2,128]{3,2,1,0:T(2,128)S(1)} %pad_maximum_fusion.4.refs_0_), channel_id=1, source_target_pairs={{0,4},{1,5},{2,6},{3,7},{4,0},{5,1},{6,2},{7,3},{8,12},{9,13},{10,... | collective-permute-start | bytes 24584 | tf_op jit(solution)/shard_map/ppermute | solution.py:34
  98.1 5.4 %collective-permute-start.21 = (f32[2,4,2,128]{3,2,1,0:T(2,128)S(1)}, f32[2,4,2,128]{3,2,1,0:T(2,128)S(1)}, u32[]{:S(2)}, u32[]{:S(2)}) collective-permute-start(f32[2,4,2,128]{3,2,1,0:T(2,128)S(1)} %pad_maximum_fusion.4.refs_0_), channel_id=1, source_target_pairs={{0,6},{1,7},{2,4},{3,5},{4,2},{5,3},{6,0},{7,1},{8,14},{9,15},{10,... | collective-permute-start | bytes 24584 | tf_op jit(solution)/shard_map/ppermute | solution.py:34
  (2 other events, 36.7 us)

commit v4 on v3

--- a/solution.py
+++ b/solution.py
@@ -255,9 +255,9 @@
 
 def put_row(taps, f, r, v):
     columns, channels = v.shape
-    at = lax.broadcasted_iota(jnp.int32, v.shape, 0)
-    left = jnp.where(at == 0, 0.0, pltpu.roll(v, 1, axis=0))
-    right = jnp.where(at == columns - 1, 0.0, pltpu.roll(v, columns - 1, axis=0))
+    edge = jnp.zeros((1, channels), F32)
+    left = jnp.concatenate([edge, v[: columns - 1]], axis=0)
+    right = jnp.concatenate([v[1:], edge], axis=0)
     taps[f, r, :, 0:channels] = left.astype(BF16)
     taps[f, r, :, channels : 2 * channels] = v.astype(BF16)
     taps[f, r, :, 2 * channels :] = right.astype(BF16)

time: 112 us -> 113 us (level)
  no operation moved by 1% of the time
where the time goes in v4:
time: 113 us; the launch traced here: 112 us
  starting transfers between devices  47.7 us (42%)
  Pallas kernels  32 us (28%)
  waiting for transfers between devices  31.1 us (28%)
    ppermute x27, starting transfers between devices, xor_send(): lax.ppermute(x, axis, [(i, i ^ mask) for i in range(lax.axis_size(axis))])  41.1 us
    ppermute x27, waiting for transfers between devices, xor_send(): lax.ppermute(x, axis, [(i, i ^ mask) for i in range(lax.axis_size(axis))])  30.4 us
    pallas_call x1, Pallas kernels, window(): call(functools.partial(last_body, len(stats), count), (shaped((frames, sp...  6.45 us
    pallas_call x1, Pallas kernels, window(): call(functools.partial(middle_body, len(stats), count), (shaped((frames,...  5.86 us
    pallas_call x2, Pallas kernels, cached(): call(cached_body, shaped((2, spots, 128), F32), flops=flops, scratch=[plt...  5.71 us
    pallas_call x1, Pallas kernels, window(): call(first_body, (shaped((frames, rows, columns, wide), BF16), shaped((2,...  4.47 us
    pallas_call x2, Pallas kernels, turn(): call(weights_body, (shape, shape), scratch=[pltpu.VMEM((3, wide, 128), BF...  4.14 us
    ppermute x2, starting transfers between devices, to_next(): lax.ppermute(x, 'tile', [(i, i + 1) for i in range(lax.axis_size('tile')...  3.73 us
  transfers between devices with their start and end apart: 31, of which 10 were waited for; matrix products, arithmetic and copies ran while one was open for 1% of the time, Pallas kernels for 20%

profile of v4, /device:TPU:0, one launch (start us, length us, event | category | flops | bytes accessed | tf_op | source)
XLA Modules:
  0.0 112.3 jit_solution(15408155328035134415)
XLA Ops:
  1.2 3.0 %collective-permute-start = (bf16[112,480]{1,0:T(8,128)(2,1)S(1)}, bf16[112,480]{1,0:T(8,128)(2,1)S(1)}, u32[]{:S(2)}, u32[]{:S(2)}) collective-permute-start(bf16[112,480]{1,0:T(8,128)(2,1)S(1)} %shard_map.100.refs_0_.m0.refs_2_.refs_4_), channel_id=1, source_target_pairs={{0,8},{8,0},{16,24},{24,16},{1,9},{9,1},{17,25},{25,17},{2,10},{10... | collective-permute-start | bytes 322568 | tf_op jit(solution)/shard_map/ppermute | solution.py:34
  4.2 1.5 %collective-permute-start.1 = (bf16[112,480]{1,0:T(8,128)(2,1)S(1)}, bf16[112,480]{1,0:T(8,128)(2,1)S(1)}, u32[]{:S(2)}, u32[]{:S(2)}) collective-permute-start(bf16[112,480]{1,0:T(8,128)(2,1)S(1)} %shard_map.100.refs_0_.m0.refs_2_.refs_4_), channel_id=1, source_target_pairs={{0,16},{8,24},{16,0},{24,8},{1,17},{9,25},{17,1},{25,9},{2,18},{10... | collective-permute-start | bytes 322568 | tf_op jit(solution)/shard_map/ppermute | solution.py:34
  5.7 2.0 %collective-permute-done.refs_1_.m1.refs_3_.refs_5_ = bf16[112,480]{1,0:T(8,128)(2,1)S(1)} collective-permute-done((bf16[112,480]{1,0:T(8,128)(2,1)S(1)}, bf16[112,480]{1,0:T(8,128)(2,1)S(1)}, u32[]{:S(2)}, u32[]{:S(2)}) %collective-permute-start) | collective-permute-done | bytes 107552 | tf_op jit(solution)/shard_map/ppermute | solution.py:34
  7.7 3.7 %collective-permute-done.1.refs_2_.m2.refs_4_.refs_6_ = bf16[112,480]{1,0:T(8,128)(2,1)S(1)} collective-permute-done((bf16[112,480]{1,0:T(8,128)(2,1)S(1)}, bf16[112,480]{1,0:T(8,128)(2,1)S(1)}, u32[]{:S(2)}, u32[]{:S(2)}) %collective-permute-start.1) | collective-permute-done | bytes 107552 | tf_op jit(solution)/shard_map/ppermute | solution.py:34
  11.4 3.7 %collective-permute-start.5 = (bf16[4,16,480]{2,1,0:T(8,128)(2,1)S(1)}, bf16[4,16,480]{2,1,0:T(8,128)(2,1)S(1)}, u32[]{:S(2)}, u32[]{:S(2)}) collective-permute-start(bf16[4,16,480]{2,1,0:T(8,128)(2,1)S(1)} %shard_map.101), channel_id=1, source_target_pairs={{0,6},{1,7},{2,4},{3,5},{4,2},{5,3},{6,0},{7,1},{8,14},{9,15},{10,... | collective-permute-start | bytes 184328 | tf_op jit(solution)/shard_map/ppermute | solution.py:34
  15.9 1.5 %shard_map.102 = (bf16[3,160,384]{2,1,0:T(8,128)(2,1)S(1)}, bf16[3,160,384]{2,1,0:T(8,128)(2,1)S(1)}, bf16[4,16,320]{2,1,0:T(8,128)(2,1)S(1)}, bf16[192,384]{1,0:T(8,128)(2,1)S(1)}, bf16[192,384]{1,0:T(8,128)(2,1)S(1)}) custom-call(bf16[2,4,160,96]{3,2,1,0:T(8,128)(2,1)} %bitcast.19, bf16[2,4,160,96]{3,2,1,0:T(8,128)(2,1)} %bitcast.20, ...), custom_call_target="tpu_custom_call" | custom-call | bytes 1048576 | tf_op jit(solution)/shard_map/pallas_call | solution.py:515
  17.4 1.3 %collective-permute-start.7 = (bf16[192,384]{1,0:T(8,128)(2,1)S(1)}, bf16[192,384]{1,0:T(8,128)(2,1)S(1)}, u32[]{:S(2)}, u32[]{:S(2)}) collective-permute-start(bf16[192,384]{1,0:T(8,128)(2,1)S(1)} %get-tuple-element.22), channel_id=1, source_target_pairs={{0,1},{1,2},{2,3},{3,4},{4,5},{5,6},{6,7},{8,9},{9,10},{10,11},{11... | collective-permute-start | bytes 442376 | tf_op jit(solution)/shard_map/ppermute | solution.py:58
  18.7 1.3 %collective-permute-start.8 = (bf16[192,384]{1,0:T(8,128)(2,1)S(1)}, bf16[192,384]{1,0:T(8,128)(2,1)S(1)}, u32[]{:S(2)}, u32[]{:S(2)}) collective-permute-start(bf16[192,384]{1,0:T(8,128)(2,1)S(1)} %get-tuple-element.24), channel_id=1, source_target_pairs={{1,0},{2,1},{3,2},{4,3},{5,4},{6,5},{7,6},{9,8},{10,9},{11,10},{12... | collective-permute-start | bytes 442376 | tf_op jit(solution)/shard_map/ppermute | solution.py:62
  20.3 2.5 %collective-permute-start.6 = (bf16[16,16,480]{2,1,0:T(8,128)(2,1)S(1)}, bf16[16,16,480]{2,1,0:T(8,128)(2,1)S(1)}, u32[]{:S(2)}, u32[]{:S(2)}) collective-permute-start(bf16[16,16,480]{2,1,0:T(8,128)(2,1)S(1)} %pad_maximum_fusion.2.near_ref), channel_id=1, source_target_pairs={{0,1},{1,0},{2,3},{3,2},{4,5},{5,4},{6,7},{7,6},{8,9},{9,8},{10,11... | collective-permute-start | bytes 737288 | tf_op jit(solution)/shard_map/ppermute | solution.py:34
  26.1 1.6 %collective-permute-start.14 = (bf16[3,160,384]{2,1,0:T(8,128)(2,1)S(1)}, bf16[3,160,384]{2,1,0:T(8,128)(2,1)S(1)}, u32[]{:S(2)}, u32[]{:S(2)}) collective-permute-start(bf16[3,160,384]{2,1,0:T(8,128)(2,1)S(1)} %get-tuple-element.29.p0), channel_id=1, source_target_pairs={{0,24},{8,16},{16,8},{24,0},{1,25},{9,17},{17,9},{25,1},{2,26},{10... | collective-permute-start | bytes 1105928 | tf_op jit(solution)/shard_map/ppermute | solution.py:34
  27.6 4.5 %shard_map.103 = (bf16[3,6,160,384]{3,2,1,0:T(8,128)(2,1)S(1)}, f32[2,384]{1,0:T(2,128)S(1)}) custom-call(s32[32]{0:T(128)S(1)} %copy-done.2, bf16[16,16,480]{2,1,0:T(8,128)(2,1)S(1)} %pad_maximum_fusion.2.near_ref, bf16[16,16,480]{2,1,0:T(8,128)(2,1)S(1)} %collective-permute-done.6.far_ref, bf16[192,384]{1,0:T(8,128)(2,1)S(1)} %collective-permute-done.7.before, ...), custom_call_target="tpu_custom_call" | custom-call | flops 318504960 | bytes 1048576 | tf_op jit(solution)/shard_map/pallas_call | solution.py:557
  32.1 2.9 %collective-permute-start.9 = (f32[2,384]{1,0:T(2,128)S(1)}, f32[2,384]{1,0:T(2,128)S(1)}, u32[]{:S(2)}, u32[]{:S(2)}) collective-permute-start(f32[2,384]{1,0:T(2,128)S(1)} %get-tuple-element.25), channel_id=1, source_target_pairs={{0,1},{1,0},{2,3},{3,2},{4,5},{5,4},{6,7},{7,6},{8,9},{9,8},{10,11... | collective-permute-start | bytes 9224 | tf_op jit(solution)/shard_map/ppermute | solution.py:34
  35.9 1.5 %collective-permute-start.10 = (f32[2,2,384]{2,1,0:T(2,128)S(1)}, f32[2,2,384]{2,1,0:T(2,128)S(1)}, u32[]{:S(2)}, u32[]{:S(2)}) collective-permute-start(f32[2,2,384]{2,1,0:T(2,128)S(1)} %pad_maximum_fusion.5), channel_id=1, source_target_pairs={{0,2},{1,3},{2,0},{3,1},{4,6},{5,7},{6,4},{7,5},{8,10},{9,11},{10,... | collective-permute-start | bytes 18440 | tf_op jit(solution)/shard_map/ppermute | solution.py:34
  37.3 2.0 %shard_map.105 = (bf16[9,384,256]{2,1,0:T(8,128)(2,1)S(1)}, bf16[9,384,256]{2,1,0:T(8,128)(2,1)S(1)}) custom-call(bf16[3,3,3,96,384]{4,3,2,1,0:T(8,128)(2,1)S(1)} %copy-done), custom_call_target="tpu_custom_call" | custom-call | bytes 1048576 | tf_op jit(solution)/shard_map/pallas_call | solution.py:536
  39.3 2.2 %shard_map.108 = (bf16[9,384,256]{2,1,0:T(8,128)(2,1)S(1)}, bf16[9,384,256]{2,1,0:T(8,128)(2,1)S(1)}) custom-call(bf16[3,3,3,96,384]{4,3,2,1,0:T(8,128)(2,1)S(1)} %copy-done.1), custom_call_target="tpu_custom_call" | custom-call | bytes 1048576 | tf_op jit(solution)/shard_map/pallas_call | solution.py:536
  41.5 2.4 %collective-permute-start.11 = (f32[4,2,384]{2,1,0:T(2,128)S(1)}, f32[4,2,384]{2,1,0:T(2,128)S(1)}, u32[]{:S(2)}, u32[]{:S(2)}) collective-permute-start(f32[4,2,384]{2,1,0:T(2,128)S(1)} %pad_maximum_fusion.3.refs_0_), channel_id=1, source_target_pairs={{0,4},{1,5},{2,6},{3,7},{4,0},{5,1},{6,2},{7,3},{8,12},{9,13},{10,... | collective-permute-start | bytes 36872 | tf_op jit(solution)/shard_map/ppermute | solution.py:34
  44.0 2.9 %shard_map.106.refs_7_ = f32[2,640,128]{2,1,0:T(8,128)S(1)} custom-call(bf16[3,160,384]{2,1,0:T(8,128)(2,1)S(1)} %get-tuple-element.29.p0, bf16[3,160,384]{2,1,0:T(8,128)(2,1)S(1)} %collective-permute-done.12.p1, bf16[3,160,384]{2,1,0:T(8,128)(2,1)S(1)} %collective-permute-done.13.p2, bf16[3,160,384]{2,1,0:T(8,128)(2,1)S(1)} %collective-permute-done.14.p3, ...), custom_call_target="tpu_custom_call" | custom-call | flops 1274019840 | bytes 1048576 | tf_op jit(solution)/shard_map/pallas_call | solution.py:546
  46.9 5.9 %shard_map.107 = (bf16[3,160,384]{2,1,0:T(8,128)(2,1)S(1)}, f32[2,128]{1,0:T(2,128)S(1)}) custom-call(f32[4,2,384]{2,1,0:T(2,128)S(1)} %pad_maximum_fusion.3.refs_0_, f32[4,2,384]{2,1,0:T(2,128)S(1)} %collective-permute-done.11.refs_1_, bf16[112,480]{1,0:T(8,128)(2,1)S(1)} %shard_map.100.refs_0_.m0.refs_2_.refs_4_, ...), custom_call_target="tpu_custom_call" | custom-call | flops 2548039680 | bytes 1048576 | tf_op jit(solution)/shard_map/pallas_call | solution.py:578
  52.7 1.6 %collective-permute-start.17 = (f32[2,128]{1,0:T(2,128)S(1)}, f32[2,128]{1,0:T(2,128)S(1)}, u32[]{:S(2)}, u32[]{:S(2)}) collective-permute-start(f32[2,128]{1,0:T(2,128)S(1)} %get-tuple-element.32), channel_id=1, source_target_pairs={{0,24},{8,16},{16,8},{24,0},{1,25},{9,17},{17,9},{25,1},{2,26},{10... | collective-permute-start | bytes 3080 | tf_op jit(solution)/shard_map/ppermute | solution.py:34
  58.5 1.3 %collective-permute-start.26 = (bf16[3,160,384]{2,1,0:T(8,128)(2,1)S(1)}, bf16[3,160,384]{2,1,0:T(8,128)(2,1)S(1)}, u32[]{:S(2)}, u32[]{:S(2)}) collective-permute-start(bf16[3,160,384]{2,1,0:T(8,128)(2,1)S(1)} %get-tuple-element.34.p0), channel_id=1, source_target_pairs={{0,8},{8,0},{16,24},{24,16},{1,9},{9,1},{17,25},{25,17},{2,10},{10... | collective-permute-start | bytes 1105928 | tf_op jit(solution)/shard_map/ppermute | solution.py:34
  60.5 1.6 %collective-permute-start.28 = (bf16[3,160,384]{2,1,0:T(8,128)(2,1)S(1)}, bf16[3,160,384]{2,1,0:T(8,128)(2,1)S(1)}, u32[]{:S(2)}, u32[]{:S(2)}) collective-permute-start(bf16[3,160,384]{2,1,0:T(8,128)(2,1)S(1)} %get-tuple-element.34.p0), channel_id=1, source_target_pairs={{0,24},{8,16},{16,8},{24,0},{1,25},{9,17},{17,9},{25,1},{2,26},{10... | collective-permute-start | bytes 1105928 | tf_op jit(solution)/shard_map/ppermute | solution.py:34
  62.1 5.6 %collective-permute-done.22.refs_9_ = bf16[3,160,384]{2,1,0:T(8,128)(2,1)S(1)} collective-permute-done((bf16[3,160,384]{2,1,0:T(8,128)(2,1)S(1)}, bf16[3,160,384]{2,1,0:T(8,128)(2,1)S(1)}, u32[]{:S(2)}, u32[]{:S(2)}) %collective-permute-start.22) | collective-permute-done | bytes 368672 | tf_op jit(solution)/shard_map/ppermute | solution.py:34
  67.8 1.4 %collective-permute-start.24 = (bf16[3,80,384]{2,1,0:T(8,128)(2,1)S(1)}, bf16[3,80,384]{2,1,0:T(8,128)(2,1)S(1)}, u32[]{:S(2)}, u32[]{:S(2)}) collective-permute-start(bf16[3,80,384]{2,1,0:T(8,128)(2,1)S(1)} %slice.40), channel_id=1, source_target_pairs={{0,16},{8,24},{16,0},{24,8},{1,17},{9,25},{17,1},{25,9},{2,18},{10... | collective-permute-start | bytes 552968 | tf_op jit(solution)/shard_map/ppermute | solution.py:34
  70.3 16.5 %collective-permute-done.24.refs_11_ = bf16[3,80,384]{2,1,0:T(8,128)(2,1)S(1)} collective-permute-done((bf16[3,80,384]{2,1,0:T(8,128)(2,1)S(1)}, bf16[3,80,384]{2,1,0:T(8,128)(2,1)S(1)}, u32[]{:S(2)}, u32[]{:S(2)}) %collective-permute-start.24) | collective-permute-done | bytes 184352 | tf_op jit(solution)/shard_map/ppermute | solution.py:34
  87.2 2.4 %collective-permute-start.29 = (bf16[3,160,384]{2,1,0:T(8,128)(2,1)S(1)}, bf16[3,160,384]{2,1,0:T(8,128)(2,1)S(1)}, u32[]{:S(2)}, u32[]{:S(2)}) collective-permute-start(bf16[3,160,384]{2,1,0:T(8,128)(2,1)S(1)} %pad_maximum_fusion), channel_id=1, source_target_pairs={{0,1},{1,2},{2,3},{3,4},{4,5},{5,6},{6,7},{8,9},{9,10},{10,11},{11... | collective-permute-start | bytes 1105928 | tf_op jit(solution)/shard_map/ppermute | solution.py:58
  89.9 1.5 %collective-permute-start.30 = (bf16[3,160,384]{2,1,0:T(8,128)(2,1)S(1)}, bf16[3,160,384]{2,1,0:T(8,128)(2,1)S(1)}, u32[]{:S(2)}, u32[]{:S(2)}) collective-permute-start(bf16[3,160,384]{2,1,0:T(8,128)(2,1)S(1)} %pad_maximum_fusion.1), channel_id=1, source_target_pairs={{1,0},{2,1},{3,2},{4,3},{5,4},{6,5},{7,6},{9,8},{10,9},{11,10},{12... | collective-permute-start | bytes 1105928 | tf_op jit(solution)/shard_map/ppermute | solution.py:62
  91.5 5.3 %collective-permute-start.19 = (f32[2,4,2,128]{3,2,1,0:T(2,128)S(1)}, f32[2,4,2,128]{3,2,1,0:T(2,128)S(1)}, u32[]{:S(2)}, u32[]{:S(2)}) collective-permute-start(f32[2,4,2,128]{3,2,1,0:T(2,128)S(1)} %pad_maximum_fusion.4.refs_0_), channel_id=1, source_target_pairs={{0,2},{1,3},{2,0},{3,1},{4,6},{5,7},{6,4},{7,5},{8,10},{9,11},{10,... | collective-permute-start | bytes 24584 | tf_op jit(solution)/shard_map/ppermute | solution.py:34
  96.8 1.3 %collective-permute-start.20 = (f32[2,4,2,128]{3,2,1,0:T(2,128)S(1)}, f32[2,4,2,128]{3,2,1,0:T(2,128)S(1)}, u32[]{:S(2)}, u32[]{:S(2)}) collective-permute-start(f32[2,4,2,128]{3,2,1,0:T(2,128)S(1)} %pad_maximum_fusion.4.refs_0_), channel_id=1, source_target_pairs={{0,4},{1,5},{2,6},{3,7},{4,0},{5,1},{6,2},{7,3},{8,12},{9,13},{10,... | collective-permute-start | bytes 24584 | tf_op jit(solution)/shard_map/ppermute | solution.py:34
  99.3 2.9 %shard_map.109.refs_13_ = f32[2,640,128]{2,1,0:T(8,128)S(1)} custom-call(bf16[3,160,384]{2,1,0:T(8,128)(2,1)S(1)} %get-tuple-element.34.p0, bf16[3,160,384]{2,1,0:T(8,128)(2,1)S(1)} %collective-permute-done.26.p1, bf16[3,160,384]{2,1,0:T(8,128)(2,1)S(1)} %collective-permute-done.27.p2, bf16[3,160,384]{2,1,0:T(8,128)(2,1)S(1)} %collective-permute-done.28.p3, ...), custom_call_target="tpu_custom_call" | custom-call | flops 1274019840 | bytes 1048576 | tf_op jit(solution)/shard_map/pallas_call | solution.py:546
  102.2 1.2 %collective-permute-done.20.refs_2_ = f32[2,4,2,128]{3,2,1,0:T(2,128)S(1)} collective-permute-done((f32[2,4,2,128]{3,2,1,0:T(2,128)S(1)}, f32[2,4,2,128]{3,2,1,0:T(2,128)S(1)}, u32[]{:S(2)}, u32[]{:S(2)}) %collective-permute-start.20) | collective-permute-done | bytes 8224 | tf_op jit(solution)/shard_map/ppermute | solution.py:34
  103.6 6.5 %shard_map.110 = (f32[3,640,128]{2,1,0:T(8,128)S(1)}, f32[2,384]{1,0:T(2,128)S(1)}) custom-call(f32[2,4,2,128]{3,2,1,0:T(2,128)S(1)} %pad_maximum_fusion.4.refs_0_, f32[2,4,2,128]{3,2,1,0:T(2,128)S(1)} %collective-permute-done.19.refs_1_, f32[2,4,2,128]{3,2,1,0:T(2,128)S(1)} %collective-permute-done.20.refs_2_, ...), custom_call_target="tpu_custom_call" | custom-call | flops 2548039680 | bytes 1048576 | tf_op jit(solution)/shard_map/pallas_call | solution.py:594
  110.0 2.1 %shard_map.111 = bf16[3,4,160,96]{3,2,1,0:T(8,128)(2,1)} custom-call(f32[3,640,128]{2,1,0:T(8,128)S(1)} %get-tuple-element.37.part_ref, f32[2,384]{1,0:T(2,128)S(1)} %get-tuple-element.38.scale_ref, bf16[3,160,384]{2,1,0:T(8,128)(2,1)S(1)} %collective-permute-done.29.up, bf16[3,160,384]{2,1,0:T(8,128)(2,1)S(1)} %collective-permute-done.30.down, ...), custom_call_target="tpu_custom_call" | custom-call | flops 637009920 | bytes 1048576 | tf_op jit(solution)/shard_map/pallas_call | solution.py:601
  (64 shorter events, 14.4 us)
Async XLA Ops:
  0.0 27.6 %copy-start.2 = (s32[32]{0:T(128)S(1)}, s32[32]{0:T(128)}, u32[]{:S(2)}) copy-start(s32[32]{0:T(128)} %map_ref.1) | copy-start | bytes 388
  1.2 6.6 %collective-permute-start = (bf16[112,480]{1,0:T(8,128)(2,1)S(1)}, bf16[112,480]{1,0:T(8,128)(2,1)S(1)}, u32[]{:S(2)}, u32[]{:S(2)}) collective-permute-start(bf16[112,480]{1,0:T(8,128)(2,1)S(1)} %shard_map.100.refs_0_.m0.refs_2_.refs_4_), channel_id=1, source_target_pairs={{0,8},{8,0},{16,24},{24,16},{1,9},{9,1},{17,25},{25,17},{2,10},{10... | collective-permute-start | bytes 322568 | tf_op jit(solution)/shard_map/ppermute | solution.py:34
  4.2 7.2 %collective-permute-start.1 = (bf16[112,480]{1,0:T(8,128)(2,1)S(1)}, bf16[112,480]{1,0:T(8,128)(2,1)S(1)}, u32[]{:S(2)}, u32[]{:S(2)}) collective-permute-start(bf16[112,480]{1,0:T(8,128)(2,1)S(1)} %shard_map.100.refs_0_.m0.refs_2_.refs_4_), channel_id=1, source_target_pairs={{0,16},{8,24},{16,0},{24,8},{1,17},{9,25},{17,1},{25,9},{2,18},{10... | collective-permute-start | bytes 322568 | tf_op jit(solution)/shard_map/ppermute | solution.py:34
  5.7 5.7 %collective-permute-start.2 = (bf16[112,480]{1,0:T(8,128)(2,1)S(1)}, bf16[112,480]{1,0:T(8,128)(2,1)S(1)}, u32[]{:S(2)}, u32[]{:S(2)}) collective-permute-start(bf16[112,480]{1,0:T(8,128)(2,1)S(1)} %shard_map.100.refs_0_.m0.refs_2_.refs_4_), channel_id=1, source_target_pairs={{0,24},{8,16},{16,8},{24,0},{1,25},{9,17},{17,9},{25,1},{2,26},{10... | collective-permute-start | bytes 322568 | tf_op jit(solution)/shard_map/ppermute | solution.py:34
  11.4 8.6 %collective-permute-start.5 = (bf16[4,16,480]{2,1,0:T(8,128)(2,1)S(1)}, bf16[4,16,480]{2,1,0:T(8,128)(2,1)S(1)}, u32[]{:S(2)}, u32[]{:S(2)}) collective-permute-start(bf16[4,16,480]{2,1,0:T(8,128)(2,1)S(1)} %shard_map.101), channel_id=1, source_target_pairs={{0,6},{1,7},{2,4},{3,5},{4,2},{5,3},{6,0},{7,1},{8,14},{9,15},{10,... | collective-permute-start | bytes 184328 | tf_op jit(solution)/shard_map/ppermute | solution.py:34
  15.1 5.2 %collective-permute-start.4 = (bf16[4,16,480]{2,1,0:T(8,128)(2,1)S(1)}, bf16[4,16,480]{2,1,0:T(8,128)(2,1)S(1)}, u32[]{:S(2)}, u32[]{:S(2)}) collective-permute-start(bf16[4,16,480]{2,1,0:T(8,128)(2,1)S(1)} %shard_map.101), channel_id=1, source_target_pairs={{0,4},{1,5},{2,6},{3,7},{4,0},{5,1},{6,2},{7,3},{8,12},{9,13},{10,... | collective-permute-start | bytes 184328 | tf_op jit(solution)/shard_map/ppermute | solution.py:34
  15.1 5.2 %collective-permute-start.3 = (bf16[4,16,480]{2,1,0:T(8,128)(2,1)S(1)}, bf16[4,16,480]{2,1,0:T(8,128)(2,1)S(1)}, u32[]{:S(2)}, u32[]{:S(2)}) collective-permute-start(bf16[4,16,480]{2,1,0:T(8,128)(2,1)S(1)} %shard_map.101), channel_id=1, source_target_pairs={{0,2},{1,3},{2,0},{3,1},{4,6},{5,7},{6,4},{7,5},{8,10},{9,11},{10,... | collective-permute-start | bytes 184328 | tf_op jit(solution)/shard_map/ppermute | solution.py:34
  17.4 5.4 %collective-permute-start.7 = (bf16[192,384]{1,0:T(8,128)(2,1)S(1)}, bf16[192,384]{1,0:T(8,128)(2,1)S(1)}, u32[]{:S(2)}, u32[]{:S(2)}) collective-permute-start(bf16[192,384]{1,0:T(8,128)(2,1)S(1)} %get-tuple-element.22), channel_id=1, source_target_pairs={{0,1},{1,2},{2,3},{3,4},{4,5},{5,6},{6,7},{8,9},{9,10},{10,11},{11... | collective-permute-start | bytes 442376 | tf_op jit(solution)/shard_map/ppermute | solution.py:58
  18.7 4.7 %collective-permute-start.8 = (bf16[192,384]{1,0:T(8,128)(2,1)S(1)}, bf16[192,384]{1,0:T(8,128)(2,1)S(1)}, u32[]{:S(2)}, u32[]{:S(2)}) collective-permute-start(bf16[192,384]{1,0:T(8,128)(2,1)S(1)} %get-tuple-element.24), channel_id=1, source_target_pairs={{1,0},{2,1},{3,2},{4,3},{5,4},{6,5},{7,6},{9,8},{10,9},{11,10},{12... | collective-permute-start | bytes 442376 | tf_op jit(solution)/shard_map/ppermute | solution.py:62
  20.3 7.3 %collective-permute-start.6 = (bf16[16,16,480]{2,1,0:T(8,128)(2,1)S(1)}, bf16[16,16,480]{2,1,0:T(8,128)(2,1)S(1)}, u32[]{:S(2)}, u32[]{:S(2)}) collective-permute-start(bf16[16,16,480]{2,1,0:T(8,128)(2,1)S(1)} %pad_maximum_fusion.2.near_ref), channel_id=1, source_target_pairs={{0,1},{1,0},{2,3},{3,2},{4,5},{5,4},{6,7},{7,6},{8,9},{9,8},{10,11... | collective-permute-start | bytes 737288 | tf_op jit(solution)/shard_map/ppermute | solution.py:34
  24.1 19.9 %collective-permute-start.12 = (bf16[3,160,384]{2,1,0:T(8,128)(2,1)S(1)}, bf16[3,160,384]{2,1,0:T(8,128)(2,1)S(1)}, u32[]{:S(2)}, u32[]{:S(2)}) collective-permute-start(bf16[3,160,384]{2,1,0:T(8,128)(2,1)S(1)} %get-tuple-element.29.p0), channel_id=1, source_target_pairs={{0,8},{8,0},{16,24},{24,16},{1,9},{9,1},{17,25},{25,17},{2,10},{10... | collective-permute-start | bytes 1105928 | tf_op jit(solution)/shard_map/ppermute | solution.py:34
  25.1 18.9 %collective-permute-start.13 = (bf16[3,160,384]{2,1,0:T(8,128)(2,1)S(1)}, bf16[3,160,384]{2,1,0:T(8,128)(2,1)S(1)}, u32[]{:S(2)}, u32[]{:S(2)}) collective-permute-start(bf16[3,160,384]{2,1,0:T(8,128)(2,1)S(1)} %get-tuple-element.29.p0), channel_id=1, source_target_pairs={{0,16},{8,24},{16,0},{24,8},{1,17},{9,25},{17,1},{25,9},{2,18},{10... | collective-permute-start | bytes 1105928 | tf_op jit(solution)/shard_map/ppermute | solution.py:34
  26.1 17.9 %collective-permute-start.14 = (bf16[3,160,384]{2,1,0:T(8,128)(2,1)S(1)}, bf16[3,160,384]{2,1,0:T(8,128)(2,1)S(1)}, u32[]{:S(2)}, u32[]{:S(2)}) collective-permute-start(bf16[3,160,384]{2,1,0:T(8,128)(2,1)S(1)} %get-tuple-element.29.p0), channel_id=1, source_target_pairs={{0,24},{8,16},{16,8},{24,0},{1,25},{9,17},{17,9},{25,1},{2,26},{10... | collective-permute-start | bytes 1105928 | tf_op jit(solution)/shard_map/ppermute | solution.py:34
  32.1 3.7 %collective-permute-start.9 = (f32[2,384]{1,0:T(2,128)S(1)}, f32[2,384]{1,0:T(2,128)S(1)}, u32[]{:S(2)}, u32[]{:S(2)}) collective-permute-start(f32[2,384]{1,0:T(2,128)S(1)} %get-tuple-element.25), channel_id=1, source_target_pairs={{0,1},{1,0},{2,3},{3,2},{4,5},{5,4},{6,7},{7,6},{8,9},{9,8},{10,11... | collective-permute-start | bytes 9224 | tf_op jit(solution)/shard_map/ppermute | solution.py:34
  35.9 5.6 %collective-permute-start.10 = (f32[2,2,384]{2,1,0:T(2,128)S(1)}, f32[2,2,384]{2,1,0:T(2,128)S(1)}, u32[]{:S(2)}, u32[]{:S(2)}) collective-permute-start(f32[2,2,384]{2,1,0:T(2,128)S(1)} %pad_maximum_fusion.5), channel_id=1, source_target_pairs={{0,2},{1,3},{2,0},{3,1},{4,6},{5,7},{6,4},{7,5},{8,10},{9,11},{10,... | collective-permute-start | bytes 18440 | tf_op jit(solution)/shard_map/ppermute | solution.py:34
  41.5 5.3 %collective-permute-start.11 = (f32[4,2,384]{2,1,0:T(2,128)S(1)}, f32[4,2,384]{2,1,0:T(2,128)S(1)}, u32[]{:S(2)}, u32[]{:S(2)}) collective-permute-start(f32[4,2,384]{2,1,0:T(2,128)S(1)} %pad_maximum_fusion.3.refs_0_), channel_id=1, source_target_pairs={{0,4},{1,5},{2,6},{3,7},{4,0},{5,1},{6,2},{7,3},{8,12},{9,13},{10,... | collective-permute-start | bytes 36872 | tf_op jit(solution)/shard_map/ppermute | solution.py:34
  52.7 5.8 %collective-permute-start.17 = (f32[2,128]{1,0:T(2,128)S(1)}, f32[2,128]{1,0:T(2,128)S(1)}, u32[]{:S(2)}, u32[]{:S(2)}) collective-permute-start(f32[2,128]{1,0:T(2,128)S(1)} %get-tuple-element.32), channel_id=1, source_target_pairs={{0,24},{8,16},{16,8},{24,0},{1,25},{9,17},{17,9},{25,1},{2,26},{10... | collective-permute-start | bytes 3080 | tf_op jit(solution)/shard_map/ppermute | solution.py:34
  54.4 5.5 %collective-permute-start.16 = (f32[2,128]{1,0:T(2,128)S(1)}, f32[2,128]{1,0:T(2,128)S(1)}, u32[]{:S(2)}, u32[]{:S(2)}) collective-permute-start(f32[2,128]{1,0:T(2,128)S(1)} %get-tuple-element.32), channel_id=1, source_target_pairs={{0,16},{8,24},{16,0},{24,8},{1,17},{9,25},{17,1},{25,9},{2,18},{10... | collective-permute-start | bytes 3080 | tf_op jit(solution)/shard_map/ppermute | solution.py:34
  55.3 5.3 %collective-permute-start.15 = (f32[2,128]{1,0:T(2,128)S(1)}, f32[2,128]{1,0:T(2,128)S(1)}, u32[]{:S(2)}, u32[]{:S(2)}) collective-permute-start(f32[2,128]{1,0:T(2,128)S(1)} %get-tuple-element.32), channel_id=1, source_target_pairs={{0,8},{8,0},{16,24},{24,16},{1,9},{9,1},{17,25},{25,17},{2,10},{10... | collective-permute-start | bytes 3080 | tf_op jit(solution)/shard_map/ppermute | solution.py:34
  56.3 11.5 %collective-permute-start.22 = (bf16[3,160,384]{2,1,0:T(8,128)(2,1)S(1)}, bf16[3,160,384]{2,1,0:T(8,128)(2,1)S(1)}, u32[]{:S(2)}, u32[]{:S(2)}) collective-permute-start(bf16[3,160,384]{2,1,0:T(8,128)(2,1)S(1)} %get-tuple-element.33.refs_8_), channel_id=1, source_target_pairs={{0,8},{8,0},{16,24},{24,16},{1,9},{9,1},{17,25},{25,17},{2,10},{10... | collective-permute-start | bytes 1105928 | tf_op jit(solution)/shard_map/ppermute | solution.py:34
  57.3 11.9 %collective-permute-start.23 = (bf16[3,160,384]{2,1,0:T(8,128)(2,1)S(1)}, bf16[3,160,384]{2,1,0:T(8,128)(2,1)S(1)}, u32[]{:S(2)}, u32[]{:S(2)}) collective-permute-start(bf16[3,160,384]{2,1,0:T(8,128)(2,1)S(1)} %get-tuple-element.33.refs_8_), channel_id=1, source_target_pairs={{0,16},{8,24},{16,0},{24,8},{1,17},{9,25},{17,1},{25,9},{2,18},{10... | collective-permute-start | bytes 1105928 | tf_op jit(solution)/shard_map/ppermute | solution.py:34
  58.5 32.9 %collective-permute-start.26 = (bf16[3,160,384]{2,1,0:T(8,128)(2,1)S(1)}, bf16[3,160,384]{2,1,0:T(8,128)(2,1)S(1)}, u32[]{:S(2)}, u32[]{:S(2)}) collective-permute-start(bf16[3,160,384]{2,1,0:T(8,128)(2,1)S(1)} %get-tuple-element.34.p0), channel_id=1, source_target_pairs={{0,8},{8,0},{16,24},{24,16},{1,9},{9,1},{17,25},{25,17},{2,10},{10... | collective-permute-start | bytes 1105928 | tf_op jit(solution)/shard_map/ppermute | solution.py:34
  59.8 37.0 %collective-permute-start.27 = (bf16[3,160,384]{2,1,0:T(8,128)(2,1)S(1)}, bf16[3,160,384]{2,1,0:T(8,128)(2,1)S(1)}, u32[]{:S(2)}, u32[]{:S(2)}) collective-permute-start(bf16[3,160,384]{2,1,0:T(8,128)(2,1)S(1)} %get-tuple-element.34.p0), channel_id=1, source_target_pairs={{0,16},{8,24},{16,0},{24,8},{1,17},{9,25},{17,1},{25,9},{2,18},{10... | collective-permute-start | bytes 1105928 | tf_op jit(solution)/shard_map/ppermute | solution.py:34
  60.5 37.6 %collective-permute-start.28 = (bf16[3,160,384]{2,1,0:T(8,128)(2,1)S(1)}, bf16[3,160,384]{2,1,0:T(8,128)(2,1)S(1)}, u32[]{:S(2)}, u32[]{:S(2)}) collective-permute-start(bf16[3,160,384]{2,1,0:T(8,128)(2,1)S(1)} %get-tuple-element.34.p0), channel_id=1, source_target_pairs={{0,24},{8,16},{16,8},{24,0},{1,25},{9,17},{17,9},{25,1},{2,26},{10... | collective-permute-start | bytes 1105928 | tf_op jit(solution)/shard_map/ppermute | solution.py:34
  67.8 19.0 %collective-permute-start.24 = (bf16[3,80,384]{2,1,0:T(8,128)(2,1)S(1)}, bf16[3,80,384]{2,1,0:T(8,128)(2,1)S(1)}, u32[]{:S(2)}, u32[]{:S(2)}) collective-permute-start(bf16[3,80,384]{2,1,0:T(8,128)(2,1)S(1)} %slice.40), channel_id=1, source_target_pairs={{0,16},{8,24},{16,0},{24,8},{1,17},{9,25},{17,1},{25,9},{2,18},{10... | collective-permute-start | bytes 552968 | tf_op jit(solution)/shard_map/ppermute | solution.py:34
  69.2 17.6 %collective-permute-start.25 = (bf16[3,80,384]{2,1,0:T(8,128)(2,1)S(1)}, bf16[3,80,384]{2,1,0:T(8,128)(2,1)S(1)}, u32[]{:S(2)}, u32[]{:S(2)}) collective-permute-start(bf16[3,80,384]{2,1,0:T(8,128)(2,1)S(1)} %slice.41), channel_id=1, source_target_pairs={{0,8},{8,0},{16,24},{24,16},{1,9},{9,1},{17,25},{25,17},{2,10},{10... | collective-permute-start | bytes 552968 | tf_op jit(solution)/shard_map/ppermute | solution.py:34
  86.8 3.1 %collective-permute-start.18 = (f32[4,2,128]{2,1,0:T(2,128)S(1)}, f32[4,2,128]{2,1,0:T(2,128)S(1)}, u32[]{:S(2)}, u32[]{:S(2)}) collective-permute-start(f32[4,2,128]{2,1,0:T(2,128)S(1)} %pad_maximum_fusion.6), channel_id=1, source_target_pairs={{0,1},{1,0},{2,3},{3,2},{4,5},{5,4},{6,7},{7,6},{8,9},{9,8},{10,11... | collective-permute-start | bytes 12296 | tf_op jit(solution)/shard_map/ppermute | solution.py:34
  87.2 22.8 %collective-permute-start.29 = (bf16[3,160,384]{2,1,0:T(8,128)(2,1)S(1)}, bf16[3,160,384]{2,1,0:T(8,128)(2,1)S(1)}, u32[]{:S(2)}, u32[]{:S(2)}) collective-permute-start(bf16[3,160,384]{2,1,0:T(8,128)(2,1)S(1)} %pad_maximum_fusion), channel_id=1, source_target_pairs={{0,1},{1,2},{2,3},{3,4},{4,5},{5,6},{6,7},{8,9},{9,10},{10,11},{11... | collective-permute-start | bytes 1105928 | tf_op jit(solution)/shard_map/ppermute | solution.py:58
  89.9 20.1 %collective-permute-start.30 = (bf16[3,160,384]{2,1,0:T(8,128)(2,1)S(1)}, bf16[3,160,384]{2,1,0:T(8,128)(2,1)S(1)}, u32[]{:S(2)}, u32[]{:S(2)}) collective-permute-start(bf16[3,160,384]{2,1,0:T(8,128)(2,1)S(1)} %pad_maximum_fusion.1), channel_id=1, source_target_pairs={{1,0},{2,1},{3,2},{4,3},{5,4},{6,5},{7,6},{9,8},{10,9},{11,10},{12... | collective-permute-start | bytes 1105928 | tf_op jit(solution)/shard_map/ppermute | solution.py:62
  91.5 10.8 %collective-permute-start.19 = (f32[2,4,2,128]{3,2,1,0:T(2,128)S(1)}, f32[2,4,2,128]{3,2,1,0:T(2,128)S(1)}, u32[]{:S(2)}, u32[]{:S(2)}) collective-permute-start(f32[2,4,2,128]{3,2,1,0:T(2,128)S(1)} %pad_maximum_fusion.4.refs_0_), channel_id=1, source_target_pairs={{0,2},{1,3},{2,0},{3,1},{4,6},{5,7},{6,4},{7,5},{8,10},{9,11},{10,... | collective-permute-start | bytes 24584 | tf_op jit(solution)/shard_map/ppermute | solution.py:34
  96.8 6.6 %collective-permute-start.20 = (f32[2,4,2,128]{3,2,1,0:T(2,128)S(1)}, f32[2,4,2,128]{3,2,1,0:T(2,128)S(1)}, u32[]{:S(2)}, u32[]{:S(2)}) collective-permute-start(f32[2,4,2,128]{3,2,1,0:T(2,128)S(1)} %pad_maximum_fusion.4.refs_0_), channel_id=1, source_target_pairs={{0,4},{1,5},{2,6},{3,7},{4,0},{5,1},{6,2},{7,3},{8,12},{9,13},{10,... | collective-permute-start | bytes 24584 | tf_op jit(solution)/shard_map/ppermute | solution.py:34
  98.1 5.4 %collective-permute-start.21 = (f32[2,4,2,128]{3,2,1,0:T(2,128)S(1)}, f32[2,4,2,128]{3,2,1,0:T(2,128)S(1)}, u32[]{:S(2)}, u32[]{:S(2)}) collective-permute-start(f32[2,4,2,128]{3,2,1,0:T(2,128)S(1)} %pad_maximum_fusion.4.refs_0_), channel_id=1, source_target_pairs={{0,6},{1,7},{2,4},{3,5},{4,2},{5,3},{6,0},{7,1},{8,14},{9,15},{10,... | collective-permute-start | bytes 24584 | tf_op jit(solution)/shard_map/ppermute | solution.py:34
  (2 other events, 36.7 us)
